TPU v7x, 512 devices: a whole 4x8x8 slice. The times are simulated.
512 devices in a mesh: sec: 16 (over y, core), cp: 32 (over x, z).
Axes of the slice: x: 4, y: 8, z: 8, core: 2. Of those that a mesh axis runs over, the one named last changes fastest.
Arguments:
- projected: bfloat16 [65536, 10240], P(('sec', 'cp')), may hold values from -6 to 6
- conv_weight: float32 [4, 10240], replicated, may hold values from -3 to 3
- conv_bias: float32 [10240], replicated, may hold values from -3 to 3
- step_size: bfloat16 [65536, 128], P(('sec', 'cp')), may hold values from 0 to 1
- log_decay: bfloat16 [65536, 128], P(('sec', 'cp')), may hold values from -1 to 0
- skip_gain: float32 [128], replicated, may hold values from 0.5 to 1.5
Outputs:
- ssd_out: bfloat16 [65536, 8192], P(('sec', 'cp'))
All inputs are finite; a program needn't handle non-finite values.
Results may differ from a plain program's by a relative error of at most 0.0034.
Values may be sent and summed in bfloat16 or wider, within the bound.
No kernel may reach another device: no remote copies, remote signals or barrier semaphores. Data moves between devices by JAX's collectives and lax.ppermute only.
A program may use at most 64 MiB of HBM per device.

v0:
```python
import jax
import jax.numpy as jnp
from jax import lax
from jax.sharding import PartitionSpec as P

HEAD_COUNT = 128
P_SIZE = 64
N = 128
G = 8
BLOCK = 256
KERNEL = 4


def passed_along(value, axis, steps):
    count = lax.axis_size(axis)
    leading, last = (max(0, -steps), min(count, count - steps))
    return lax.ppermute(value, axis, [(source, source + steps) for source in range(leading, last)])


def causal_conv(columns, rim_rows, weights, biases):
    padded = jnp.concatenate([rim_rows, columns], 0)
    length = columns.shape[0]
    summed = biases[None, :] + weights[0][None, :] * padded[0:length].astype(jnp.float32)
    for offset in range(1, KERNEL):
        summed = summed + weights[offset][None, :] * padded[offset : offset + length].astype(
            jnp.float32
        )
    return jax.nn.silu(summed).astype(jnp.bfloat16)


def per_target(columns, row_count, heads_here, group_heads):
    return jnp.repeat(columns.reshape(row_count, G, N), group_heads // heads_here, axis=1)


def per_device(projected, conv_weight, conv_bias, step_size, log_decay, skip_gain):
    targets = lax.axis_size("cp")
    row_count = projected.shape[0]
    heads_here = HEAD_COUNT // targets
    group_heads = HEAD_COUNT // G
    groups_here = max(1, heads_here // group_heads)
    width_x = HEAD_COUNT * P_SIZE
    width_g = G * N
    rim_rows = passed_along(projected[row_count - (KERNEL - 1) :], ("sec", "cp"), 1)
    mixed_cols = causal_conv(projected, rim_rows, conv_weight, conv_bias)
    send_b = per_target(
        mixed_cols[:, width_x : width_x + width_g], row_count, heads_here, group_heads
    )
    send_c = per_target(mixed_cols[:, width_x + width_g :], row_count, heads_here, group_heads)
    send_bc = jnp.concatenate([send_b, send_c], axis=2).reshape(
        row_count, targets * 2 * groups_here * N
    )
    head_x, head_bc, head_step, head_decay = (
        lax.all_to_all(mixed_cols[:, :width_x], "cp", split_axis=1, concat_axis=0, tiled=True),
        lax.all_to_all(send_bc, "cp", split_axis=1, concat_axis=0, tiled=True),
        lax.all_to_all(step_size, "cp", split_axis=1, concat_axis=0, tiled=True),
        lax.all_to_all(log_decay, "cp", split_axis=1, concat_axis=0, tiled=True),
    )
    position = lax.axis_index("cp")
    section_rows = head_x.shape[0]
    blocks = section_rows // BLOCK
    repeat_count = heads_here // groups_here
    values = head_x.reshape(blocks, BLOCK, heads_here, P_SIZE)
    keys_b = jnp.repeat(
        head_bc[:, : groups_here * N].reshape(blocks, BLOCK, groups_here, N), repeat_count, axis=2
    )
    query_c = jnp.repeat(
        head_bc[:, groups_here * N :].reshape(blocks, BLOCK, groups_here, N), repeat_count, axis=2
    )
    decay_log = head_decay.astype(jnp.float32).reshape(blocks, BLOCK, heads_here)
    steps_f = head_step.astype(jnp.float32).reshape(blocks, BLOCK, heads_here)
    running = jnp.cumsum(decay_log, axis=1)
    block_end = running[:, -1:, :]
    weighted_b = (
        keys_b.astype(jnp.float32) * (jnp.exp(block_end - running) * steps_f)[..., None]
    ).astype(jnp.bfloat16)
    block_states = jnp.einsum(
        "cshn,cshp->chnp", weighted_b, values, preferred_element_type=jnp.float32
    )
    block_gain = jnp.exp(block_end[:, 0, :])

    def advance(carried, inputs_now):
        state_now, decay_now = carried
        add_state, gain_now = inputs_now
        return (
            (gain_now[:, None, None] * state_now + add_state, decay_now * gain_now),
            (state_now, decay_now),
        )

    start_state = jnp.zeros((heads_here, N, P_SIZE), jnp.float32)
    start_decay = jnp.ones((heads_here,), jnp.float32)
    (section_state, section_decay), (local_entering, decay_before) = lax.scan(
        advance, (start_state, start_decay), (block_states, block_gain)
    )

    def relay_step(turn_index, incoming):
        outgoing = section_decay[:, None, None] * incoming + section_state
        return passed_along(outgoing, "sec", 1)

    carried_in = lax.fori_loop(
        0, lax.axis_size("sec") - 1, relay_step, jnp.zeros_like(section_state)
    )
    entering = local_entering + decay_before[:, :, None, None] * carried_in[None]
    skip_here = lax.dynamic_slice_in_dim(skip_gain, position * heads_here, heads_here, 0)
    causal_mask = lax.broadcasted_iota(jnp.int32, (BLOCK, BLOCK), 0) >= lax.broadcasted_iota(
        jnp.int32, (BLOCK, BLOCK), 1
    )

    def block_output(inputs_now):
        xblock, bblock, cblock, runblock, stepblock, stateblock = inputs_now
        scores = jnp.einsum("thn,shn->hts", cblock, bblock, preferred_element_type=jnp.float32)
        running_t = runblock.T
        log_gap = jnp.where(
            causal_mask[None], running_t[:, :, None] - running_t[:, None, :], -jnp.inf
        )
        mix_weights = (scores * jnp.exp(log_gap) * stepblock.T[:, None, :]).astype(jnp.bfloat16)
        within = jnp.einsum("hts,shp->thp", mix_weights, xblock, preferred_element_type=jnp.float32)
        carried_part = (
            jnp.einsum(
                "thn,hnp->thp",
                cblock.astype(jnp.float32),
                stateblock,
                precision=lax.Precision.HIGHEST,
                preferred_element_type=jnp.float32,
            )
            * jnp.exp(runblock)[:, :, None]
        )
        return (
            within + carried_part + skip_here[None, :, None] * xblock.astype(jnp.float32)
        ).astype(jnp.bfloat16)

    outputs = lax.map(block_output, (values, keys_b, query_c, running, steps_f, entering))
    outputs = outputs.reshape(section_rows, heads_here * P_SIZE)
    return lax.all_to_all(outputs, "cp", split_axis=0, concat_axis=1, tiled=True)


def solution(mesh):
    in_specs = (
        P(("sec", "cp"), None),
        P(),
        P(),
        P(("sec", "cp"), None),
        P(("sec", "cp"), None),
        P(),
    )
    out_specs = P(("sec", "cp"), None)
    return jax.shard_map(
        per_device, mesh=mesh, in_specs=in_specs, out_specs=out_specs, check_vma=False
    )
```

profile of v0, /device:TPU:25, one launch (start us, length us, event | category | flops | bytes accessed | tf_op | source)
XLA Modules:
  0.0 500.2 jit_solution(10638179416322447657)
XLA Ops:
  6.4 12.0 %all-to-all-start.2 = ((bf16[128,32,4]{0,2,1:T(4,128)(2,1)}), bf16[128,32,4]{0,2,1:T(4,128)(2,1)S(1)}, u32[]{:S(2)}, u32[]{:S(2)}) async-start(bf16[128,32,4]{0,2,1:T(4,128)(2,1)} %bitcast.13), calls=%async_computation.2 | async-start | bytes 65536 | tf_op jit(solution)/shard_map/all_to_all | solution.py:56
  21.3 7.2 %multiply_convert_fusion.1 = bf16[128,10240]{1,0:T(8,128)(2,1)S(1)} fusion(bf16[128,10240]{1,0:T(8,128)(2,1)} %param.12, bf16[3,10240]{1,0:T(4,128)(2,1)S(1)} %collective-permute-done.1, f32[10240]{0:T(1024)S(1)} %bitcast.148, f32[10240]{0:T(1024)S(1)} %bitcast.149, f32[10240]{0:T(1024)S(1)} %bitcast.147, f32[10240]{0:T(1024)S(1)} %bitcast.146, f32[10240]{0:T(1024)} %param.14), kind=kLoop, calls=%fused_computation.48 | loop fusion | flops 34078720 | bytes 5509120 | tf_op jit(solution)/shard_map/convert_element_type | solution.py:28
  28.6 9.2 %all-to-all-start.3 = ((bf16[128,32,4]{0,2,1:T(4,128)(2,1)}), bf16[128,32,4]{0,2,1:T(4,128)(2,1)S(1)}, u32[]{:S(2)}, u32[]{:S(2)}) async-start(bf16[128,32,4]{0,2,1:T(4,128)(2,1)} %bitcast.17), calls=%async_computation.3 | async-start | bytes 65536 | tf_op jit(solution)/shard_map/all_to_all | solution.py:55
  40.0 6.7 %all-to-all-done.3 = bf16[128,32,4]{0,2,1:T(4,128)(2,1)S(1)} async-done(((bf16[128,32,4]{0,2,1:T(4,128)(2,1)}), bf16[128,32,4]{0,2,1:T(4,128)(2,1)S(1)}, u32[]{:S(2)}, u32[]{:S(2)}) %all-to-all-start.3) | async-done | bytes 32800 | tf_op jit(solution)/shard_map/all_to_all | solution.py:55
  57.0 42.8 %all-to-all-done.1 = bf16[128,32,256]{2,0,1:T(8,128)(2,1)} async-done(((bf16[128,32,256]{2,0,1:T(8,128)(2,1)}), bf16[128,32,256]{2,0,1:T(8,128)(2,1)}, u32[]{:S(2)}, u32[]{:S(2)}) %all-to-all-start.1) | async-done | bytes 2097184 | tf_op jit(solution)/shard_map/all_to_all | solution.py:54
  99.8 5.9 %all-to-all-start = ((bf16[128,32,256]{0,2,1:T(8,128)(2,1)}), bf16[128,32,256]{0,2,1:T(8,128)(2,1)S(1)}, u32[]{:S(2)}, u32[]{:S(2)}) async-start(bf16[128,32,256]{0,2,1:T(8,128)(2,1)} %bitcast.4), calls=%async_computation | async-start | bytes 4194304 | tf_op jit(solution)/shard_map/all_to_all | solution.py:53
  113.8 40.0 %all-to-all-done = bf16[128,32,256]{0,2,1:T(8,128)(2,1)S(1)} async-done(((bf16[128,32,256]{0,2,1:T(8,128)(2,1)}), bf16[128,32,256]{0,2,1:T(8,128)(2,1)S(1)}, u32[]{:S(2)}, u32[]{:S(2)}) %all-to-all-start) | async-done | bytes 2097184 | tf_op jit(solution)/shard_map/all_to_all | solution.py:53
  161.2 6.5 %fusion.41 = f32[16,4,128,64]{3,2,1,0:T(8,128)} fusion(f32[16,256,4]{1,2,0:T(4,128)S(1)} %copy.62, f32[16,256,128]{2,1,0:T(8,128)S(1)} %copy-done, bf16[16,256,4,64]{1,0,3,2:T(8,128)(2,1)S(1)} %reshape.89), kind=kOutput, calls=%fused_computation.49 | convolution fusion | flops 272629760 | bytes 6356992 | tf_op jit(solution)/shard_map/cshn,cshp->chnp/dot_general | solution.py:76
  167.7 49.3 %while.40 = (s32[]{:T(128)}, f32[4,128,64]{2,1,0:T(8,128)S(1)}, f32[4]{0:T(128)S(1)}, f32[16,4,128,64]{3,2,1,0:T(8,128)}, f32[16,4]{1,0:T(8,128)}, /*index=5*/f3...) while((s32[]{:T(128)}, f32[4,128,64]{2,1,0:T(8,128)S(1)}, f32[4]{0:T(128)S(1)}, ...), condition=%wide.region_3.4_spmd.clone, body=%wide.region_2.3_spmd.clone.sunk | while | flops 131083 | bytes 787189 | solution.py:91
  217.0 137.0 %while.38 = (s32[]{:T(128)}, f32[4,128,64]{2,1,0:T(8,128)S(1)}, f32[4]{0:T(128)S(1)}, f32[4,128,64]{2,1,0:T(8,128)S(1)}, s32[]{:T(128)}) while((s32[]{:T(128)}, f32[4,128,64]{2,1,0:T(8,128)S(1)}, f32[4]{0:T(128)S(1)}, f32[4,128,64]{2,1,0:T(8,128)S(1)}, s32[]{:T(128)}) %tuple.76), condition=%wide.region_5.6_spmd, body=%wide.region_4.5_spmd.sunk | while | flops 65538 | bytes 917621 | solution.py:99
  217.1 7.7 %collective-permute-start = (f32[4,128,64]{2,1,0:T(8,128)S(1)}, f32[4,128,64]{2,1,0:T(8,128)S(1)}, u32[]{:S(2)}, u32[]{:S(2)}) collective-permute-start(f32[4,128,64]{2,1,0:T(8,128)S(1)} %multiply_add_fusion.3), channel_id=1, source_target_pairs={{0,32},{32,64},{64,96},{96,128},{128,160},{160,192},{192,224},{224... | collective-permute-start | bytes 393224 | tf_op jit(solution)/shard_map/while/body/eval_jaxpr/ppermute | solution.py:17
  228.2 5.6 %collective-permute-start = (f32[4,128,64]{2,1,0:T(8,128)S(1)}, f32[4,128,64]{2,1,0:T(8,128)S(1)}, u32[]{:S(2)}, u32[]{:S(2)}) collective-permute-start(f32[4,128,64]{2,1,0:T(8,128)S(1)} %multiply_add_fusion.3), channel_id=1, source_target_pairs={{0,32},{32,64},{64,96},{96,128},{128,160},{160,192},{192,224},{224... | collective-permute-start | bytes 393224 | tf_op jit(solution)/shard_map/while/body/eval_jaxpr/ppermute | solution.py:17
  237.2 5.6 %collective-permute-start = (f32[4,128,64]{2,1,0:T(8,128)S(1)}, f32[4,128,64]{2,1,0:T(8,128)S(1)}, u32[]{:S(2)}, u32[]{:S(2)}) collective-permute-start(f32[4,128,64]{2,1,0:T(8,128)S(1)} %multiply_add_fusion.3), channel_id=1, source_target_pairs={{0,32},{32,64},{64,96},{96,128},{128,160},{160,192},{192,224},{224... | collective-permute-start | bytes 393224 | tf_op jit(solution)/shard_map/while/body/eval_jaxpr/ppermute | solution.py:17
  246.2 5.6 %collective-permute-start = (f32[4,128,64]{2,1,0:T(8,128)S(1)}, f32[4,128,64]{2,1,0:T(8,128)S(1)}, u32[]{:S(2)}, u32[]{:S(2)}) collective-permute-start(f32[4,128,64]{2,1,0:T(8,128)S(1)} %multiply_add_fusion.3), channel_id=1, source_target_pairs={{0,32},{32,64},{64,96},{96,128},{128,160},{160,192},{192,224},{224... | collective-permute-start | bytes 393224 | tf_op jit(solution)/shard_map/while/body/eval_jaxpr/ppermute | solution.py:17
  255.2 5.6 %collective-permute-start = (f32[4,128,64]{2,1,0:T(8,128)S(1)}, f32[4,128,64]{2,1,0:T(8,128)S(1)}, u32[]{:S(2)}, u32[]{:S(2)}) collective-permute-start(f32[4,128,64]{2,1,0:T(8,128)S(1)} %multiply_add_fusion.3), channel_id=1, source_target_pairs={{0,32},{32,64},{64,96},{96,128},{128,160},{160,192},{192,224},{224... | collective-permute-start | bytes 393224 | tf_op jit(solution)/shard_map/while/body/eval_jaxpr/ppermute | solution.py:17
  264.2 5.6 %collective-permute-start = (f32[4,128,64]{2,1,0:T(8,128)S(1)}, f32[4,128,64]{2,1,0:T(8,128)S(1)}, u32[]{:S(2)}, u32[]{:S(2)}) collective-permute-start(f32[4,128,64]{2,1,0:T(8,128)S(1)} %multiply_add_fusion.3), channel_id=1, source_target_pairs={{0,32},{32,64},{64,96},{96,128},{128,160},{160,192},{192,224},{224... | collective-permute-start | bytes 393224 | tf_op jit(solution)/shard_map/while/body/eval_jaxpr/ppermute | solution.py:17
  282.2 5.6 %collective-permute-start = (f32[4,128,64]{2,1,0:T(8,128)S(1)}, f32[4,128,64]{2,1,0:T(8,128)S(1)}, u32[]{:S(2)}, u32[]{:S(2)}) collective-permute-start(f32[4,128,64]{2,1,0:T(8,128)S(1)} %multiply_add_fusion.3), channel_id=1, source_target_pairs={{0,32},{32,64},{64,96},{96,128},{128,160},{160,192},{192,224},{224... | collective-permute-start | bytes 393224 | tf_op jit(solution)/shard_map/while/body/eval_jaxpr/ppermute | solution.py:17
  291.2 5.6 %collective-permute-start = (f32[4,128,64]{2,1,0:T(8,128)S(1)}, f32[4,128,64]{2,1,0:T(8,128)S(1)}, u32[]{:S(2)}, u32[]{:S(2)}) collective-permute-start(f32[4,128,64]{2,1,0:T(8,128)S(1)} %multiply_add_fusion.3), channel_id=1, source_target_pairs={{0,32},{32,64},{64,96},{96,128},{128,160},{160,192},{192,224},{224... | collective-permute-start | bytes 393224 | tf_op jit(solution)/shard_map/while/body/eval_jaxpr/ppermute | solution.py:17
  300.2 5.6 %collective-permute-start = (f32[4,128,64]{2,1,0:T(8,128)S(1)}, f32[4,128,64]{2,1,0:T(8,128)S(1)}, u32[]{:S(2)}, u32[]{:S(2)}) collective-permute-start(f32[4,128,64]{2,1,0:T(8,128)S(1)} %multiply_add_fusion.3), channel_id=1, source_target_pairs={{0,32},{32,64},{64,96},{96,128},{128,160},{160,192},{192,224},{224... | collective-permute-start | bytes 393224 | tf_op jit(solution)/shard_map/while/body/eval_jaxpr/ppermute | solution.py:17
  309.2 5.6 %collective-permute-start = (f32[4,128,64]{2,1,0:T(8,128)S(1)}, f32[4,128,64]{2,1,0:T(8,128)S(1)}, u32[]{:S(2)}, u32[]{:S(2)}) collective-permute-start(f32[4,128,64]{2,1,0:T(8,128)S(1)} %multiply_add_fusion.3), channel_id=1, source_target_pairs={{0,32},{32,64},{64,96},{96,128},{128,160},{160,192},{192,224},{224... | collective-permute-start | bytes 393224 | tf_op jit(solution)/shard_map/while/body/eval_jaxpr/ppermute | solution.py:17
  318.2 5.6 %collective-permute-start = (f32[4,128,64]{2,1,0:T(8,128)S(1)}, f32[4,128,64]{2,1,0:T(8,128)S(1)}, u32[]{:S(2)}, u32[]{:S(2)}) collective-permute-start(f32[4,128,64]{2,1,0:T(8,128)S(1)} %multiply_add_fusion.3), channel_id=1, source_target_pairs={{0,32},{32,64},{64,96},{96,128},{128,160},{160,192},{192,224},{224... | collective-permute-start | bytes 393224 | tf_op jit(solution)/shard_map/while/body/eval_jaxpr/ppermute | solution.py:17
  327.2 5.6 %collective-permute-start = (f32[4,128,64]{2,1,0:T(8,128)S(1)}, f32[4,128,64]{2,1,0:T(8,128)S(1)}, u32[]{:S(2)}, u32[]{:S(2)}) collective-permute-start(f32[4,128,64]{2,1,0:T(8,128)S(1)} %multiply_add_fusion.3), channel_id=1, source_target_pairs={{0,32},{32,64},{64,96},{96,128},{128,160},{160,192},{192,224},{224... | collective-permute-start | bytes 393224 | tf_op jit(solution)/shard_map/while/body/eval_jaxpr/ppermute | solution.py:17
  367.4 70.7 %while.39 = (s32[]{:T(128)}, bf16[16,256,4,64]{1,3,2,0:T(8,128)(2,1)}, bf16[16,256,4,64]{1,3,2,0:T(8,128)(2,1)}, bf16[16,256,4,128]{3,1,2,0:T(8,128)(2,1)}, bf16...) while((s32[]{:T(128)}, ...), condition=%wide.region_7.8_spmd.clone, body=%wide.region_6.7_spmd.clone.sunk | while | flops 203096064 | bytes 2018925 | solution.py:131
  445.4 51.9 %all_to_all.77 = bf16[32,128,256]{1,2,0:T(8,128)(2,1)S(1)} all-to-all(bf16[32,128,256]{1,2,0:T(8,128)(2,1)S(1)} %copy.71), channel_id=1, replica_groups=mesh['sec'=16,'cp'=32] {'cp'}, dimensions={0} | all-to-all | bytes 4194304 | tf_op jit(solution)/shard_map/all_to_all | solution.py:133
  (253 shorter events, 247.8 us)
Async XLA Ops:
  1.0 20.3 %collective-permute-start.1 = (bf16[3,10240]{1,0:T(4,128)(2,1)S(1)}, bf16[3,10240]{1,0:T(4,128)(2,1)S(1)}, u32[]{:S(2)}, u32[]{:S(2)}) collective-permute-start(bf16[3,10240]{1,0:T(4,128)(2,1)S(1)} %slice.49), channel_id=1, source_target_pairs={{0,1},{1,2},{2,3},{3,4},{4,5},{5,6},{6,7},{7,8},{8,9},{9,10},{10,1... | collective-permute-start | bytes 184328 | tf_op jit(solution)/shard_map/ppermute | solution.py:17
  6.4 22.2 %all-to-all-start.2 = ((bf16[128,32,4]{0,2,1:T(4,128)(2,1)}), bf16[128,32,4]{0,2,1:T(4,128)(2,1)S(1)}, u32[]{:S(2)}, u32[]{:S(2)}) async-start(bf16[128,32,4]{0,2,1:T(4,128)(2,1)} %bitcast.13), calls=%async_computation.2 | async-start | bytes 65536 | tf_op jit(solution)/shard_map/all_to_all | solution.py:56
  28.6 18.0 %all-to-all-start.3 = ((bf16[128,32,4]{0,2,1:T(4,128)(2,1)}), bf16[128,32,4]{0,2,1:T(4,128)(2,1)S(1)}, u32[]{:S(2)}, u32[]{:S(2)}) async-start(bf16[128,32,4]{0,2,1:T(4,128)(2,1)} %bitcast.17), calls=%async_computation.3 | async-start | bytes 65536 | tf_op jit(solution)/shard_map/all_to_all | solution.py:55
  46.6 53.2 %all-to-all-start.1 = ((bf16[128,32,256]{2,0,1:T(8,128)(2,1)}), bf16[128,32,256]{2,0,1:T(8,128)(2,1)}, u32[]{:S(2)}, u32[]{:S(2)}) async-start(bf16[128,32,256]{2,0,1:T(8,128)(2,1)} %pad_maximum_fusion.1), calls=%async_computation.1 | async-start | bytes 4194304 | tf_op jit(solution)/shard_map/all_to_all | solution.py:54
  52.9 52.9 %copy-start.3 = (f32[128]{0:T(128)S(1)}, f32[128]{0:T(128)}, u32[]{:S(2)}) copy-start(f32[128]{0:T(128)} %param.17) | copy-start | bytes 1540
  99.8 53.9 %all-to-all-start = ((bf16[128,32,256]{0,2,1:T(8,128)(2,1)}), bf16[128,32,256]{0,2,1:T(8,128)(2,1)S(1)}, u32[]{:S(2)}, u32[]{:S(2)}) async-start(bf16[128,32,256]{0,2,1:T(8,128)(2,1)} %bitcast.4), calls=%async_computation | async-start | bytes 4194304 | tf_op jit(solution)/shard_map/all_to_all | solution.py:53
  159.1 2.1 copy-start
  217.0 137.1 %copy-start.2 = (f32[16,4]{1,0:T(8,128)S(1)}, f32[16,4]{1,0:T(8,128)}, u32[]{:S(2)}) copy-start(f32[16,4]{1,0:T(8,128)} %get-tuple-element.120) | copy-start | bytes 772
  217.1 11.0 %collective-permute-start = (f32[4,128,64]{2,1,0:T(8,128)S(1)}, f32[4,128,64]{2,1,0:T(8,128)S(1)}, u32[]{:S(2)}, u32[]{:S(2)}) collective-permute-start(f32[4,128,64]{2,1,0:T(8,128)S(1)} %multiply_add_fusion.3), channel_id=1, source_target_pairs={{0,32},{32,64},{64,96},{96,128},{128,160},{160,192},{192,224},{224... | collective-permute-start | bytes 393224 | tf_op jit(solution)/shard_map/while/body/eval_jaxpr/ppermute | solution.py:17
  228.2 8.9 %collective-permute-start = (f32[4,128,64]{2,1,0:T(8,128)S(1)}, f32[4,128,64]{2,1,0:T(8,128)S(1)}, u32[]{:S(2)}, u32[]{:S(2)}) collective-permute-start(f32[4,128,64]{2,1,0:T(8,128)S(1)} %multiply_add_fusion.3), channel_id=1, source_target_pairs={{0,32},{32,64},{64,96},{96,128},{128,160},{160,192},{192,224},{224... | collective-permute-start | bytes 393224 | tf_op jit(solution)/shard_map/while/body/eval_jaxpr/ppermute | solution.py:17
  237.2 8.9 %collective-permute-start = (f32[4,128,64]{2,1,0:T(8,128)S(1)}, f32[4,128,64]{2,1,0:T(8,128)S(1)}, u32[]{:S(2)}, u32[]{:S(2)}) collective-permute-start(f32[4,128,64]{2,1,0:T(8,128)S(1)} %multiply_add_fusion.3), channel_id=1, source_target_pairs={{0,32},{32,64},{64,96},{96,128},{128,160},{160,192},{192,224},{224... | collective-permute-start | bytes 393224 | tf_op jit(solution)/shard_map/while/body/eval_jaxpr/ppermute | solution.py:17
  246.2 8.9 %collective-permute-start = (f32[4,128,64]{2,1,0:T(8,128)S(1)}, f32[4,128,64]{2,1,0:T(8,128)S(1)}, u32[]{:S(2)}, u32[]{:S(2)}) collective-permute-start(f32[4,128,64]{2,1,0:T(8,128)S(1)} %multiply_add_fusion.3), channel_id=1, source_target_pairs={{0,32},{32,64},{64,96},{96,128},{128,160},{160,192},{192,224},{224... | collective-permute-start | bytes 393224 | tf_op jit(solution)/shard_map/while/body/eval_jaxpr/ppermute | solution.py:17
  255.2 8.9 %collective-permute-start = (f32[4,128,64]{2,1,0:T(8,128)S(1)}, f32[4,128,64]{2,1,0:T(8,128)S(1)}, u32[]{:S(2)}, u32[]{:S(2)}) collective-permute-start(f32[4,128,64]{2,1,0:T(8,128)S(1)} %multiply_add_fusion.3), channel_id=1, source_target_pairs={{0,32},{32,64},{64,96},{96,128},{128,160},{160,192},{192,224},{224... | collective-permute-start | bytes 393224 | tf_op jit(solution)/shard_map/while/body/eval_jaxpr/ppermute | solution.py:17
  264.2 8.9 %collective-permute-start = (f32[4,128,64]{2,1,0:T(8,128)S(1)}, f32[4,128,64]{2,1,0:T(8,128)S(1)}, u32[]{:S(2)}, u32[]{:S(2)}) collective-permute-start(f32[4,128,64]{2,1,0:T(8,128)S(1)} %multiply_add_fusion.3), channel_id=1, source_target_pairs={{0,32},{32,64},{64,96},{96,128},{128,160},{160,192},{192,224},{224... | collective-permute-start | bytes 393224 | tf_op jit(solution)/shard_map/while/body/eval_jaxpr/ppermute | solution.py:17
  273.2 8.9 %collective-permute-start = (f32[4,128,64]{2,1,0:T(8,128)S(1)}, f32[4,128,64]{2,1,0:T(8,128)S(1)}, u32[]{:S(2)}, u32[]{:S(2)}) collective-permute-start(f32[4,128,64]{2,1,0:T(8,128)S(1)} %multiply_add_fusion.3), channel_id=1, source_target_pairs={{0,32},{32,64},{64,96},{96,128},{128,160},{160,192},{192,224},{224... | collective-permute-start | bytes 393224 | tf_op jit(solution)/shard_map/while/body/eval_jaxpr/ppermute | solution.py:17
  282.2 8.9 %collective-permute-start = (f32[4,128,64]{2,1,0:T(8,128)S(1)}, f32[4,128,64]{2,1,0:T(8,128)S(1)}, u32[]{:S(2)}, u32[]{:S(2)}) collective-permute-start(f32[4,128,64]{2,1,0:T(8,128)S(1)} %multiply_add_fusion.3), channel_id=1, source_target_pairs={{0,32},{32,64},{64,96},{96,128},{128,160},{160,192},{192,224},{224... | collective-permute-start | bytes 393224 | tf_op jit(solution)/shard_map/while/body/eval_jaxpr/ppermute | solution.py:17
  291.2 8.9 %collective-permute-start = (f32[4,128,64]{2,1,0:T(8,128)S(1)}, f32[4,128,64]{2,1,0:T(8,128)S(1)}, u32[]{:S(2)}, u32[]{:S(2)}) collective-permute-start(f32[4,128,64]{2,1,0:T(8,128)S(1)} %multiply_add_fusion.3), channel_id=1, source_target_pairs={{0,32},{32,64},{64,96},{96,128},{128,160},{160,192},{192,224},{224... | collective-permute-start | bytes 393224 | tf_op jit(solution)/shard_map/while/body/eval_jaxpr/ppermute | solution.py:17
  300.2 8.9 %collective-permute-start = (f32[4,128,64]{2,1,0:T(8,128)S(1)}, f32[4,128,64]{2,1,0:T(8,128)S(1)}, u32[]{:S(2)}, u32[]{:S(2)}) collective-permute-start(f32[4,128,64]{2,1,0:T(8,128)S(1)} %multiply_add_fusion.3), channel_id=1, source_target_pairs={{0,32},{32,64},{64,96},{96,128},{128,160},{160,192},{192,224},{224... | collective-permute-start | bytes 393224 | tf_op jit(solution)/shard_map/while/body/eval_jaxpr/ppermute | solution.py:17
  309.2 8.9 %collective-permute-start = (f32[4,128,64]{2,1,0:T(8,128)S(1)}, f32[4,128,64]{2,1,0:T(8,128)S(1)}, u32[]{:S(2)}, u32[]{:S(2)}) collective-permute-start(f32[4,128,64]{2,1,0:T(8,128)S(1)} %multiply_add_fusion.3), channel_id=1, source_target_pairs={{0,32},{32,64},{64,96},{96,128},{128,160},{160,192},{192,224},{224... | collective-permute-start | bytes 393224 | tf_op jit(solution)/shard_map/while/body/eval_jaxpr/ppermute | solution.py:17
  318.2 8.9 %collective-permute-start = (f32[4,128,64]{2,1,0:T(8,128)S(1)}, f32[4,128,64]{2,1,0:T(8,128)S(1)}, u32[]{:S(2)}, u32[]{:S(2)}) collective-permute-start(f32[4,128,64]{2,1,0:T(8,128)S(1)} %multiply_add_fusion.3), channel_id=1, source_target_pairs={{0,32},{32,64},{64,96},{96,128},{128,160},{160,192},{192,224},{224... | collective-permute-start | bytes 393224 | tf_op jit(solution)/shard_map/while/body/eval_jaxpr/ppermute | solution.py:17
  327.2 8.9 %collective-permute-start = (f32[4,128,64]{2,1,0:T(8,128)S(1)}, f32[4,128,64]{2,1,0:T(8,128)S(1)}, u32[]{:S(2)}, u32[]{:S(2)}) collective-permute-start(f32[4,128,64]{2,1,0:T(8,128)S(1)} %multiply_add_fusion.3), channel_id=1, source_target_pairs={{0,32},{32,64},{64,96},{96,128},{128,160},{160,192},{192,224},{224... | collective-permute-start | bytes 393224 | tf_op jit(solution)/shard_map/while/body/eval_jaxpr/ppermute | solution.py:17
  336.2 8.9 %collective-permute-start = (f32[4,128,64]{2,1,0:T(8,128)S(1)}, f32[4,128,64]{2,1,0:T(8,128)S(1)}, u32[]{:S(2)}, u32[]{:S(2)}) collective-permute-start(f32[4,128,64]{2,1,0:T(8,128)S(1)} %multiply_add_fusion.3), channel_id=1, source_target_pairs={{0,32},{32,64},{64,96},{96,128},{128,160},{160,192},{192,224},{224... | collective-permute-start | bytes 393224 | tf_op jit(solution)/shard_map/while/body/eval_jaxpr/ppermute | solution.py:17
  345.2 8.9 %collective-permute-start = (f32[4,128,64]{2,1,0:T(8,128)S(1)}, f32[4,128,64]{2,1,0:T(8,128)S(1)}, u32[]{:S(2)}, u32[]{:S(2)}) collective-permute-start(f32[4,128,64]{2,1,0:T(8,128)S(1)} %multiply_add_fusion.3), channel_id=1, source_target_pairs={{0,32},{32,64},{64,96},{96,128},{128,160},{160,192},{192,224},{224... | collective-permute-start | bytes 393224 | tf_op jit(solution)/shard_map/while/body/eval_jaxpr/ppermute | solution.py:17
  361.4 3.0 copy-start.1
where the time goes:
time: 504 us; the launch traced here: 500 us
  waiting for transfers between devices  139 us (28%)
  starting transfers between devices  122 us (24%)
  local copies, waits for them, and re-layouts  73 us (14%)
  matrix products  65.3 us (13%)
  blocking collectives  51.9 us (10%)
  other arithmetic  48.3 us (10%)
    ppermute x16, starting transfers between devices, passed_along(): lax.ppermute(value, axis, [(source, source + steps) for source in range(l...  90.1 us
    all_to_all x1, blocking collectives, per_device(): lax.all_to_all(outputs, 'cp', split_axis=0, concat_axis=1, tiled=True)  51.9 us
    ppermute x16, waiting for transfers between devices, passed_along(): lax.ppermute(value, axis, [(source, source + steps) for source in range(l...  49.4 us
    all_to_all x1, waiting for transfers between devices, per_device(): lax.all_to_all(send_bc, 'cp', split_axis=1, concat_axis=0, tiled=True)  42.8 us
    all_to_all x1, waiting for transfers between devices, per_device(): lax.all_to_all(mixed_cols[:, :width_x], 'cp', split_axis=1, concat_axis=0...  40 us
    dot_general x16, matrix products, block_output(): jnp.einsum('hts,shp->thp', mix_weights, xblock, preferred_element_type=jn...  37.3 us
    dot_general x16, matrix products, block_output(): jnp.einsum('thn,hnp->thp', cblock.astype(jnp.float32), stateblock, precis...  21.4 us
    dynamic_update_slice x16, local copies, waits for them, and re-layouts, per_device(): lax.scan(advance, (start_state, start_decay), (block_states, block_gain))  20.7 us
  transfers between devices with their start and end apart: 20, of which 18 were waited for; matrix products, arithmetic and copies ran while one was open for 5% of the time, Pallas kernels for 0%

commit v1 on v0

v1 whole, which is shorter than its diff:
```python
import jax
import jax.numpy as jnp
from jax import lax
from jax.experimental import pallas as pl
from jax.experimental.pallas import tpu as pltpu
from jax.sharding import PartitionSpec as P

HEAD_COUNT = 128
P_SIZE = 64
N = 128
G = 8
KERNEL = 4
GROUP_HEADS = HEAD_COUNT // G
GROUP_WIDTH = GROUP_HEADS * P_SIZE
WIDTH_X = HEAD_COUNT * P_SIZE
F32 = jnp.float32
BF16 = jnp.bfloat16


def lower_ones(rows):
    down = lax.broadcasted_iota(jnp.int32, (rows, rows), 0)
    across = lax.broadcasted_iota(jnp.int32, (rows, rows), 1)
    return down >= across


def dot(a, b, a_dim, b_dim):
    return lax.dot_general(a, b, (((a_dim,), (b_dim,)), ((), ())), preferred_element_type=F32)


def running_sum(decay):
    return dot(lower_ones(decay.shape[0]).astype(BF16), decay, 1, 0)


def over_heads(columns):
    rows = columns.shape[0]
    left = lax.broadcasted_iota(jnp.int32, (rows, 2 * P_SIZE), 1) < P_SIZE
    return jnp.concatenate(
        [
            jnp.where(left, columns[:, h : h + 1], columns[:, h + 1 : h + 2])
            for h in range(0, columns.shape[1], 2)
        ],
        axis=1,
    )


def conv_silu(columns, rim, weights, biases, pad):
    rows = columns.shape[0]
    width = columns.shape[1]
    pad[8 - (KERNEL - 1) : 8, 0:width] = rim.astype(F32)
    pad[8 : 8 + rows, 0:width] = columns.astype(F32)
    summed = biases
    for tap in range(KERNEL):
        first = 8 - (KERNEL - 1) + tap
        summed = summed + weights[tap : tap + 1, :] * pad[first : first + rows, 0:width]
    return (summed / (1.0 + jnp.exp(-summed))).astype(BF16)


def conv_states_kernel(
    x_in, b_in, c_in, x_rim, b_rim, c_rim, x_w, b_w, c_w, x_bias, b_bias, c_bias, step, decay,
    x_out, b_out, c_out, states, pad,
):
    values = conv_silu(x_in[...], x_rim[...], x_w[...], x_bias[...], pad)
    keys_b = conv_silu(b_in[...], b_rim[...], b_w[...], b_bias[...], pad)
    query_c = conv_silu(c_in[...], c_rim[...], c_w[...], c_bias[...], pad)
    x_out[...] = values
    b_out[...] = keys_b
    c_out[...] = query_c
    running = running_sum(decay[0])
    rows = running.shape[0]
    weight = jnp.exp(running[rows - 1 : rows, :] - running) * step[0].astype(F32)
    weighted = (values.astype(F32) * over_heads(weight)).astype(BF16)
    targets, _, width = states.shape
    for target in range(targets):
        states[target] = dot(
            keys_b, weighted[:, target * width : (target + 1) * width], 0, 0
        ).astype(BF16)


def within_kernel(x_in, b_in, c_in, step_t, decay, decay_t, skip, out):
    scores = dot(c_in[...], b_in[...], 1, 1)
    causal = lower_ones(scores.shape[0])
    running = running_sum(decay[0])
    running_t = dot(decay_t[0], causal.astype(BF16), 1, 1)
    steps = step_t[0].astype(F32)
    scores = jnp.where(causal, scores, 0.0)
    for pair in range(GROUP_HEADS // 2):
        parts = []
        x_pair = x_in[:, pair * 2 * P_SIZE : (pair + 1) * 2 * P_SIZE]
        for h in (2 * pair, 2 * pair + 1):
            gap = jnp.where(causal, running[:, h : h + 1] - running_t[h : h + 1, :], -jnp.inf)
            mix = (scores * jnp.exp(gap) * steps[h : h + 1, :]).astype(BF16)
            parts.append(dot(mix, x_pair[:, (h % 2) * P_SIZE : (h % 2 + 1) * P_SIZE], 1, 0))
        at = slice(pair * 2 * P_SIZE, (pair + 1) * 2 * P_SIZE)
        out[:, at] = jnp.concatenate(parts, axis=1) + skip[:, at] * x_pair.astype(F32)


def section_total_kernel(states, gains, total):
    chunks = states.shape[0]
    for part in range(N // 32):
        at = slice(part * 32, (part + 1) * 32)
        carried = states[0, at, :].astype(F32)
        for chunk in range(1, chunks):
            carried = gains[chunk : chunk + 1, :] * carried + states[chunk, at, :].astype(F32)
        total[at, :] = carried


def entering_kernel(states, gains, totals, section_gains, entering):
    chunks = states.shape[0]
    sections = totals.shape[0]
    for part in range(N // 32):
        at = slice(part * 32, (part + 1) * 32)
        carried = section_gains[0:1, :] * totals[0, at, :].astype(F32)
        for section in range(1, sections):
            carried = carried + section_gains[section : section + 1, :] * totals[
                section, at, :
            ].astype(F32)
        for chunk in range(chunks):
            entering[chunk, at, :] = carried.astype(BF16)
            carried = gains[chunk : chunk + 1, :] * carried + states[chunk, at, :].astype(F32)


def outputs_kernel(within, c_in, decay, entering, out):
    growth = over_heads(jnp.exp(running_sum(decay[0])))
    query_c = c_in[...]
    targets, _, width = entering.shape
    for target in range(targets):
        at = slice(target * width, (target + 1) * width)
        out[:, at] = (within[:, at] + growth[:, at] * dot(query_c, entering[target], 1, 0)).astype(
            BF16
        )


def whole(shape):
    return pl.BlockSpec(shape, lambda g: (0,) * len(shape))


def per_device(projected, conv_weight, conv_bias, step_size, log_decay, skip_gain):
    targets = lax.axis_size("cp")
    sections = lax.axis_size("sec")
    rows = projected.shape[0]
    width_all = projected.shape[1]
    heads_here = HEAD_COUNT // targets
    width_here = heads_here * P_SIZE
    group_targets = targets // G
    devices = targets * sections

    rim = lax.ppermute(
        projected[rows - (KERNEL - 1) :],
        ("sec", "cp"),
        [(source, source + 1) for source in range(devices - 1)],
    )
    chunk_decay = jnp.sum(log_decay.astype(F32), axis=0, keepdims=True)
    all_decay = lax.all_gather(chunk_decay, ("sec", "cp"), axis=0, tiled=True)

    decay_g = log_decay.reshape(rows, G, GROUP_HEADS).transpose(1, 0, 2)
    step_g = step_size.reshape(rows, G, GROUP_HEADS).transpose(1, 0, 2)
    decay_t = log_decay.T.reshape(G, GROUP_HEADS, rows)
    step_t = step_size.T.reshape(G, GROUP_HEADS, rows)
    bias = conv_bias.reshape(1, width_all)
    skip_wide = jnp.repeat(skip_gain, P_SIZE).reshape(1, WIDTH_X)

    b_first = WIDTH_X // N
    c_first = b_first + G

    def x_spec(height):
        return pl.BlockSpec((height, GROUP_WIDTH), lambda g: (0, g))

    def bc_spec(height, first=0):
        return pl.BlockSpec((height, N), lambda g: (0, first + g))

    def three(height):
        return [x_spec(height), bc_spec(height, b_first), bc_spec(height, c_first)]

    head_spec = pl.BlockSpec((1, rows, GROUP_HEADS), lambda g: (g, 0, 0))
    head_t_spec = pl.BlockSpec((1, GROUP_HEADS, rows), lambda g: (g, 0, 0))
    states_spec = pl.BlockSpec((group_targets, N, width_here), lambda g: (g, 0, 0))
    params = pltpu.CompilerParams(vmem_limit_bytes=48 * 2**20)

    values, keys_b, query_c, states = pl.pallas_call(
        conv_states_kernel,
        grid=(G,),
        in_specs=three(rows) + three(KERNEL - 1) + three(KERNEL) + three(1) + [head_spec, head_spec],
        out_specs=[x_spec(rows), bc_spec(rows), bc_spec(rows), states_spec],
        out_shape=[
            jax.ShapeDtypeStruct((rows, WIDTH_X), BF16),
            jax.ShapeDtypeStruct((rows, G * N), BF16),
            jax.ShapeDtypeStruct((rows, G * N), BF16),
            jax.ShapeDtypeStruct((targets, N, width_here), BF16),
        ],
        scratch_shapes=[pltpu.VMEM((rows + 8, GROUP_WIDTH), F32)],
        compiler_params=params,
        name="conv_states",
    )(
        projected, projected, projected, rim, rim, rim, conv_weight, conv_weight, conv_weight,
        bias, bias, bias, step_g, decay_g,
    )

    states_here = lax.all_to_all(states, "cp", split_axis=0, concat_axis=0, tiled=True)

    within = pl.pallas_call(
        within_kernel,
        grid=(G,),
        in_specs=[x_spec(rows), bc_spec(rows), bc_spec(rows), head_t_spec, head_spec, head_t_spec, x_spec(1)],
        out_specs=x_spec(rows),
        out_shape=jax.ShapeDtypeStruct((rows, WIDTH_X), F32),
        compiler_params=params,
        name="within",
    )(values, keys_b, query_c, step_t, decay_g, decay_t, skip_wide)

    section = lax.axis_index("sec")
    position = lax.axis_index("cp")
    decay_here = lax.dynamic_slice_in_dim(all_decay, position * heads_here, heads_here, 1)
    decay_here = decay_here.reshape(sections, targets, heads_here)
    chunk_gain = jnp.exp(lax.dynamic_index_in_dim(decay_here, section, 0, keepdims=False))
    chunk_gain = jnp.repeat(chunk_gain, P_SIZE, axis=1)
    section_decay = jnp.sum(decay_here, axis=1)
    earlier = lax.broadcasted_iota(jnp.int32, (sections, sections), 0)
    later = lax.broadcasted_iota(jnp.int32, (sections, sections), 1)
    between = (later > earlier) & (later < section)
    section_gap = jnp.sum(jnp.where(between[:, :, None], section_decay[None], 0.0), axis=1)
    before = lax.broadcasted_iota(jnp.int32, (sections, 1), 0) < section
    section_gain = jnp.where(before, jnp.exp(section_gap), 0.0)
    section_gain = jnp.repeat(section_gain, P_SIZE, axis=1)

    total = pl.pallas_call(
        section_total_kernel,
        out_shape=jax.ShapeDtypeStruct((N, width_here), F32),
        compiler_params=params,
        name="section_total",
    )(states_here, chunk_gain)
    totals = lax.all_gather(total, "sec")
    entering = pl.pallas_call(
        entering_kernel,
        out_shape=jax.ShapeDtypeStruct((targets, N, width_here), BF16),
        compiler_params=params,
        name="entering",
    )(states_here, chunk_gain, totals, section_gain)

    entering_all = lax.all_to_all(entering, "cp", split_axis=0, concat_axis=0, tiled=True)

    return pl.pallas_call(
        outputs_kernel,
        grid=(G,),
        in_specs=[x_spec(rows), bc_spec(rows), head_spec, states_spec],
        out_specs=x_spec(rows),
        out_shape=jax.ShapeDtypeStruct((rows, WIDTH_X), BF16),
        compiler_params=params,
        name="outputs",
    )(within, query_c, decay_g, entering_all)


def solution(mesh):
    in_specs = (
        P(("sec", "cp"), None),
        P(),
        P(),
        P(("sec", "cp"), None),
        P(("sec", "cp"), None),
        P(),
    )
    out_specs = P(("sec", "cp"), None)
    return jax.shard_map(
        per_device, mesh=mesh, in_specs=in_specs, out_specs=out_specs, check_vma=False
    )
```

time: 504 us -> 291 us (0.58)
  the two profiles are of different devices: /device:TPU:25 before, /device:TPU:8 now
where the time goes in v1:
time: 291 us; the launch traced here: 290 us
  blocking collectives  127 us (44%)
  waiting for transfers between devices  87.2 us (30%)
  Pallas kernels  29.9 us (10%)
  starting transfers between devices  20.9 us (7%)
  between operations  13.6 us (5%)
  local copies, waits for them, and re-layouts  12.1 us (4%)
    all_gather x1, blocking collectives, per_device(): all_decay = lax.all_gather(chunk_decay, ('sec', 'cp'), axis=0, tiled=True)  127 us
    all_to_all x1, waiting for transfers between devices, per_device(): lax.all_to_all(entering, 'cp', split_axis=0, concat_axis=0, tiled=True)  39.8 us
    all_gather x1, waiting for transfers between devices, per_device(): totals = lax.all_gather(total, 'sec')  39.2 us
    all_to_all x1, starting transfers between devices, per_device(): lax.all_to_all(entering, 'cp', split_axis=0, concat_axis=0, tiled=True)  10.3 us
    pallas_call x1, Pallas kernels, per_device(): pl.pallas_call(conv_states_kernel, grid=(G,), in_specs=three(rows) + thre...  9.87 us
    unnamed x22, local copies, waits for them, and re-layouts  9.15 us
    pallas_call x1, Pallas kernels, per_device(): pl.pallas_call(within_kernel, grid=(G,), in_specs=[x_spec(rows), bc_spec(...  8.56 us
    ppermute x1, waiting for transfers between devices, per_device(): lax.ppermute(projected[rows - (KERNEL - 1):], ('sec', 'cp'), [(source, so...  8.17 us
  transfers between devices with their start and end apart: 4, of which 3 were waited for; matrix products, arithmetic and copies ran while one was open for 1% of the time, Pallas kernels for 3%

profile of v1, /device:TPU:8, one launch (start us, length us, event | category | flops | bytes accessed | tf_op | source)
XLA Modules:
  0.0 290.3 jit_solution(2793201628531442943)
XLA Ops:
  6.5 1.0 slice.3
  7.5 4.3 %collective-permute-start = (bf16[3,10240]{1,0:T(4,128)(2,1)S(1)}, bf16[3,10240]{1,0:T(4,128)(2,1)S(1)}, u32[]{:S(2)}, u32[]{:S(2)}) collective-permute-start(bf16[3,10240]{1,0:T(4,128)(2,1)S(1)} %slice.3), channel_id=1, source_target_pairs={{0,1},{1,2},{2,3},{3,4},{4,5},{5,6},{6,7},{7,8},{8,9},{9,10},{10,1... | collective-permute-start | bytes 184328 | tf_op jit(solution)/shard_map/ppermute | solution.py:147
  11.8 0.9 copy.29
  12.7 0.2 copy.30
  12.8 0.9 copy.27
  13.7 0.2 copy.28
  13.9 8.2 %collective-permute-done.x_rim.b_rim.c_rim = bf16[3,10240]{1,0:T(4,128)(2,1)S(1)} collective-permute-done((bf16[3,10240]{1,0:T(4,128)(2,1)S(1)}, bf16[3,10240]{1,0:T(4,128)(2,1)S(1)}, u32[]{:S(2)}, u32[]{:S(2)}) %collective-permute-start) | collective-permute-done | bytes 61472 | tf_op jit(solution)/shard_map/ppermute | solution.py:147
  22.1 0.9 copy-done.4
  23.0 0.8 copy-done.5
  23.8 9.9 %conv_states.1 = (bf16[128,8192]{1,0:T(8,128)(2,1)S(1)}, bf16[128,1024]{1,0:T(8,128)(2,1)S(1)}, bf16[128,1024]{1,0:T(8,128)(2,1)S(1)}, bf16[32,128,256]{2,1,0:T(8,128)(2,1)S(1)}) custom-call(bf16[128,10240]{1,0:T(8,128)(2,1)} %c_in.1, bf16[128,10240]{1,0:T(8,128)(2,1)} %c_in.1, bf16[128,10240]{1,0:T(8,128)(2,1)} %c_in.1, ...), custom_call_target="tpu_custom_call" | custom-call | tf_op jit(solution)/shard_map/conv_states/pallas_call | solution.py:179
  33.7 1.3 copy-done.1
  35.0 1.3 copy-done.3
  36.3 6.2 %all-to-all-start = ((bf16[32,128,256]{2,1,0:T(8,128)(2,1)}), bf16[32,128,256]{2,1,0:T(8,128)(2,1)S(1)}, u32[]{:S(2)}, u32[]{:S(2)}) async-start(bf16[32,128,256]{2,1,0:T(8,128)(2,1)} %copy-done.3), calls=%async_computation | async-start | bytes 4194304 | tf_op jit(solution)/shard_map/all_to_all | solution.py:198
  42.6 126.6 %all-gather.2 = f32[512,1,128]{2,1,0:T(1,128)S(1)} all-gather(f32[1,1,128]{2,1,0:T(1,128)S(1)} %bitcast.32), channel_id=2, replica_groups=mesh['sec'=16,'cp'=32] {'sec','cp'}, dimensions={0}, use_global_device_ids=true | all-gather | bytes 262656 | tf_op jit(solution)/shard_map/all_gather | solution.py:153
  169.2 0.6 constant_dynamic-slice_fusion
  170.2 1.1 section_total.1
  171.9 39.2 %all-gather.5.cloned.1.call-done = f32[2048,256]{1,0:T(8,128)} async-done(((f32[128,256]{1,0:T(8,128)}), f32[2048,256]{1,0:T(8,128)}) %all-gather.5.cloned.1.call-update) | async-done | bytes 2097168 | tf_op jit(solution)/shard_map/all_gather | solution.py:231
  211.1 2.2 entering.1
  213.3 1.3 copy-done
  214.6 10.3 %all-to-all-start.1 = ((bf16[32,128,256]{2,1,0:T(8,128)(2,1)}), bf16[32,128,256]{2,1,0:T(8,128)(2,1)S(1)}, u32[]{:S(2)}, u32[]{:S(2)}) async-start(bf16[32,128,256]{2,1,0:T(8,128)(2,1)} %copy-done), calls=%async_computation.1 | async-start | bytes 4194304 | tf_op jit(solution)/shard_map/all_to_all | solution.py:239
  225.4 1.6 copy-done.2
  227.0 8.6 %within.1 = f32[128,8192]{1,0:T(8,128)} custom-call(bf16[128,8192]{1,0:T(8,128)(2,1)S(1)} %copy-done.2, bf16[128,1024]{1,0:T(8,128)(2,1)S(1)} %get-tuple-element.10.b_in, bf16[128,1024]{1,0:T(8,128)(2,1)S(1)} %get-tuple-element.11.c_in, bf16[8,16,128]{2,1,0:T(8,128)(2,1)S(1)} %bitcast.22, bf16[8,128,16]{2,1,0:T(8,128)(2,1)S(1)} %bitcast.16, ...), custom_call_target="tpu_custom_call" | custom-call | tf_op jit(solution)/shard_map/within/pallas_call | solution.py:200
  235.6 39.8 %all-to-all-done.1.entering = bf16[32,128,256]{2,1,0:T(8,128)(2,1)S(1)} async-done(((bf16[32,128,256]{2,1,0:T(8,128)(2,1)}), bf16[32,128,256]{2,1,0:T(8,128)(2,1)S(1)}, u32[]{:S(2)}, u32[]{:S(2)}) %all-to-all-start.1) | async-done | bytes 2097184 | tf_op jit(solution)/shard_map/all_to_all | solution.py:239
  275.3 8.2 %outputs.1 = bf16[128,8192]{1,0:T(8,128)(2,1)} custom-call(f32[128,8192]{1,0:T(8,128)} %within.1, bf16[128,1024]{1,0:T(8,128)(2,1)S(1)} %get-tuple-element.11.c_in, bf16[8,128,16]{2,1,0:T(8,128)(2,1)S(1)} %bitcast.17, bf16[32,128,256]{2,1,0:T(8,128)(2,1)S(1)} %all-to-all-done.1.entering), custom_call_target="tpu_custom_call" | custom-call | tf_op jit(solution)/shard_map/outputs/pallas_call | solution.py:241
  (34 shorter events, 1.4 us)
Async XLA Ops:
  7.5 14.6 %collective-permute-start = (bf16[3,10240]{1,0:T(4,128)(2,1)S(1)}, bf16[3,10240]{1,0:T(4,128)(2,1)S(1)}, u32[]{:S(2)}, u32[]{:S(2)}) collective-permute-start(bf16[3,10240]{1,0:T(4,128)(2,1)S(1)} %slice.3), channel_id=1, source_target_pairs={{0,1},{1,2},{2,3},{3,4},{4,5},{5,6},{6,7},{7,8},{8,9},{9,10},{10,1... | collective-permute-start | bytes 184328 | tf_op jit(solution)/shard_map/ppermute | solution.py:147
  22.1 0.9 copy-start.4
  23.0 0.8 copy-start.5
  33.7 1.3 copy-start.1
  35.0 1.3 copy-start.3
  36.3 6.3 %copy-start.6 = (bf16[128,128]{1,0:T(8,128)(2,1)S(1)}, bf16[128,128]{1,0:T(8,128)(2,1)}, u32[]{:S(2)}) copy-start(bf16[128,128]{1,0:T(8,128)(2,1)} %param.10) | copy-start | bytes 98308
  36.3 133.9 %all-to-all-start = ((bf16[32,128,256]{2,1,0:T(8,128)(2,1)}), bf16[32,128,256]{2,1,0:T(8,128)(2,1)S(1)}, u32[]{:S(2)}, u32[]{:S(2)}) async-start(bf16[32,128,256]{2,1,0:T(8,128)(2,1)} %copy-done.3), calls=%async_computation | async-start | bytes 4194304 | tf_op jit(solution)/shard_map/all_to_all | solution.py:198
  42.5 168.5 %all-gather.5.cloned.1.call-start = ((), (), s32[]{:S(2)}) async-start(), calls=%async_computation.2 | async-start | bytes 2228224 | tf_op jit(solution)/shard_map/all_gather | solution.py:231
  213.3 1.3 copy-start
  214.6 10.3 %copy-start.8 = (f32[128]{0:T(128)S(1)}, f32[128]{0:T(128)}, u32[]{:S(2)}) copy-start(f32[128]{0:T(128)} %param.11) | copy-start | bytes 1540
  214.6 10.5 %copy-start.7 = (bf16[128,128]{1,0:T(8,128)(2,1)S(1)}, bf16[128,128]{1,0:T(8,128)(2,1)}, u32[]{:S(2)}) copy-start(bf16[128,128]{1,0:T(8,128)(2,1)} %param.9) | copy-start | bytes 98308
  214.6 60.7 %all-to-all-start.1 = ((bf16[32,128,256]{2,1,0:T(8,128)(2,1)}), bf16[32,128,256]{2,1,0:T(8,128)(2,1)S(1)}, u32[]{:S(2)}, u32[]{:S(2)}) async-start(bf16[32,128,256]{2,1,0:T(8,128)(2,1)} %copy-done), calls=%async_computation.1 | async-start | bytes 4194304 | tf_op jit(solution)/shard_map/all_to_all | solution.py:239
  225.4 1.6 copy-start.2
Sparse Core Ops, SparseCore 0:
  171.5 39.5 all-gather.4

commit v2 on v1

v2 whole, which is shorter than its diff:
```python
import functools

import jax
import jax.numpy as jnp
from jax import lax
from jax.experimental import pallas as pl
from jax.experimental.pallas import tpu as pltpu
from jax.sharding import PartitionSpec as P

HEAD_COUNT = 128
P_SIZE = 64
N = 128
G = 8
KERNEL = 4
GROUP_HEADS = HEAD_COUNT // G
GROUP_WIDTH = GROUP_HEADS * P_SIZE
WIDTH_X = HEAD_COUNT * P_SIZE
F32 = jnp.float32
BF16 = jnp.bfloat16
HALVES = 2


def lower_ones(rows):
    down = lax.broadcasted_iota(jnp.int32, (rows, rows), 0)
    across = lax.broadcasted_iota(jnp.int32, (rows, rows), 1)
    return down >= across


def dot(a, b, a_dim, b_dim):
    return lax.dot_general(a, b, (((a_dim,), (b_dim,)), ((), ())), preferred_element_type=F32)


def running_sum(decay):
    return dot(lower_ones(decay.shape[0]).astype(BF16), decay, 1, 0)


def group_columns(columns, group):
    heads = columns.shape[1]
    return pltpu.roll(columns, lax.rem(heads - group * GROUP_HEADS, heads), 1)[:, :GROUP_HEADS]


def over_heads(columns):
    rows = columns.shape[0]
    left = lax.broadcasted_iota(jnp.int32, (rows, 2 * P_SIZE), 1) < P_SIZE
    return jnp.concatenate(
        [
            jnp.where(left, columns[:, h : h + 1], columns[:, h + 1 : h + 2])
            for h in range(0, columns.shape[1], 2)
        ],
        axis=1,
    )


def conv_silu(columns, rim, weights, biases, pad):
    rows = columns.shape[0]
    width = columns.shape[1]
    pad[8 - (KERNEL - 1) : 8, 0:width] = rim.astype(F32)
    pad[8 : 8 + rows, 0:width] = columns.astype(F32)
    summed = biases
    for tap in range(KERNEL):
        first = 8 - (KERNEL - 1) + tap
        summed = summed + weights[tap : tap + 1, :] * pad[first : first + rows, 0:width]
    return (summed / (1.0 + jnp.exp(-summed))).astype(BF16)


def conv_states_kernel(
    first_group, x_in, b_in, c_in, x_rim, b_rim, c_rim, x_w, b_w, c_w, x_bias, b_bias, c_bias, step, decay,
    x_out, b_out, c_out, states, pad,
):
    values = conv_silu(x_in[...], x_rim[...], x_w[...], x_bias[...], pad)
    keys_b = conv_silu(b_in[...], b_rim[...], b_w[...], b_bias[...], pad)
    query_c = conv_silu(c_in[...], c_rim[...], c_w[...], c_bias[...], pad)
    x_out[...] = values
    b_out[...] = keys_b
    c_out[...] = query_c
    group = first_group + pl.program_id(0)
    rows = x_in.shape[0]
    running = group_columns(running_sum(decay[...]), group)
    steps = group_columns(step[...].astype(F32), group)
    weight = jnp.exp(running[rows - 1 : rows, :] - running) * steps
    weighted = (values.astype(F32) * over_heads(weight)).astype(BF16)
    targets, _, width = states.shape
    total = over_heads(running[rows - 1 : rows, :])
    high = total.astype(BF16).astype(F32)
    middle = (total - high).astype(BF16).astype(F32)
    row = lax.broadcasted_iota(jnp.int32, (8, total.shape[1]), 0)
    pieces = jnp.where(row == 0, high, jnp.where(row == 1, middle, total - high - middle))
    pieces = jnp.where(row < 3, pieces, 0.0).astype(BF16)
    for target in range(targets):
        at = slice(target * width, (target + 1) * width)
        states[target, 0:N, :] = dot(keys_b, weighted[:, at], 0, 0).astype(BF16)
        states[target, N : N + 8, :] = pieces[:, at]


def within_kernel(first_group, x_in, b_in, c_in, step, decay, skip, out, running_all, steps_all):
    scores = dot(c_in[...], b_in[...], 1, 1)
    causal = lower_ones(scores.shape[0])
    @pl.when(pl.program_id(0) == 0)
    def _():
        running_all[...] = dot(decay[...], causal.astype(BF16), 0, 1)
        steps_all[...] = step[...].astype(F32).T

    group = first_group + pl.program_id(0)
    running = group_columns(running_sum(decay[...]), group)
    heads = pl.ds(pl.multiple_of(group * GROUP_HEADS, GROUP_HEADS), GROUP_HEADS)
    running_t = running_all[heads, :]
    steps = steps_all[heads, :]
    scores = jnp.where(causal, scores, 0.0)
    for pair in range(GROUP_HEADS // 2):
        parts = []
        x_pair = x_in[:, pair * 2 * P_SIZE : (pair + 1) * 2 * P_SIZE]
        for h in (2 * pair, 2 * pair + 1):
            gap = jnp.where(causal, running[:, h : h + 1] - running_t[h : h + 1, :], -jnp.inf)
            mix = (scores * jnp.exp(gap) * steps[h : h + 1, :]).astype(BF16)
            parts.append(dot(mix, x_pair[:, (h % 2) * P_SIZE : (h % 2 + 1) * P_SIZE], 1, 0))
        at = slice(pair * 2 * P_SIZE, (pair + 1) * 2 * P_SIZE)
        out[:, at] = jnp.concatenate(parts, axis=1) + skip[:, at] * x_pair.astype(F32)


def chunk_decays(states):
    return jnp.sum(states[:, N : N + 8, :].astype(F32), axis=1)


def section_total_kernel(states, total):
    chunks = states.shape[0]
    decays = chunk_decays(states)
    gains = jnp.exp(decays)
    for part in range(N // 32):
        at = slice(part * 32, (part + 1) * 32)
        carried = states[0, at, :].astype(F32)
        for chunk in range(1, chunks):
            carried = gains[chunk : chunk + 1, :] * carried + states[chunk, at, :].astype(F32)
        total[at, :] = carried
    total[N : N + 8, :] = jnp.broadcast_to(
        jnp.sum(decays, axis=0, keepdims=True), (8, total.shape[1])
    )


def entering_kernel(states, carried_in, entering):
    chunks = states.shape[0]
    gains = jnp.exp(chunk_decays(states))
    for part in range(N // 32):
        at = slice(part * 32, (part + 1) * 32)
        carried = carried_in[at, :]
        for chunk in range(chunks):
            entering[chunk, at, :] = carried.astype(BF16)
            carried = gains[chunk : chunk + 1, :] * carried + states[chunk, at, :].astype(F32)


def outputs_kernel(first_group, within, c_in, decay, entering, *rest):
    out = rest[-1]
    group = first_group + pl.program_id(0)
    growth = over_heads(jnp.exp(group_columns(running_sum(decay[...]), group)))
    query_c = c_in[...]
    targets, _, width = entering.shape
    for target in range(targets):
        at = slice(target * width, (target + 1) * width)
        out[:, at] = (within[:, at] + growth[:, at] * dot(query_c, entering[target], 1, 0)).astype(
            BF16
        )


def join_kernel(got, before, through, before_out, through_out):
    for later, out in ((before, before_out), (through, through_out)):
        out[0:N, :] = jnp.exp(later[N : N + 1, :]) * got[0:N, :] + later[0:N, :]
        out[N : N + 8, :] = got[N : N + 8, :] + later[N : N + 8, :]


def before_section(total, params):
    sections = lax.axis_size("sec")
    join = pl.pallas_call(
        join_kernel,
        out_shape=[jax.ShapeDtypeStruct(total.shape, F32)] * 2,
        compiler_params=params,
        name="join",
    )
    through = total
    before = jnp.zeros_like(total)
    steps = 1
    while steps < sections:
        got = lax.ppermute(
            through, "sec", [(source, source + steps) for source in range(sections - steps)]
        )
        before, through = join(got, before, through)
        steps *= 2
    return before


def per_device(projected, conv_weight, conv_bias, step_size, log_decay, skip_gain):
    targets = lax.axis_size("cp")
    sections = lax.axis_size("sec")
    rows = projected.shape[0]
    width_all = projected.shape[1]
    devices = targets * sections
    groups = G // HALVES
    width_half = groups * GROUP_WIDTH
    width_here = width_half // targets
    group_targets = GROUP_WIDTH // width_here

    rim = lax.ppermute(
        projected[rows - (KERNEL - 1) :],
        ("sec", "cp"),
        [(source, source + 1) for source in range(devices - 1)],
    )
    bias = conv_bias.reshape(1, width_all)
    skip_wide = jnp.repeat(skip_gain, P_SIZE).reshape(1, WIDTH_X)
    params = pltpu.CompilerParams(vmem_limit_bytes=16 * 2**20)
    b_first = WIDTH_X // N
    c_first = b_first + G

    def columns_spec(height, width, first=0):
        return pl.BlockSpec((height, width), lambda g: (0, first + g))

    per_token = pl.BlockSpec((rows, HEAD_COUNT), lambda g: (0, 0))
    states_spec = pl.BlockSpec((group_targets, N + 8, width_here), lambda g: (g, 0, 0))
    entering_spec = pl.BlockSpec((group_targets, N, width_here), lambda g: (g, 0, 0))

    def conv_states(half):
        first = half * groups

        def three(height):
            return [
                columns_spec(height, GROUP_WIDTH, first),
                columns_spec(height, N, b_first + first),
                columns_spec(height, N, c_first + first),
            ]

        return pl.pallas_call(
            functools.partial(conv_states_kernel, first),
            grid=(groups,),
            in_specs=three(rows) + three(KERNEL - 1) + three(KERNEL) + three(1) + [per_token] * 2,
            out_specs=[
                columns_spec(rows, GROUP_WIDTH),
                columns_spec(rows, N),
                columns_spec(rows, N),
                states_spec,
            ],
            out_shape=[
                jax.ShapeDtypeStruct((rows, width_half), BF16),
                jax.ShapeDtypeStruct((rows, groups * N), BF16),
                jax.ShapeDtypeStruct((rows, groups * N), BF16),
                jax.ShapeDtypeStruct((targets, N + 8, width_here), BF16),
            ],
            scratch_shapes=[pltpu.VMEM((rows + 8, GROUP_WIDTH), F32)],
            compiler_params=params,
            name="conv_states",
        )(
            projected, projected, projected, rim, rim, rim, conv_weight, conv_weight, conv_weight,
            bias, bias, bias, step_size, log_decay,
        )

    def within_chunk(half, values, keys_b, query_c):
        first = half * groups
        return pl.pallas_call(
            functools.partial(within_kernel, first),
            grid=(groups,),
            in_specs=[
                columns_spec(rows, GROUP_WIDTH),
                columns_spec(rows, N),
                columns_spec(rows, N),
                per_token,
                per_token,
                columns_spec(1, GROUP_WIDTH, first),
            ],
            out_specs=columns_spec(rows, GROUP_WIDTH),
            out_shape=jax.ShapeDtypeStruct((rows, width_half), F32),
            scratch_shapes=[pltpu.VMEM((HEAD_COUNT, rows), F32)] * 2,
            compiler_params=params,
            name="within",
        )(values, keys_b, query_c, step_size, log_decay, skip_wide)

    def section_total(states):
        return pl.pallas_call(
            section_total_kernel,
            out_shape=jax.ShapeDtypeStruct((N + 8, width_here), F32),
            compiler_params=params,
            name="section_total",
        )(states)

    def entering_states(states, carried_in):
        return pl.pallas_call(
            entering_kernel,
            out_shape=jax.ShapeDtypeStruct((targets, N, width_here), BF16),
            compiler_params=params,
            name="entering",
        )(states, carried_in)

    def outputs(half, within, query_c, entering, so_far):
        first = half * groups
        carried = [] if so_far is None else [so_far]
        return pl.pallas_call(
            functools.partial(outputs_kernel, first),
            grid=(groups,),
            in_specs=[
                columns_spec(rows, GROUP_WIDTH),
                columns_spec(rows, N),
                per_token,
                entering_spec,
            ]
            + [pl.BlockSpec(memory_space=pl.ANY)] * len(carried),
            out_specs=columns_spec(rows, GROUP_WIDTH, first),
            out_shape=jax.ShapeDtypeStruct((rows, WIDTH_X), BF16),
            input_output_aliases={4: 0} if carried else {},
            compiler_params=params,
            name="outputs",
        )(within, query_c, log_decay, entering, *carried)

    def exchanged(value):
        return lax.all_to_all(value, "cp", split_axis=0, concat_axis=0, tiled=True)

    convs = [conv_states(half) for half in range(HALVES)]
    states = [exchanged(conv[3]) for conv in convs]
    withins = [within_chunk(half, *convs[half][:3]) for half in range(HALVES)]
    arrived = []
    leaving = None
    for half in range(HALVES):
        state = states[half]
        if half:
            state, leaving = lax.optimization_barrier((state, leaving))
            arrived.append(exchanged(leaving))
        leaving = entering_states(state, before_section(section_total(state), params))
    if arrived:
        arrived[-1], leaving = lax.optimization_barrier((arrived[-1], leaving))
    arrived.append(exchanged(leaving))
    result = None
    for half in range(HALVES):
        result = outputs(half, withins[half], convs[half][2], arrived[half], result)
    return result


def solution(mesh):
    in_specs = (
        P(("sec", "cp"), None),
        P(),
        P(),
        P(("sec", "cp"), None),
        P(("sec", "cp"), None),
        P(),
    )
    out_specs = P(("sec", "cp"), None)
    return jax.shard_map(
        per_device, mesh=mesh, in_specs=in_specs, out_specs=out_specs, check_vma=False
    )
```

time: 291 us -> 190 us (0.65)
  the two profiles are of different devices: /device:TPU:8 before, /device:TPU:96 now
where the time goes in v2:
time: 190 us; the launch traced here: 188 us
  waiting for transfers between devices  83 us (44%)
  starting transfers between devices  57.4 us (30%)
  Pallas kernels  31.9 us (17%)
  local copies, waits for them, and re-layouts  15.8 us (8%)
    ppermute x8, waiting for transfers between devices, before_section(): lax.ppermute(through, 'sec', [(source, source + steps) for source in rang...  50.9 us
    all_to_all x4, starting transfers between devices, exchanged(): return lax.all_to_all(value, 'cp', split_axis=0, concat_axis=0, tiled=True)  38.8 us
    all_to_all x4, waiting for transfers between devices, exchanged(): return lax.all_to_all(value, 'cp', split_axis=0, concat_axis=0, tiled=True)  30 us
    unnamed x48, local copies, waits for them, and re-layouts  14.6 us
    ppermute x8, starting transfers between devices, before_section(): lax.ppermute(through, 'sec', [(source, source + steps) for source in rang...  14.4 us
    pallas_call x2, Pallas kernels, conv_states(): pl.pallas_call(functools.partial(conv_states_kernel, first), grid=(groups...  9.81 us
    pallas_call x2, Pallas kernels, within_chunk(): pl.pallas_call(functools.partial(within_kernel, first), grid=(groups,), i...  9.17 us
    pallas_call x2, Pallas kernels, outputs(): pl.pallas_call(functools.partial(outputs_kernel, first), grid=(groups,),...  6.89 us
  transfers between devices with their start and end apart: 13, of which 11 were waited for; matrix products, arithmetic and copies ran while one was open for 0% of the time, Pallas kernels for 13%

profile of v2, /device:TPU:96, one launch (start us, length us, event | category | flops | bytes accessed | tf_op | source)
XLA Modules:
  0.0 188.4 jit_solution(9826041835502008962)
XLA Ops:
  1.0 4.3 %collective-permute-start = (bf16[3,10240]{1,0:T(4,128)(2,1)S(1)}, bf16[3,10240]{1,0:T(4,128)(2,1)S(1)}, u32[]{:S(2)}, u32[]{:S(2)}) collective-permute-start(bf16[3,10240]{1,0:T(4,128)(2,1)S(1)} %slice.3), channel_id=1, source_target_pairs={{0,1},{1,2},{2,3},{3,4},{4,5},{5,6},{6,7},{7,8},{8,9},{9,10},{10,1... | collective-permute-start | bytes 184328 | tf_op jit(solution)/shard_map/ppermute | solution.py:200
  5.3 2.0 %collective-permute-done.x_rim.b_rim.c_rim = bf16[3,10240]{1,0:T(4,128)(2,1)S(1)} collective-permute-done((bf16[3,10240]{1,0:T(4,128)(2,1)S(1)}, bf16[3,10240]{1,0:T(4,128)(2,1)S(1)}, u32[]{:S(2)}, u32[]{:S(2)}) %collective-permute-start) | collective-permute-done | bytes 61472 | tf_op jit(solution)/shard_map/ppermute | solution.py:200
  12.3 4.9 %conv_states.3 = (bf16[128,4096]{1,0:T(8,128)(2,1)S(1)}, bf16[128,512]{1,0:T(8,128)(2,1)S(1)}, bf16[128,512]{1,0:T(8,128)(2,1)S(1)}, bf16[32,136,128]{2,1,0:T(8,128)(2,1)S(1)}) custom-call(bf16[128,10240]{1,0:T(8,128)(2,1)S(1)} %copy-done, bf16[128,10240]{1,0:T(8,128)(2,1)S(1)} %copy-done, bf16[128,10240]{1,0:T(8,128)(2,1)S(1)} %copy-done, ...), custom_call_target="tpu_custom_call" | custom-call | tf_op jit(solution)/shard_map/conv_states/pallas_call | solution.py:228
  19.8 14.0 %all-to-all-start.1 = ((bf16[32,136,128]{2,1,0:T(8,128)(2,1)}), bf16[32,136,128]{2,1,0:T(8,128)(2,1)}, u32[]{:S(2)}, u32[]{:S(2)}) async-start(bf16[32,136,128]{2,1,0:T(8,128)(2,1)} %copy-done.12), calls=%async_computation.1 | async-start | bytes 2228224 | tf_op jit(solution)/shard_map/all_to_all | solution.py:309
  33.8 4.9 %conv_states.2 = (bf16[128,4096]{1,0:T(8,128)(2,1)S(1)}, bf16[128,512]{1,0:T(8,128)(2,1)S(1)}, bf16[128,512]{1,0:T(8,128)(2,1)S(1)}, bf16[32,136,128]{2,1,0:T(8,128)(2,1)S(1)}) custom-call(bf16[128,10240]{1,0:T(8,128)(2,1)S(1)} %copy-done.1, bf16[128,10240]{1,0:T(8,128)(2,1)S(1)} %copy-done.1, bf16[128,10240]{1,0:T(8,128)(2,1)S(1)} %copy-done.1, ...), custom_call_target="tpu_custom_call" | custom-call | tf_op jit(solution)/shard_map/conv_states/pallas_call | solution.py:228
  40.7 22.6 %all-to-all-done.1.states = bf16[32,136,128]{2,1,0:T(8,128)(2,1)} async-done(((bf16[32,136,128]{2,1,0:T(8,128)(2,1)}), bf16[32,136,128]{2,1,0:T(8,128)(2,1)}, u32[]{:S(2)}, u32[]{:S(2)}) %all-to-all-start.1) | async-done | bytes 1114144 | tf_op jit(solution)/shard_map/all_to_all | solution.py:309
  63.3 5.3 %all-to-all-start = ((bf16[32,136,128]{2,1,0:T(8,128)(2,1)}), bf16[32,136,128]{2,1,0:T(8,128)(2,1)S(1)}, u32[]{:S(2)}, u32[]{:S(2)}) async-start(bf16[32,136,128]{2,1,0:T(8,128)(2,1)} %copy-done.11), calls=%async_computation | async-start | bytes 2228224 | tf_op jit(solution)/shard_map/all_to_all | solution.py:309
  72.1 4.9 %collective-permute-done.1.got = f32[136,128]{1,0:T(8,128)S(1)} collective-permute-done((f32[136,128]{1,0:T(8,128)S(1)}, f32[136,128]{1,0:T(8,128)S(1)}, u32[]{:S(2)}, u32[]{:S(2)}) %collective-permute-start.1) | collective-permute-done | bytes 69664 | tf_op jit(solution)/shard_map/ppermute | solution.py:181
  77.0 2.2 %collective-permute-start.2 = (f32[136,128]{1,0:T(8,128)S(1)}, f32[136,128]{1,0:T(8,128)S(1)}, u32[]{:S(2)}, u32[]{:S(2)}) collective-permute-start(f32[136,128]{1,0:T(8,128)S(1)} %get-tuple-element.36.through), channel_id=1, source_target_pairs={{0,64},{32,96},{64,128},{96,160},{128,192},{160,224},{192,256},{22... | collective-permute-start | bytes 208904 | tf_op jit(solution)/shard_map/ppermute | solution.py:181
  79.2 5.2 %collective-permute-done.2.got = f32[136,128]{1,0:T(8,128)S(1)} collective-permute-done((f32[136,128]{1,0:T(8,128)S(1)}, f32[136,128]{1,0:T(8,128)S(1)}, u32[]{:S(2)}, u32[]{:S(2)}) %collective-permute-start.2) | collective-permute-done | bytes 69664 | tf_op jit(solution)/shard_map/ppermute | solution.py:181
  86.4 6.4 %collective-permute-done.3.got = f32[136,128]{1,0:T(8,128)S(1)} collective-permute-done((f32[136,128]{1,0:T(8,128)S(1)}, f32[136,128]{1,0:T(8,128)S(1)}, u32[]{:S(2)}, u32[]{:S(2)}) %collective-permute-start.3) | collective-permute-done | bytes 69664 | tf_op jit(solution)/shard_map/ppermute | solution.py:181
  94.1 8.8 %collective-permute-done.4.got = f32[136,128]{1,0:T(8,128)S(1)} collective-permute-done((f32[136,128]{1,0:T(8,128)S(1)}, f32[136,128]{1,0:T(8,128)S(1)}, u32[]{:S(2)}, u32[]{:S(2)}) %collective-permute-start.4) | collective-permute-done | bytes 69664 | tf_op jit(solution)/shard_map/ppermute | solution.py:181
  103.6 2.5 %entering.2 = bf16[32,128,128]{2,1,0:T(8,128)(2,1)} custom-call(bf16[32,136,128]{2,1,0:T(8,128)(2,1)} %all-to-all-done.1.states, f32[136,128]{1,0:T(8,128)S(1)} %get-tuple-element.42.carried_in), custom_call_target="tpu_custom_call" | custom-call | tf_op jit(solution)/shard_map/entering/pallas_call | solution.py:281
  106.1 9.8 %all-to-all-start.2 = ((bf16[32,128,128]{2,1,0:T(8,128)(2,1)}), bf16[32,128,128]{2,1,0:T(8,128)(2,1)S(1)}, u32[]{:S(2)}, u32[]{:S(2)}) async-start(bf16[32,128,128]{2,1,0:T(8,128)(2,1)} %entering.2), calls=%async_computation.2 | async-start | bytes 2097152 | tf_op jit(solution)/shard_map/all_to_all | solution.py:309
  118.1 4.9 %collective-permute-done.5.got = f32[136,128]{1,0:T(8,128)S(1)} collective-permute-done((f32[136,128]{1,0:T(8,128)S(1)}, f32[136,128]{1,0:T(8,128)S(1)}, u32[]{:S(2)}, u32[]{:S(2)}) %collective-permute-start.5) | collective-permute-done | bytes 69664 | tf_op jit(solution)/shard_map/ppermute | solution.py:181
  124.9 5.5 %collective-permute-done.6.got = f32[136,128]{1,0:T(8,128)S(1)} collective-permute-done((f32[136,128]{1,0:T(8,128)S(1)}, f32[136,128]{1,0:T(8,128)S(1)}, u32[]{:S(2)}, u32[]{:S(2)}) %collective-permute-start.6) | collective-permute-done | bytes 69664 | tf_op jit(solution)/shard_map/ppermute | solution.py:181
  132.4 6.4 %collective-permute-done.7.got = f32[136,128]{1,0:T(8,128)S(1)} collective-permute-done((f32[136,128]{1,0:T(8,128)S(1)}, f32[136,128]{1,0:T(8,128)S(1)}, u32[]{:S(2)}, u32[]{:S(2)}) %collective-permute-start.7) | collective-permute-done | bytes 69664 | tf_op jit(solution)/shard_map/ppermute | solution.py:181
  140.1 8.8 %collective-permute-done.8.got = f32[136,128]{1,0:T(8,128)S(1)} collective-permute-done((f32[136,128]{1,0:T(8,128)S(1)}, f32[136,128]{1,0:T(8,128)S(1)}, u32[]{:S(2)}, u32[]{:S(2)}) %collective-permute-start.8) | collective-permute-done | bytes 69664 | tf_op jit(solution)/shard_map/ppermute | solution.py:181
  151.8 9.8 %all-to-all-start.3 = ((bf16[32,128,128]{2,1,0:T(8,128)(2,1)}), bf16[32,128,128]{2,1,0:T(8,128)(2,1)S(1)}, u32[]{:S(2)}, u32[]{:S(2)}) async-start(bf16[32,128,128]{2,1,0:T(8,128)(2,1)} %copy-done.4), calls=%async_computation.3 | async-start | bytes 2097152 | tf_op jit(solution)/shard_map/all_to_all | solution.py:309
  162.7 4.6 %within.3 = f32[128,4096]{1,0:T(8,128)S(1)} custom-call(bf16[128,4096]{1,0:T(8,128)(2,1)S(1)} %copy-done.14, bf16[128,512]{1,0:T(8,128)(2,1)S(1)} %copy-done.20, bf16[128,512]{1,0:T(8,128)(2,1)S(1)} %get-tuple-element.55.c_in, bf16[128,128]{1,0:T(8,128)(2,1)S(1)} %copy-done.18, bf16[128,128]{1,0:T(8,128)(2,1)S(1)} %copy-done.10, ...), custom_call_target="tpu_custom_call" | custom-call | tf_op jit(solution)/shard_map/within/pallas_call | solution.py:254
  169.6 4.6 %within.2 = f32[128,4096]{1,0:T(8,128)S(1)} custom-call(bf16[128,4096]{1,0:T(8,128)(2,1)S(1)} %copy-done.16, bf16[128,512]{1,0:T(8,128)(2,1)S(1)} %copy-done.22, bf16[128,512]{1,0:T(8,128)(2,1)S(1)} %get-tuple-element.33.c_in, bf16[128,128]{1,0:T(8,128)(2,1)S(1)} %copy-done.18, bf16[128,128]{1,0:T(8,128)(2,1)S(1)} %copy-done.10, ...), custom_call_target="tpu_custom_call" | custom-call | tf_op jit(solution)/shard_map/within/pallas_call | solution.py:254
  174.2 3.4 %outputs.2.rest_0_ = bf16[128,8192]{1,0:T(8,128)(2,1)} custom-call(f32[128,4096]{1,0:T(8,128)S(1)} %within.3, bf16[128,512]{1,0:T(8,128)(2,1)S(1)} %get-tuple-element.55.c_in, bf16[128,128]{1,0:T(8,128)(2,1)S(1)} %copy-done.10, bf16[32,128,128]{2,1,0:T(8,128)(2,1)S(1)} %copy-done.6), custom_call_target="tpu_custom_call" | custom-call | tf_op jit(solution)/shard_map/outputs/pallas_call | solution.py:291
  177.6 7.4 %all-to-all-done.3.entering = bf16[32,128,128]{2,1,0:T(8,128)(2,1)S(1)} async-done(((bf16[32,128,128]{2,1,0:T(8,128)(2,1)}), bf16[32,128,128]{2,1,0:T(8,128)(2,1)S(1)}, u32[]{:S(2)}, u32[]{:S(2)}) %all-to-all-start.3) | async-done | bytes 1048608 | tf_op jit(solution)/shard_map/all_to_all | solution.py:309
  185.0 3.4 %outputs.3 = bf16[128,8192]{1,0:T(8,128)(2,1)} custom-call(f32[128,4096]{1,0:T(8,128)S(1)} %within.2, bf16[128,512]{1,0:T(8,128)(2,1)S(1)} %get-tuple-element.33.c_in, bf16[128,128]{1,0:T(8,128)(2,1)S(1)} %copy-done.10, bf16[32,128,128]{2,1,0:T(8,128)(2,1)S(1)} %all-to-all-done.3.entering, ...), custom_call_target="tpu_custom_call", output_to_operand_aliasing={{}: (4, {})} | custom-call | tf_op jit(solution)/shard_map/outputs/pallas_call | solution.py:291
  (72 shorter events, 31.5 us)
Async XLA Ops:
  1.0 6.3 %collective-permute-start = (bf16[3,10240]{1,0:T(4,128)(2,1)S(1)}, bf16[3,10240]{1,0:T(4,128)(2,1)S(1)}, u32[]{:S(2)}, u32[]{:S(2)}) collective-permute-start(bf16[3,10240]{1,0:T(4,128)(2,1)S(1)} %slice.3), channel_id=1, source_target_pairs={{0,1},{1,2},{2,3},{3,4},{4,5},{5,6},{6,7},{7,8},{8,9},{9,10},{10,1... | collective-permute-start | bytes 184328 | tf_op jit(solution)/shard_map/ppermute | solution.py:200
  7.3 1.7 copy-start
  12.3 21.5 %copy-start.1 = (bf16[128,10240]{1,0:T(8,128)(2,1)S(1)}, bf16[128,10240]{1,0:T(8,128)(2,1)}, u32[]{:S(2)}) copy-start(bf16[128,10240]{1,0:T(8,128)(2,1)} %c_in.3) | copy-start | bytes 7864324
  19.8 14.0 %copy-start.3 = (f32[4,10240]{1,0:T(4,128)S(1)}, f32[4,10240]{1,0:T(4,128)}, u32[]{:S(2)}) copy-start(f32[4,10240]{1,0:T(4,128)} %c_w.3) | copy-start | bytes 491524
  19.8 14.0 %copy-start.8 = (f32[10240]{0:T(1024)S(1)}, f32[10240]{0:T(1024)}, u32[]{:S(2)}) copy-start(f32[10240]{0:T(1024)} %param.8) | copy-start | bytes 122884
  19.8 14.0 %copy-start.10 = (bf16[128,128]{1,0:T(8,128)(2,1)S(1)}, bf16[128,128]{1,0:T(8,128)(2,1)}, u32[]{:S(2)}) copy-start(bf16[128,128]{1,0:T(8,128)(2,1)} %decay.11) | copy-start | bytes 98308
  19.8 14.0 %copy-start.18 = (bf16[128,128]{1,0:T(8,128)(2,1)S(1)}, bf16[128,128]{1,0:T(8,128)(2,1)}, u32[]{:S(2)}) copy-start(bf16[128,128]{1,0:T(8,128)(2,1)} %step.7) | copy-start | bytes 98308
  19.8 43.6 %all-to-all-start.1 = ((bf16[32,136,128]{2,1,0:T(8,128)(2,1)}), bf16[32,136,128]{2,1,0:T(8,128)(2,1)}, u32[]{:S(2)}, u32[]{:S(2)}) async-start(bf16[32,136,128]{2,1,0:T(8,128)(2,1)} %copy-done.12), calls=%async_computation.1 | async-start | bytes 2228224 | tf_op jit(solution)/shard_map/all_to_all | solution.py:309
  40.7 62.9 %copy-start.21 = (bf16[128,512]{1,0:T(8,128)(2,1)}, bf16[128,512]{1,0:T(8,128)(2,1)S(1)}, u32[]{:S(2)}) copy-start(bf16[128,512]{1,0:T(8,128)(2,1)S(1)} %get-tuple-element.32.b_in) | copy-start | bytes 393220
  63.3 42.7 %all-to-all-start = ((bf16[32,136,128]{2,1,0:T(8,128)(2,1)}), bf16[32,136,128]{2,1,0:T(8,128)(2,1)S(1)}, u32[]{:S(2)}, u32[]{:S(2)}) async-start(bf16[32,136,128]{2,1,0:T(8,128)(2,1)} %copy-done.11), calls=%async_computation | async-start | bytes 2228224 | tf_op jit(solution)/shard_map/all_to_all | solution.py:309
  70.1 6.8 %collective-permute-start.1 = (f32[136,128]{1,0:T(8,128)S(1)}, f32[136,128]{1,0:T(8,128)S(1)}, u32[]{:S(2)}, u32[]{:S(2)}) collective-permute-start(f32[136,128]{1,0:T(8,128)S(1)} %section_total.2.through), channel_id=1, source_target_pairs={{0,32},{32,64},{64,96},{96,128},{128,160},{160,192},{192,224},{224... | collective-permute-start | bytes 208904 | tf_op jit(solution)/shard_map/ppermute | solution.py:181
  77.0 7.4 %collective-permute-start.2 = (f32[136,128]{1,0:T(8,128)S(1)}, f32[136,128]{1,0:T(8,128)S(1)}, u32[]{:S(2)}, u32[]{:S(2)}) collective-permute-start(f32[136,128]{1,0:T(8,128)S(1)} %get-tuple-element.36.through), channel_id=1, source_target_pairs={{0,64},{32,96},{64,128},{96,160},{128,192},{160,224},{192,256},{22... | collective-permute-start | bytes 208904 | tf_op jit(solution)/shard_map/ppermute | solution.py:181
  84.5 8.3 %collective-permute-start.3 = (f32[136,128]{1,0:T(8,128)S(1)}, f32[136,128]{1,0:T(8,128)S(1)}, u32[]{:S(2)}, u32[]{:S(2)}) collective-permute-start(f32[136,128]{1,0:T(8,128)S(1)} %get-tuple-element.38.through), channel_id=1, source_target_pairs={{0,128},{32,160},{64,192},{96,224},{128,256},{160,288},{192,320},{... | collective-permute-start | bytes 208904 | tf_op jit(solution)/shard_map/ppermute | solution.py:181
  92.8 10.1 %collective-permute-start.4 = (f32[136,128]{1,0:T(8,128)S(1)}, f32[136,128]{1,0:T(8,128)S(1)}, u32[]{:S(2)}, u32[]{:S(2)}) collective-permute-start(f32[136,128]{1,0:T(8,128)S(1)} %get-tuple-element.40.through), channel_id=1, source_target_pairs={{0,256},{32,288},{64,320},{96,352},{128,384},{160,416},{192,448},{... | collective-permute-start | bytes 208904 | tf_op jit(solution)/shard_map/ppermute | solution.py:181
  106.1 44.8 %all-to-all-start.2 = ((bf16[32,128,128]{2,1,0:T(8,128)(2,1)}), bf16[32,128,128]{2,1,0:T(8,128)(2,1)S(1)}, u32[]{:S(2)}, u32[]{:S(2)}) async-start(bf16[32,128,128]{2,1,0:T(8,128)(2,1)} %entering.2), calls=%async_computation.2 | async-start | bytes 2097152 | tf_op jit(solution)/shard_map/all_to_all | solution.py:309
  116.2 6.8 %collective-permute-start.5 = (f32[136,128]{1,0:T(8,128)S(1)}, f32[136,128]{1,0:T(8,128)S(1)}, u32[]{:S(2)}, u32[]{:S(2)}) collective-permute-start(f32[136,128]{1,0:T(8,128)S(1)} %section_total.3.through), channel_id=1, source_target_pairs={{0,32},{32,64},{64,96},{96,128},{128,160},{160,192},{192,224},{224... | collective-permute-start | bytes 208904 | tf_op jit(solution)/shard_map/ppermute | solution.py:181
  123.0 7.4 %collective-permute-start.6 = (f32[136,128]{1,0:T(8,128)S(1)}, f32[136,128]{1,0:T(8,128)S(1)}, u32[]{:S(2)}, u32[]{:S(2)}) collective-permute-start(f32[136,128]{1,0:T(8,128)S(1)} %get-tuple-element.45.through), channel_id=1, source_target_pairs={{0,64},{32,96},{64,128},{96,160},{128,192},{160,224},{192,256},{22... | collective-permute-start | bytes 208904 | tf_op jit(solution)/shard_map/ppermute | solution.py:181
  130.5 8.3 %collective-permute-start.7 = (f32[136,128]{1,0:T(8,128)S(1)}, f32[136,128]{1,0:T(8,128)S(1)}, u32[]{:S(2)}, u32[]{:S(2)}) collective-permute-start(f32[136,128]{1,0:T(8,128)S(1)} %get-tuple-element.47.through), channel_id=1, source_target_pairs={{0,128},{32,160},{64,192},{96,224},{128,256},{160,288},{192,320},{... | collective-permute-start | bytes 208904 | tf_op jit(solution)/shard_map/ppermute | solution.py:181
  138.8 10.1 %collective-permute-start.8 = (f32[136,128]{1,0:T(8,128)S(1)}, f32[136,128]{1,0:T(8,128)S(1)}, u32[]{:S(2)}, u32[]{:S(2)}) collective-permute-start(f32[136,128]{1,0:T(8,128)S(1)} %get-tuple-element.49.through), channel_id=1, source_target_pairs={{0,256},{32,288},{64,320},{96,352},{128,384},{160,416},{192,448},{... | collective-permute-start | bytes 208904 | tf_op jit(solution)/shard_map/ppermute | solution.py:181
  149.6 12.1 %copy-start.23 = (f32[128]{0:T(128)S(1)}, f32[128]{0:T(128)}, u32[]{:S(2)}) copy-start(f32[128]{0:T(128)} %param.11) | copy-start | bytes 1540
  150.9 11.0 %copy-start.14 = (bf16[128,4096]{1,0:T(8,128)(2,1)S(1)}, bf16[128,4096]{1,0:T(8,128)(2,1)}, u32[]{:S(2)}) copy-start(bf16[128,4096]{1,0:T(8,128)(2,1)} %copy-done.13) | copy-start | bytes 3145732
  151.8 33.2 %all-to-all-start.3 = ((bf16[32,128,128]{2,1,0:T(8,128)(2,1)}), bf16[32,128,128]{2,1,0:T(8,128)(2,1)S(1)}, u32[]{:S(2)}, u32[]{:S(2)}) async-start(bf16[32,128,128]{2,1,0:T(8,128)(2,1)} %copy-done.4), calls=%async_computation.3 | async-start | bytes 2097152 | tf_op jit(solution)/shard_map/all_to_all | solution.py:309
  167.3 6.8 %copy-start.6 = (bf16[32,128,128]{2,1,0:T(8,128)(2,1)S(1)}, bf16[32,128,128]{2,1,0:T(8,128)(2,1)}, u32[]{:S(2)}) copy-start(bf16[32,128,128]{2,1,0:T(8,128)(2,1)} %copy-done.5) | copy-start | bytes 3145732
  167.3 1.3 copy-start.16
  (13 other events, 11.6 us)

commit v3 on v2

--- a/solution.py
+++ b/solution.py
@@ -18,6 +18,7 @@
 F32 = jnp.float32
 BF16 = jnp.bfloat16
 HALVES = 2
+RADIX = 4
 
 
 def lower_ones(rows):
@@ -61,6 +62,18 @@
         first = 8 - (KERNEL - 1) + tap
         summed = summed + weights[tap : tap + 1, :] * pad[first : first + rows, 0:width]
     return (summed / (1.0 + jnp.exp(-summed))).astype(BF16)
+
+
+def decay_rows(total):
+    high = total.astype(BF16).astype(F32)
+    middle = (total - high).astype(BF16).astype(F32)
+    row = lax.broadcasted_iota(jnp.int32, (8, total.shape[1]), 0)
+    pieces = jnp.where(row == 0, high, jnp.where(row == 1, middle, total - high - middle))
+    return jnp.where(row < 3, pieces, 0.0).astype(BF16)
+
+
+def decay_of(rows):
+    return jnp.sum(rows.astype(F32), axis=0, keepdims=True)
 
 
 def conv_states_kernel(
@@ -80,12 +93,7 @@
     weight = jnp.exp(running[rows - 1 : rows, :] - running) * steps
     weighted = (values.astype(F32) * over_heads(weight)).astype(BF16)
     targets, _, width = states.shape
-    total = over_heads(running[rows - 1 : rows, :])
-    high = total.astype(BF16).astype(F32)
-    middle = (total - high).astype(BF16).astype(F32)
-    row = lax.broadcasted_iota(jnp.int32, (8, total.shape[1]), 0)
-    pieces = jnp.where(row == 0, high, jnp.where(row == 1, middle, total - high - middle))
-    pieces = jnp.where(row < 3, pieces, 0.0).astype(BF16)
+    pieces = decay_rows(over_heads(running[rows - 1 : rows, :]))
     for target in range(targets):
         at = slice(target * width, (target + 1) * width)
         states[target, 0:N, :] = dot(keys_b, weighted[:, at], 0, 0).astype(BF16)
@@ -130,18 +138,37 @@
         carried = states[0, at, :].astype(F32)
         for chunk in range(1, chunks):
             carried = gains[chunk : chunk + 1, :] * carried + states[chunk, at, :].astype(F32)
-        total[at, :] = carried
-    total[N : N + 8, :] = jnp.broadcast_to(
-        jnp.sum(decays, axis=0, keepdims=True), (8, total.shape[1])
-    )
-
-
-def entering_kernel(states, carried_in, entering):
+        total[at, :] = carried.astype(BF16)
+    total[N : N + 8, :] = decay_rows(jnp.sum(decays, axis=0, keepdims=True))
+
+
+def chained(parts, at):
+    state = parts[-1][at, :].astype(F32)
+    for part in reversed(parts[:-1]):
+        gain = jnp.exp(decay_of(part[N : N + 8, :]))
+        state = part[at, :].astype(F32) + gain * state
+    return state
+
+
+def join_kernel(own, *parts):
+    *nearby, before, through = parts
+    decay_own = decay_of(own[N : N + 8, :])
+    decay_near = sum(decay_of(part[N : N + 8, :]) for part in nearby)
+    near = chained(nearby, slice(0, N))
+    before[0:N, :] = near
+    before[N : N + 8, :] = jnp.broadcast_to(decay_near, (8, near.shape[1]))
+    through[0:N, :] = (own[0:N, :].astype(F32) + jnp.exp(decay_own) * near).astype(BF16)
+    through[N : N + 8, :] = decay_rows(decay_own + decay_near)
+
+
+def entering_kernel(states, before, *parts):
+    *earlier, entering = parts
     chunks = states.shape[0]
     gains = jnp.exp(chunk_decays(states))
+    gain_near = jnp.exp(before[N : N + 1, :])
     for part in range(N // 32):
         at = slice(part * 32, (part + 1) * 32)
-        carried = carried_in[at, :]
+        carried = before[at, :] + gain_near * chained(earlier, at)
         for chunk in range(chunks):
             entering[chunk, at, :] = carried.astype(BF16)
             carried = gains[chunk : chunk + 1, :] * carried + states[chunk, at, :].astype(F32)
@@ -160,35 +187,32 @@
         )
 
 
-def join_kernel(got, before, through, before_out, through_out):
-    for later, out in ((before, before_out), (through, through_out)):
-        out[0:N, :] = jnp.exp(later[N : N + 1, :]) * got[0:N, :] + later[0:N, :]
-        out[N : N + 8, :] = got[N : N + 8, :] + later[N : N + 8, :]
+def from_earlier(value, step, count):
+    sections = lax.axis_size("sec")
+    return [
+        lax.ppermute(value, "sec", [(source, source + by) for source in range(sections - by)])
+        for by in range(step, step * count, step)
+        if by < sections
+    ]
 
 
 def before_section(total, params):
-    sections = lax.axis_size("sec")
-    join = pl.pallas_call(
+    before, through = pl.pallas_call(
         join_kernel,
-        out_shape=[jax.ShapeDtypeStruct(total.shape, F32)] * 2,
+        out_shape=[
+            jax.ShapeDtypeStruct(total.shape, F32),
+            jax.ShapeDtypeStruct(total.shape, BF16),
+        ],
         compiler_params=params,
         name="join",
-    )
-    through = total
-    before = jnp.zeros_like(total)
-    steps = 1
-    while steps < sections:
-        got = lax.ppermute(
-            through, "sec", [(source, source + steps) for source in range(sections - steps)]
-        )
-        before, through = join(got, before, through)
-        steps *= 2
-    return before
+    )(total, *from_earlier(total, 1, RADIX))
+    return before, *from_earlier(through, RADIX, RADIX)
 
 
 def per_device(projected, conv_weight, conv_bias, step_size, log_decay, skip_gain):
     targets = lax.axis_size("cp")
     sections = lax.axis_size("sec")
+    assert sections <= RADIX * RADIX
     rows = projected.shape[0]
     width_all = projected.shape[1]
     devices = targets * sections
@@ -236,10 +260,10 @@
                 states_spec,
             ],
             out_shape=[
-                jax.ShapeDtypeStruct((rows, width_half), BF16),
-                jax.ShapeDtypeStruct((rows, groups * N), BF16),
-                jax.ShapeDtypeStruct((rows, groups * N), BF16),
-                jax.ShapeDtypeStruct((targets, N + 8, width_here), BF16),
+                pltpu.HBM((rows, width_half), BF16),
+                pltpu.HBM((rows, groups * N), BF16),
+                pltpu.HBM((rows, groups * N), BF16),
+                pltpu.HBM((targets, N + 8, width_here), BF16),
             ],
             scratch_shapes=[pltpu.VMEM((rows + 8, GROUP_WIDTH), F32)],
             compiler_params=params,
@@ -263,7 +287,7 @@
                 columns_spec(1, GROUP_WIDTH, first),
             ],
             out_specs=columns_spec(rows, GROUP_WIDTH),
-            out_shape=jax.ShapeDtypeStruct((rows, width_half), F32),
+            out_shape=pltpu.HBM((rows, width_half), F32),
             scratch_shapes=[pltpu.VMEM((HEAD_COUNT, rows), F32)] * 2,
             compiler_params=params,
             name="within",
@@ -272,7 +296,7 @@
     def section_total(states):
         return pl.pallas_call(
             section_total_kernel,
-            out_shape=jax.ShapeDtypeStruct((N + 8, width_here), F32),
+            out_shape=jax.ShapeDtypeStruct((N + 8, width_here), BF16),
             compiler_params=params,
             name="section_total",
         )(states)
@@ -280,10 +304,10 @@
     def entering_states(states, carried_in):
         return pl.pallas_call(
             entering_kernel,
-            out_shape=jax.ShapeDtypeStruct((targets, N, width_here), BF16),
+            out_shape=pltpu.HBM((targets, N, width_here), BF16),
             compiler_params=params,
             name="entering",
-        )(states, carried_in)
+        )(states, *carried_in)
 
     def outputs(half, within, query_c, entering, so_far):
         first = half * groups
@@ -306,8 +330,13 @@
         )(within, query_c, log_decay, entering, *carried)
 
     def exchanged(value):
-        return lax.all_to_all(value, "cp", split_axis=0, concat_axis=0, tiled=True)
-
+        swapped = lax.all_to_all(value, "cp", split_axis=0, concat_axis=0, tiled=True)
+        return pltpu.with_memory_space_constraint(swapped, pltpu.HBM)
+
+    projected, conv_weight, bias, step_size, log_decay, skip_wide = (
+        pltpu.with_memory_space_constraint(value, pltpu.HBM)
+        for value in (projected, conv_weight, bias, step_size, log_decay, skip_wide)
+    )
     convs = [conv_states(half) for half in range(HALVES)]
     states = [exchanged(conv[3]) for conv in convs]
     withins = [within_chunk(half, *convs[half][:3]) for half in range(HALVES)]

time: 190 us -> 168 us (0.88)
  the two profiles are of different devices: /device:TPU:96 before, /device:TPU:16 now
where the time goes in v3:
time: 168 us; the launch traced here: 167 us
  starting transfers between devices  63.6 us (38%)
  waiting for transfers between devices  56.8 us (34%)
  Pallas kernels  43.2 us (26%)
  local copies, waits for them, and re-layouts  2.81 us (2%)
    all_to_all x4, waiting for transfers between devices, exchanged(): lax.all_to_all(value, 'cp', split_axis=0, concat_axis=0, tiled=True)  33.1 us
    ppermute x12, starting transfers between devices, from_earlier(): lax.ppermute(value, 'sec', [(source, source + by) for source in range(sec...  31.1 us
    all_to_all x4, starting transfers between devices, exchanged(): lax.all_to_all(value, 'cp', split_axis=0, concat_axis=0, tiled=True)  28.3 us
    ppermute x12, waiting for transfers between devices, from_earlier(): lax.ppermute(value, 'sec', [(source, source + by) for source in range(sec...  13.4 us
    pallas_call x2, Pallas kernels, conv_states(): pl.pallas_call(functools.partial(conv_states_kernel, first), grid=(groups...  12.9 us
    pallas_call x2, Pallas kernels, within_chunk(): pl.pallas_call(functools.partial(within_kernel, first), grid=(groups,), i...  12.3 us
    ppermute x1, waiting for transfers between devices, per_device(): lax.ppermute(projected[rows - (KERNEL - 1):], ('sec', 'cp'), [(source, so...  10.3 us
    pallas_call x2, Pallas kernels, outputs(): pl.pallas_call(functools.partial(outputs_kernel, first), grid=(groups,),...  9.6 us
  transfers between devices with their start and end apart: 17, of which 9 were waited for; matrix products, arithmetic and copies ran while one was open for 0% of the time, Pallas kernels for 19%

profile of v3, /device:TPU:16, one launch (start us, length us, event | category | flops | bytes accessed | tf_op | source)
XLA Modules:
  0.0 166.8 jit_solution(3529501464285691330)
XLA Ops:
  1.0 4.3 %collective-permute-start = (bf16[3,10240]{1,0:T(4,128)(2,1)S(1)}, bf16[3,10240]{1,0:T(4,128)(2,1)S(1)}, u32[]{:S(2)}, u32[]{:S(2)}) collective-permute-start(bf16[3,10240]{1,0:T(4,128)(2,1)S(1)} %slice.3), channel_id=1, source_target_pairs={{0,1},{1,2},{2,3},{3,4},{4,5},{5,6},{6,7},{7,8},{8,9},{9,10},{10,1... | collective-permute-start | bytes 184328 | tf_op jit(solution)/shard_map/ppermute | solution.py:224
  5.3 10.3 %collective-permute-done.x_rim.b_rim.c_rim = bf16[3,10240]{1,0:T(4,128)(2,1)S(1)} collective-permute-done((bf16[3,10240]{1,0:T(4,128)(2,1)S(1)}, bf16[3,10240]{1,0:T(4,128)(2,1)S(1)}, u32[]{:S(2)}, u32[]{:S(2)}) %collective-permute-start) | collective-permute-done | bytes 61472 | tf_op jit(solution)/shard_map/ppermute | solution.py:224
  15.6 6.5 %conv_states.3 = (bf16[128,4096]{1,0:T(8,128)(2,1)}, bf16[128,512]{1,0:T(8,128)(2,1)}, bf16[128,512]{1,0:T(8,128)(2,1)}, bf16[32,136,128]{2,1,0:T(8,128)(2,1)}) custom-call(bf16[128,10240]{1,0:T(8,128)(2,1)} %c_in.3, bf16[128,10240]{1,0:T(8,128)(2,1)} %c_in.3, bf16[128,10240]{1,0:T(8,128)(2,1)} %c_in.3, ...), custom_call_target="tpu_custom_call" | custom-call | tf_op jit(solution)/shard_map/conv_states/pallas_call | solution.py:252
  22.0 6.1 %all-to-all-start.1 = ((bf16[32,136,128]{2,1,0:T(8,128)(2,1)}), bf16[32,136,128]{2,1,0:T(8,128)(2,1)S(1)}, u32[]{:S(2)}, u32[]{:S(2)}) async-start(bf16[32,136,128]{2,1,0:T(8,128)(2,1)} %get-tuple-element.25), calls=%async_computation.1 | async-start | bytes 2228224 | tf_op jit(solution)/shard_map/all_to_all | solution.py:333
  28.1 6.5 %conv_states.2 = (bf16[128,4096]{1,0:T(8,128)(2,1)}, bf16[128,512]{1,0:T(8,128)(2,1)}, bf16[128,512]{1,0:T(8,128)(2,1)}, bf16[32,136,128]{2,1,0:T(8,128)(2,1)}) custom-call(bf16[128,10240]{1,0:T(8,128)(2,1)} %c_in.3, bf16[128,10240]{1,0:T(8,128)(2,1)} %c_in.3, bf16[128,10240]{1,0:T(8,128)(2,1)} %c_in.3, ...), custom_call_target="tpu_custom_call" | custom-call | tf_op jit(solution)/shard_map/conv_states/pallas_call | solution.py:252
  34.6 22.8 %all-to-all-done.1.states = bf16[32,136,128]{2,1,0:T(8,128)(2,1)S(1)} async-done(((bf16[32,136,128]{2,1,0:T(8,128)(2,1)}), bf16[32,136,128]{2,1,0:T(8,128)(2,1)S(1)}, u32[]{:S(2)}, u32[]{:S(2)}) %all-to-all-start.1) | async-done | bytes 1114144 | tf_op jit(solution)/shard_map/all_to_all | solution.py:333
  57.5 4.9 %all-to-all-start = ((bf16[32,136,128]{2,1,0:T(8,128)(2,1)}), bf16[32,136,128]{2,1,0:T(8,128)(2,1)S(1)}, u32[]{:S(2)}, u32[]{:S(2)}) async-start(bf16[32,136,128]{2,1,0:T(8,128)(2,1)} %get-tuple-element.24), calls=%async_computation | async-start | bytes 2228224 | tf_op jit(solution)/shard_map/all_to_all | solution.py:333
  66.0 4.7 %collective-permute-start.2 = (bf16[136,128]{1,0:T(8,128)(2,1)S(1)}, bf16[136,128]{1,0:T(8,128)(2,1)S(1)}, u32[]{:S(2)}, u32[]{:S(2)}) collective-permute-start(bf16[136,128]{1,0:T(8,128)(2,1)S(1)} %section_total.2.own), channel_id=1, source_target_pairs={{0,64},{32,96},{64,128},{96,160},{128,192},{160,224},{192,256},{22... | collective-permute-start | bytes 104456 | tf_op jit(solution)/shard_map/ppermute | solution.py:193
  70.7 4.1 %collective-permute-start.1 = (bf16[136,128]{1,0:T(8,128)(2,1)S(1)}, bf16[136,128]{1,0:T(8,128)(2,1)S(1)}, u32[]{:S(2)}, u32[]{:S(2)}) collective-permute-start(bf16[136,128]{1,0:T(8,128)(2,1)S(1)} %section_total.2.own), channel_id=1, source_target_pairs={{0,32},{32,64},{64,96},{96,128},{128,160},{160,192},{192,224},{224... | collective-permute-start | bytes 104456 | tf_op jit(solution)/shard_map/ppermute | solution.py:193
  77.2 4.0 %collective-permute-start.5 = (bf16[136,128]{1,0:T(8,128)(2,1)S(1)}, bf16[136,128]{1,0:T(8,128)(2,1)S(1)}, u32[]{:S(2)}, u32[]{:S(2)}) collective-permute-start(bf16[136,128]{1,0:T(8,128)(2,1)S(1)} %get-tuple-element.27), channel_id=1, source_target_pairs={{0,256},{32,288},{64,320},{96,352},{128,384},{160,416},{192,448},{... | collective-permute-start | bytes 104456 | tf_op jit(solution)/shard_map/ppermute | solution.py:193
  83.4 4.5 %collective-permute-done.4.parts_0_ = bf16[136,128]{1,0:T(8,128)(2,1)S(1)} collective-permute-done((bf16[136,128]{1,0:T(8,128)(2,1)S(1)}, bf16[136,128]{1,0:T(8,128)(2,1)S(1)}, u32[]{:S(2)}, u32[]{:S(2)}) %collective-permute-start.4) | collective-permute-done | bytes 34848 | tf_op jit(solution)/shard_map/ppermute | solution.py:193
  87.9 2.6 %entering.2 = bf16[32,128,128]{2,1,0:T(8,128)(2,1)} custom-call(bf16[32,136,128]{2,1,0:T(8,128)(2,1)} %copy-done.9, f32[136,128]{1,0:T(8,128)S(1)} %get-tuple-element.26.before, bf16[136,128]{1,0:T(8,128)(2,1)S(1)} %collective-permute-done.4.parts_0_, bf16[136,128]{1,0:T(8,128)(2,1)S(1)} %collective-permute-done.5.parts_1_, ...), custom_call_target="tpu_custom_call" | custom-call | tf_op jit(solution)/shard_map/entering/pallas_call | solution.py:305
  92.0 8.3 %all-to-all-start.2 = ((bf16[32,128,128]{2,1,0:T(8,128)(2,1)}), bf16[32,128,128]{2,1,0:T(8,128)(2,1)S(1)}, u32[]{:S(2)}, u32[]{:S(2)}) async-start(bf16[32,128,128]{2,1,0:T(8,128)(2,1)} %entering.2), calls=%async_computation.2 | async-start | bytes 2097152 | tf_op jit(solution)/shard_map/all_to_all | solution.py:333
  105.7 4.2 %collective-permute-start.7 = (bf16[136,128]{1,0:T(8,128)(2,1)S(1)}, bf16[136,128]{1,0:T(8,128)(2,1)S(1)}, u32[]{:S(2)}, u32[]{:S(2)}) collective-permute-start(bf16[136,128]{1,0:T(8,128)(2,1)S(1)} %section_total.3.own), channel_id=1, source_target_pairs={{0,32},{32,64},{64,96},{96,128},{128,160},{160,192},{192,224},{224... | collective-permute-start | bytes 104456 | tf_op jit(solution)/shard_map/ppermute | solution.py:193
  109.9 2.9 %collective-permute-done.7.parts_0_ = bf16[136,128]{1,0:T(8,128)(2,1)S(1)} collective-permute-done((bf16[136,128]{1,0:T(8,128)(2,1)S(1)}, bf16[136,128]{1,0:T(8,128)(2,1)S(1)}, u32[]{:S(2)}, u32[]{:S(2)}) %collective-permute-start.7) | collective-permute-done | bytes 34848 | tf_op jit(solution)/shard_map/ppermute | solution.py:193
  115.8 2.4 %collective-permute-start.10 = (bf16[136,128]{1,0:T(8,128)(2,1)S(1)}, bf16[136,128]{1,0:T(8,128)(2,1)S(1)}, u32[]{:S(2)}, u32[]{:S(2)}) collective-permute-start(bf16[136,128]{1,0:T(8,128)(2,1)S(1)} %get-tuple-element.31), channel_id=1, source_target_pairs={{0,128},{32,160},{64,192},{96,224},{128,256},{160,288},{192,320},{... | collective-permute-start | bytes 104456 | tf_op jit(solution)/shard_map/ppermute | solution.py:193
  118.3 4.3 %collective-permute-done.10.parts_0_ = bf16[136,128]{1,0:T(8,128)(2,1)S(1)} collective-permute-done((bf16[136,128]{1,0:T(8,128)(2,1)S(1)}, bf16[136,128]{1,0:T(8,128)(2,1)S(1)}, u32[]{:S(2)}, u32[]{:S(2)}) %collective-permute-start.10) | collective-permute-done | bytes 34848 | tf_op jit(solution)/shard_map/ppermute | solution.py:193
  122.6 2.7 %entering.3 = bf16[32,128,128]{2,1,0:T(8,128)(2,1)} custom-call(bf16[32,136,128]{2,1,0:T(8,128)(2,1)} %copy-done.8, f32[136,128]{1,0:T(8,128)S(1)} %get-tuple-element.30.before, bf16[136,128]{1,0:T(8,128)(2,1)S(1)} %collective-permute-done.10.parts_0_, bf16[136,128]{1,0:T(8,128)(2,1)S(1)} %collective-permute-done.11.parts_1_, ...), custom_call_target="tpu_custom_call" | custom-call | tf_op jit(solution)/shard_map/entering/pallas_call | solution.py:305
  127.2 9.0 %all-to-all-start.3 = ((bf16[32,128,128]{2,1,0:T(8,128)(2,1)}), bf16[32,128,128]{2,1,0:T(8,128)(2,1)}, u32[]{:S(2)}, u32[]{:S(2)}) async-start(bf16[32,128,128]{2,1,0:T(8,128)(2,1)} %entering.3), calls=%async_computation.3 | async-start | bytes 2097152 | tf_op jit(solution)/shard_map/all_to_all | solution.py:333
  137.0 6.1 %within.3 = f32[128,4096]{1,0:T(8,128)} custom-call(bf16[128,4096]{1,0:T(8,128)(2,1)S(1)} %copy-done.2, bf16[128,512]{1,0:T(8,128)(2,1)S(1)} %copy-done.6, bf16[128,512]{1,0:T(8,128)(2,1)S(1)} %copy-done.5, bf16[128,128]{1,0:T(8,128)(2,1)} %step.7, bf16[128,128]{1,0:T(8,128)(2,1)} %decay.11, f32[1,8192]{1,0:T(1,128)} %reshape_reshape.3.skip), custom_call_target="tpu_custom_call" | custom-call | tf_op jit(solution)/shard_map/within/pallas_call | solution.py:278
  143.1 6.3 %within.2 = f32[128,4096]{1,0:T(8,128)} custom-call(bf16[128,4096]{1,0:T(8,128)(2,1)S(1)} %copy-done.3, bf16[128,512]{1,0:T(8,128)(2,1)S(1)} %copy-done.7, bf16[128,512]{1,0:T(8,128)(2,1)S(1)} %copy-done.4, bf16[128,128]{1,0:T(8,128)(2,1)} %step.7, bf16[128,128]{1,0:T(8,128)(2,1)} %decay.11, f32[1,8192]{1,0:T(1,128)} %reshape_reshape.3.skip), custom_call_target="tpu_custom_call" | custom-call | tf_op jit(solution)/shard_map/within/pallas_call | solution.py:278
  149.4 4.9 %outputs.2.rest_0_ = bf16[128,8192]{1,0:T(8,128)(2,1)} custom-call(f32[128,4096]{1,0:T(8,128)S(1)} %copy-done.1, bf16[128,512]{1,0:T(8,128)(2,1)S(1)} %copy-done.5, bf16[128,128]{1,0:T(8,128)(2,1)} %decay.11, bf16[32,128,128]{2,1,0:T(8,128)(2,1)} %copy-done.10), custom_call_target="tpu_custom_call" | custom-call | tf_op jit(solution)/shard_map/outputs/pallas_call | solution.py:315
  154.2 7.8 %all-to-all-done.3.entering = bf16[32,128,128]{2,1,0:T(8,128)(2,1)} async-done(((bf16[32,128,128]{2,1,0:T(8,128)(2,1)}), bf16[32,128,128]{2,1,0:T(8,128)(2,1)}, u32[]{:S(2)}, u32[]{:S(2)}) %all-to-all-start.3) | async-done | bytes 1048608 | tf_op jit(solution)/shard_map/all_to_all | solution.py:333
  162.0 4.7 %outputs.3 = bf16[128,8192]{1,0:T(8,128)(2,1)} custom-call(f32[128,4096]{1,0:T(8,128)S(1)} %copy-done, bf16[128,512]{1,0:T(8,128)(2,1)S(1)} %copy-done.4, bf16[128,128]{1,0:T(8,128)(2,1)} %decay.11, bf16[32,128,128]{2,1,0:T(8,128)(2,1)} %all-to-all-done.3.entering, bf16[128,8192]{1,0:T(8,128)(2,1)} %outputs.2.rest_0_), custom_call_target="tpu_custom_call", output_to_operand_aliasing={{}: (4, {})} | custom-call | tf_op jit(solution)/shard_map/outputs/pallas_call | solution.py:315
  (49 shorter events, 21.8 us)
Async XLA Ops:
  1.0 14.6 %collective-permute-start = (bf16[3,10240]{1,0:T(4,128)(2,1)S(1)}, bf16[3,10240]{1,0:T(4,128)(2,1)S(1)}, u32[]{:S(2)}, u32[]{:S(2)}) collective-permute-start(bf16[3,10240]{1,0:T(4,128)(2,1)S(1)} %slice.3), channel_id=1, source_target_pairs={{0,1},{1,2},{2,3},{3,4},{4,5},{5,6},{6,7},{7,8},{8,9},{9,10},{10,1... | collective-permute-start | bytes 184328 | tf_op jit(solution)/shard_map/ppermute | solution.py:224
  22.0 35.4 %all-to-all-start.1 = ((bf16[32,136,128]{2,1,0:T(8,128)(2,1)}), bf16[32,136,128]{2,1,0:T(8,128)(2,1)S(1)}, u32[]{:S(2)}, u32[]{:S(2)}) async-start(bf16[32,136,128]{2,1,0:T(8,128)(2,1)} %get-tuple-element.25), calls=%async_computation.1 | async-start | bytes 2228224 | tf_op jit(solution)/shard_map/all_to_all | solution.py:333
  57.5 34.5 %all-to-all-start = ((bf16[32,136,128]{2,1,0:T(8,128)(2,1)}), bf16[32,136,128]{2,1,0:T(8,128)(2,1)S(1)}, u32[]{:S(2)}, u32[]{:S(2)}) async-start(bf16[32,136,128]{2,1,0:T(8,128)(2,1)} %get-tuple-element.24), calls=%async_computation | async-start | bytes 2228224 | tf_op jit(solution)/shard_map/all_to_all | solution.py:333
  63.9 10.9 %collective-permute-start.3 = (bf16[136,128]{1,0:T(8,128)(2,1)S(1)}, bf16[136,128]{1,0:T(8,128)(2,1)S(1)}, u32[]{:S(2)}, u32[]{:S(2)}) collective-permute-start(bf16[136,128]{1,0:T(8,128)(2,1)S(1)} %section_total.2.own), channel_id=1, source_target_pairs={{0,96},{32,128},{64,160},{96,192},{128,224},{160,256},{192,288},{2... | collective-permute-start | bytes 104456 | tf_op jit(solution)/shard_map/ppermute | solution.py:193
  66.0 8.8 %collective-permute-start.2 = (bf16[136,128]{1,0:T(8,128)(2,1)S(1)}, bf16[136,128]{1,0:T(8,128)(2,1)S(1)}, u32[]{:S(2)}, u32[]{:S(2)}) collective-permute-start(bf16[136,128]{1,0:T(8,128)(2,1)S(1)} %section_total.2.own), channel_id=1, source_target_pairs={{0,64},{32,96},{64,128},{96,160},{128,192},{160,224},{192,256},{22... | collective-permute-start | bytes 104456 | tf_op jit(solution)/shard_map/ppermute | solution.py:193
  70.7 5.8 %collective-permute-start.1 = (bf16[136,128]{1,0:T(8,128)(2,1)S(1)}, bf16[136,128]{1,0:T(8,128)(2,1)S(1)}, u32[]{:S(2)}, u32[]{:S(2)}) collective-permute-start(bf16[136,128]{1,0:T(8,128)(2,1)S(1)} %section_total.2.own), channel_id=1, source_target_pairs={{0,32},{32,64},{64,96},{96,128},{128,160},{160,192},{192,224},{224... | collective-permute-start | bytes 104456 | tf_op jit(solution)/shard_map/ppermute | solution.py:193
  76.6 6.9 %collective-permute-start.6 = (bf16[136,128]{1,0:T(8,128)(2,1)S(1)}, bf16[136,128]{1,0:T(8,128)(2,1)S(1)}, u32[]{:S(2)}, u32[]{:S(2)}) collective-permute-start(bf16[136,128]{1,0:T(8,128)(2,1)S(1)} %get-tuple-element.27), channel_id=1, source_target_pairs={{0,384},{32,416},{64,448},{96,480},{1,385},{33,417},{65,449},{97,4... | collective-permute-start | bytes 104456 | tf_op jit(solution)/shard_map/ppermute | solution.py:193
  77.2 6.2 %collective-permute-start.5 = (bf16[136,128]{1,0:T(8,128)(2,1)S(1)}, bf16[136,128]{1,0:T(8,128)(2,1)S(1)}, u32[]{:S(2)}, u32[]{:S(2)}) collective-permute-start(bf16[136,128]{1,0:T(8,128)(2,1)S(1)} %get-tuple-element.27), channel_id=1, source_target_pairs={{0,256},{32,288},{64,320},{96,352},{128,384},{160,416},{192,448},{... | collective-permute-start | bytes 104456 | tf_op jit(solution)/shard_map/ppermute | solution.py:193
  81.2 6.7 %collective-permute-start.4 = (bf16[136,128]{1,0:T(8,128)(2,1)S(1)}, bf16[136,128]{1,0:T(8,128)(2,1)S(1)}, u32[]{:S(2)}, u32[]{:S(2)}) collective-permute-start(bf16[136,128]{1,0:T(8,128)(2,1)S(1)} %get-tuple-element.27), channel_id=1, source_target_pairs={{0,128},{32,160},{64,192},{96,224},{128,256},{160,288},{192,320},{... | collective-permute-start | bytes 104456 | tf_op jit(solution)/shard_map/ppermute | solution.py:193
  92.0 8.4 %copy-start.8 = (bf16[32,136,128]{2,1,0:T(8,128)(2,1)}, bf16[32,136,128]{2,1,0:T(8,128)(2,1)S(1)}, u32[]{:S(2)}) copy-start(bf16[32,136,128]{2,1,0:T(8,128)(2,1)S(1)} %all-to-all-done.states) | copy-start | bytes 3342340
  92.0 34.2 %all-to-all-start.2 = ((bf16[32,128,128]{2,1,0:T(8,128)(2,1)}), bf16[32,128,128]{2,1,0:T(8,128)(2,1)S(1)}, u32[]{:S(2)}, u32[]{:S(2)}) async-start(bf16[32,128,128]{2,1,0:T(8,128)(2,1)} %entering.2), calls=%async_computation.2 | async-start | bytes 2097152 | tf_op jit(solution)/shard_map/all_to_all | solution.py:333
  101.8 8.0 %collective-permute-start.9 = (bf16[136,128]{1,0:T(8,128)(2,1)S(1)}, bf16[136,128]{1,0:T(8,128)(2,1)S(1)}, u32[]{:S(2)}, u32[]{:S(2)}) collective-permute-start(bf16[136,128]{1,0:T(8,128)(2,1)S(1)} %section_total.3.own), channel_id=1, source_target_pairs={{0,96},{32,128},{64,160},{96,192},{128,224},{160,256},{192,288},{2... | collective-permute-start | bytes 104456 | tf_op jit(solution)/shard_map/ppermute | solution.py:193
  103.8 6.1 %collective-permute-start.8 = (bf16[136,128]{1,0:T(8,128)(2,1)S(1)}, bf16[136,128]{1,0:T(8,128)(2,1)S(1)}, u32[]{:S(2)}, u32[]{:S(2)}) collective-permute-start(bf16[136,128]{1,0:T(8,128)(2,1)S(1)} %section_total.3.own), channel_id=1, source_target_pairs={{0,64},{32,96},{64,128},{96,160},{128,192},{160,224},{192,256},{22... | collective-permute-start | bytes 104456 | tf_op jit(solution)/shard_map/ppermute | solution.py:193
  105.7 7.1 %collective-permute-start.7 = (bf16[136,128]{1,0:T(8,128)(2,1)S(1)}, bf16[136,128]{1,0:T(8,128)(2,1)S(1)}, u32[]{:S(2)}, u32[]{:S(2)}) collective-permute-start(bf16[136,128]{1,0:T(8,128)(2,1)S(1)} %section_total.3.own), channel_id=1, source_target_pairs={{0,32},{32,64},{64,96},{96,128},{128,160},{160,192},{192,224},{224... | collective-permute-start | bytes 104456 | tf_op jit(solution)/shard_map/ppermute | solution.py:193
  112.9 5.4 %collective-permute-start.12 = (bf16[136,128]{1,0:T(8,128)(2,1)S(1)}, bf16[136,128]{1,0:T(8,128)(2,1)S(1)}, u32[]{:S(2)}, u32[]{:S(2)}) collective-permute-start(bf16[136,128]{1,0:T(8,128)(2,1)S(1)} %get-tuple-element.31), channel_id=1, source_target_pairs={{0,384},{32,416},{64,448},{96,480},{1,385},{33,417},{65,449},{97,4... | collective-permute-start | bytes 104456 | tf_op jit(solution)/shard_map/ppermute | solution.py:193
  113.5 4.7 %collective-permute-start.11 = (bf16[136,128]{1,0:T(8,128)(2,1)S(1)}, bf16[136,128]{1,0:T(8,128)(2,1)S(1)}, u32[]{:S(2)}, u32[]{:S(2)}) collective-permute-start(bf16[136,128]{1,0:T(8,128)(2,1)S(1)} %get-tuple-element.31), channel_id=1, source_target_pairs={{0,256},{32,288},{64,320},{96,352},{128,384},{160,416},{192,448},{... | collective-permute-start | bytes 104456 | tf_op jit(solution)/shard_map/ppermute | solution.py:193
  115.8 6.7 %collective-permute-start.10 = (bf16[136,128]{1,0:T(8,128)(2,1)S(1)}, bf16[136,128]{1,0:T(8,128)(2,1)S(1)}, u32[]{:S(2)}, u32[]{:S(2)}) collective-permute-start(bf16[136,128]{1,0:T(8,128)(2,1)S(1)} %get-tuple-element.31), channel_id=1, source_target_pairs={{0,128},{32,160},{64,192},{96,224},{128,256},{160,288},{192,320},{... | collective-permute-start | bytes 104456 | tf_op jit(solution)/shard_map/ppermute | solution.py:193
  122.5 13.6 %copy-start.11 = (f32[128]{0:T(128)S(1)}, f32[128]{0:T(128)}, u32[]{:S(2)}) copy-start(f32[128]{0:T(128)} %param.11) | copy-start | bytes 1540
  122.6 14.5 %copy-start.2 = (bf16[128,4096]{1,0:T(8,128)(2,1)S(1)}, bf16[128,4096]{1,0:T(8,128)(2,1)}, u32[]{:S(2)}) copy-start(bf16[128,4096]{1,0:T(8,128)(2,1)} %get-tuple-element.33.x_in) | copy-start | bytes 3145732
  122.6 14.5 %copy-start.5 = (bf16[128,512]{1,0:T(8,128)(2,1)S(1)}, bf16[128,512]{1,0:T(8,128)(2,1)}, u32[]{:S(2)}) copy-start(bf16[128,512]{1,0:T(8,128)(2,1)} %get-tuple-element.35.c_in) | copy-start | bytes 393220
  122.6 14.5 %copy-start.6 = (bf16[128,512]{1,0:T(8,128)(2,1)S(1)}, bf16[128,512]{1,0:T(8,128)(2,1)}, u32[]{:S(2)}) copy-start(bf16[128,512]{1,0:T(8,128)(2,1)} %get-tuple-element.34.b_in) | copy-start | bytes 393220
  127.2 34.8 %all-to-all-start.3 = ((bf16[32,128,128]{2,1,0:T(8,128)(2,1)}), bf16[32,128,128]{2,1,0:T(8,128)(2,1)}, u32[]{:S(2)}, u32[]{:S(2)}) async-start(bf16[32,128,128]{2,1,0:T(8,128)(2,1)} %entering.3), calls=%async_computation.3 | async-start | bytes 2097152 | tf_op jit(solution)/shard_map/all_to_all | solution.py:333
  136.2 6.9 %copy-start.3 = (bf16[128,4096]{1,0:T(8,128)(2,1)S(1)}, bf16[128,4096]{1,0:T(8,128)(2,1)}, u32[]{:S(2)}) copy-start(bf16[128,4096]{1,0:T(8,128)(2,1)} %get-tuple-element.21.x_in) | copy-start | bytes 3145732
  149.4 12.7 %copy-start = (f32[128,4096]{1,0:T(8,128)S(1)}, f32[128,4096]{1,0:T(8,128)}, u32[]{:S(2)}) copy-start(f32[128,4096]{1,0:T(8,128)} %within.2) | copy-start | bytes 6291460
  (5 other events, 25.9 us)

commit v4 on v3

--- a/solution.py
+++ b/solution.py
@@ -19,6 +19,8 @@
 BF16 = jnp.bfloat16
 HALVES = 2
 RADIX = 4
+CONV_GROUPS = 4
+OUTPUT_GROUPS = 4
 
 
 def lower_ones(rows):
@@ -40,36 +42,49 @@
     return pltpu.roll(columns, lax.rem(heads - group * GROUP_HEADS, heads), 1)[:, :GROUP_HEADS]
 
 
-def over_heads(columns):
-    rows = columns.shape[0]
-    left = lax.broadcasted_iota(jnp.int32, (rows, 2 * P_SIZE), 1) < P_SIZE
-    return jnp.concatenate(
-        [
-            jnp.where(left, columns[:, h : h + 1], columns[:, h + 1 : h + 2])
-            for h in range(0, columns.shape[1], 2)
-        ],
-        axis=1,
-    )
-
-
-def conv_silu(columns, rim, weights, biases, pad):
-    rows = columns.shape[0]
-    width = columns.shape[1]
-    pad[8 - (KERNEL - 1) : 8, 0:width] = rim.astype(F32)
-    pad[8 : 8 + rows, 0:width] = columns.astype(F32)
-    summed = biases
-    for tap in range(KERNEL):
-        first = 8 - (KERNEL - 1) + tap
-        summed = summed + weights[tap : tap + 1, :] * pad[first : first + rows, 0:width]
+def three_parts(value):
+    high = value.astype(BF16).astype(F32)
+    middle = (value - high).astype(BF16).astype(F32)
+    return high, middle, value - high - middle
+
+
+def spread_matrix():
+    row = lax.broadcasted_iota(jnp.int32, (HEAD_COUNT, GROUP_WIDTH), 0)
+    lane = lax.broadcasted_iota(jnp.int32, (HEAD_COUNT, GROUP_WIDTH), 1)
+    head = lax.rem(row, GROUP_HEADS)
+    return ((lane // P_SIZE == head) & (row < 3 * GROUP_HEADS)).astype(BF16)
+
+
+def over_heads(parts, group, spread):
+    rows = parts[0].shape[0]
+    lane = lax.broadcasted_iota(jnp.int32, (rows, HEAD_COUNT), 1)
+    picked = jnp.zeros((rows, HEAD_COUNT), F32)
+    for place, part in enumerate(parts):
+        by = lax.rem(HEAD_COUNT + (place - group) * GROUP_HEADS, HEAD_COUNT)
+        moved = pltpu.roll(part, by, 1)
+        inside = (lane >= place * GROUP_HEADS) & (lane < (place + 1) * GROUP_HEADS)
+        picked = jnp.where(inside, moved, picked)
+    return dot(picked.astype(BF16), spread, 1, 0)
+
+
+def conv_silu(columns, rim, weights, biases):
+    rows, width = columns.shape
+    shape = (8 - (KERNEL - 1), width)
+    extended = jnp.concatenate([jnp.zeros(shape, F32), rim.astype(F32), columns.astype(F32)], axis=0)
+    before = pltpu.roll(extended, 1, 0)
+    earlier = pltpu.roll(weights[1:2, :] * extended + weights[0:1, :] * before, 2, 0)
+    summed = biases + (weights[3:4, :] * extended + weights[2:3, :] * before) + earlier
+    summed = summed[8:, :]
     return (summed / (1.0 + jnp.exp(-summed))).astype(BF16)
 
 
-def decay_rows(total):
-    high = total.astype(BF16).astype(F32)
-    middle = (total - high).astype(BF16).astype(F32)
-    row = lax.broadcasted_iota(jnp.int32, (8, total.shape[1]), 0)
-    pieces = jnp.where(row == 0, high, jnp.where(row == 1, middle, total - high - middle))
-    return jnp.where(row < 3, pieces, 0.0).astype(BF16)
+def decay_rows(*totals):
+    row = lax.broadcasted_iota(jnp.int32, (8, totals[0].shape[1]), 0)
+    value = jnp.zeros(row.shape, F32)
+    for which, total in enumerate(totals):
+        for place, part in enumerate(three_parts(total)):
+            value = jnp.where(row == 3 * which + place, part, value)
+    return value.astype(BF16)
 
 
 def decay_of(rows):
@@ -78,26 +93,47 @@
 
 def conv_states_kernel(
     first_group, x_in, b_in, c_in, x_rim, b_rim, c_rim, x_w, b_w, c_w, x_bias, b_bias, c_bias, step, decay,
-    x_out, b_out, c_out, states, pad,
+    x_out, b_out, c_out, states, spread,
 ):
-    values = conv_silu(x_in[...], x_rim[...], x_w[...], x_bias[...], pad)
-    keys_b = conv_silu(b_in[...], b_rim[...], b_w[...], b_bias[...], pad)
-    query_c = conv_silu(c_in[...], c_rim[...], c_w[...], c_bias[...], pad)
-    x_out[...] = values
-    b_out[...] = keys_b
-    c_out[...] = query_c
-    group = first_group + pl.program_id(0)
     rows = x_in.shape[0]
-    running = group_columns(running_sum(decay[...]), group)
-    steps = group_columns(step[...].astype(F32), group)
-    weight = jnp.exp(running[rows - 1 : rows, :] - running) * steps
-    weighted = (values.astype(F32) * over_heads(weight)).astype(BF16)
-    targets, _, width = states.shape
-    pieces = decay_rows(over_heads(running[rows - 1 : rows, :]))
-    for target in range(targets):
-        at = slice(target * width, (target + 1) * width)
-        states[target, 0:N, :] = dot(keys_b, weighted[:, at], 0, 0).astype(BF16)
-        states[target, N : N + 8, :] = pieces[:, at]
+    groups = x_in.shape[1] // GROUP_WIDTH
+    targets, height, width = states.shape
+    running_all = running_sum(decay[...])
+    weight_parts = three_parts(
+        jnp.exp(running_all[rows - 1 : rows, :] - running_all) * step[...].astype(F32)
+    )
+    last_parts = three_parts(running_all[rows - 8 : rows, :])
+
+    @pl.when(pl.program_id(0) == 0)
+    def _():
+        spread[...] = spread_matrix()
+
+    for local in range(groups):
+        group = first_group + pl.program_id(0) * groups + local
+        wide = slice(local * GROUP_WIDTH, (local + 1) * GROUP_WIDTH)
+        narrow = slice(local * N, (local + 1) * N)
+        values = conv_silu(x_in[:, wide], x_rim[:, wide], x_w[:, wide], x_bias[:, wide])
+        keys_b = conv_silu(b_in[:, narrow], b_rim[:, narrow], b_w[:, narrow], b_bias[:, narrow])
+        query_c = conv_silu(c_in[:, narrow], c_rim[:, narrow], c_w[:, narrow], c_bias[:, narrow])
+        x_out[:, wide] = values
+        b_out[:, narrow] = keys_b
+        c_out[:, narrow] = query_c
+        weighted = (values.astype(F32) * over_heads(weight_parts, group, spread[...])).astype(BF16)
+        summed = dot(keys_b, weighted, 0, 0).astype(BF16)
+        here = range(targets // groups)
+        for at in here:
+            lanes = slice(at * width, (at + 1) * width)
+            states[local * len(here) + at, 0:N, :] = summed[:, lanes]
+        if height > N:
+            pieces = decay_rows(
+                *(
+                    over_heads(last_parts, group + half * (G // HALVES), spread[...])[7:8, :]
+                    for half in range(HALVES)
+                )
+            )
+            for at in here:
+                lanes = slice(at * width, (at + 1) * width)
+                states[local * len(here) + at, N:height, :] = pieces[:, lanes]
 
 
 def within_kernel(first_group, x_in, b_in, c_in, step, decay, skip, out, running_all, steps_all):
@@ -125,21 +161,21 @@
         out[:, at] = jnp.concatenate(parts, axis=1) + skip[:, at] * x_pair.astype(F32)
 
 
-def chunk_decays(states):
-    return jnp.sum(states[:, N : N + 8, :].astype(F32), axis=1)
-
-
-def section_total_kernel(states, total):
+def chunk_decays(decays, half):
+    return jnp.sum(decays[:, 3 * half : 3 * half + 3, :].astype(F32), axis=1)
+
+
+def section_total_kernel(half, states, decays, total):
     chunks = states.shape[0]
-    decays = chunk_decays(states)
-    gains = jnp.exp(decays)
+    sums = chunk_decays(decays, half)
+    gains = jnp.exp(sums)
     for part in range(N // 32):
         at = slice(part * 32, (part + 1) * 32)
         carried = states[0, at, :].astype(F32)
         for chunk in range(1, chunks):
             carried = gains[chunk : chunk + 1, :] * carried + states[chunk, at, :].astype(F32)
         total[at, :] = carried.astype(BF16)
-    total[N : N + 8, :] = decay_rows(jnp.sum(decays, axis=0, keepdims=True))
+    total[N : N + 8, :] = decay_rows(jnp.sum(sums, axis=0, keepdims=True))
 
 
 def chained(parts, at):
@@ -161,10 +197,10 @@
     through[N : N + 8, :] = decay_rows(decay_own + decay_near)
 
 
-def entering_kernel(states, before, *parts):
+def entering_kernel(half, states, decays, before, *parts):
     *earlier, entering = parts
     chunks = states.shape[0]
-    gains = jnp.exp(chunk_decays(states))
+    gains = jnp.exp(chunk_decays(decays, half))
     gain_near = jnp.exp(before[N : N + 1, :])
     for part in range(N // 32):
         at = slice(part * 32, (part + 1) * 32)
@@ -175,16 +211,24 @@
 
 
 def outputs_kernel(first_group, within, c_in, decay, entering, *rest):
-    out = rest[-1]
-    group = first_group + pl.program_id(0)
-    growth = over_heads(jnp.exp(group_columns(running_sum(decay[...]), group)))
-    query_c = c_in[...]
+    out, spread = rest[-2:]
+    groups = out.shape[1] // GROUP_WIDTH
     targets, _, width = entering.shape
-    for target in range(targets):
-        at = slice(target * width, (target + 1) * width)
-        out[:, at] = (within[:, at] + growth[:, at] * dot(query_c, entering[target], 1, 0)).astype(
-            BF16
-        )
+    growth_parts = three_parts(jnp.exp(running_sum(decay[...])))
+
+    @pl.when(pl.program_id(0) == 0)
+    def _():
+        spread[...] = spread_matrix()
+
+    for local in range(groups):
+        group = first_group + pl.program_id(0) * groups + local
+        growth = over_heads(growth_parts, group, spread[...])
+        query_c = c_in[:, local * N : (local + 1) * N]
+        for at in range(targets // groups):
+            lanes = slice(at * width, (at + 1) * width)
+            wide = slice(local * GROUP_WIDTH + at * width, local * GROUP_WIDTH + (at + 1) * width)
+            carried = dot(query_c, entering[local * (targets // groups) + at], 1, 0)
+            out[:, wide] = (within[:, wide] + growth[:, lanes] * carried).astype(BF16)
 
 
 def from_earlier(value, step, count):
@@ -236,36 +280,39 @@
         return pl.BlockSpec((height, width), lambda g: (0, first + g))
 
     per_token = pl.BlockSpec((rows, HEAD_COUNT), lambda g: (0, 0))
-    states_spec = pl.BlockSpec((group_targets, N + 8, width_here), lambda g: (g, 0, 0))
-    entering_spec = pl.BlockSpec((group_targets, N, width_here), lambda g: (g, 0, 0))
-
     def conv_states(half):
-        first = half * groups
+        at_once = CONV_GROUPS
+        first = half * groups // at_once
+        wide = at_once * GROUP_WIDTH
+        narrow = at_once * N
+        state_rows = N if half else N + 8
 
         def three(height):
             return [
-                columns_spec(height, GROUP_WIDTH, first),
-                columns_spec(height, N, b_first + first),
-                columns_spec(height, N, c_first + first),
+                columns_spec(height, wide, first),
+                columns_spec(height, narrow, b_first // at_once + first),
+                columns_spec(height, narrow, c_first // at_once + first),
             ]
 
         return pl.pallas_call(
-            functools.partial(conv_states_kernel, first),
-            grid=(groups,),
+            functools.partial(conv_states_kernel, half * groups),
+            grid=(groups // at_once,),
             in_specs=three(rows) + three(KERNEL - 1) + three(KERNEL) + three(1) + [per_token] * 2,
             out_specs=[
-                columns_spec(rows, GROUP_WIDTH),
-                columns_spec(rows, N),
-                columns_spec(rows, N),
-                states_spec,
+                columns_spec(rows, wide),
+                columns_spec(rows, narrow),
+                columns_spec(rows, narrow),
+                pl.BlockSpec(
+                    (at_once * group_targets, state_rows, width_here), lambda g: (g, 0, 0)
+                ),
             ],
             out_shape=[
                 pltpu.HBM((rows, width_half), BF16),
                 pltpu.HBM((rows, groups * N), BF16),
                 pltpu.HBM((rows, groups * N), BF16),
-                pltpu.HBM((targets, N + 8, width_here), BF16),
+                pltpu.HBM((targets, state_rows, width_here), BF16),
             ],
-            scratch_shapes=[pltpu.VMEM((rows + 8, GROUP_WIDTH), F32)],
+            scratch_shapes=[pltpu.VMEM((HEAD_COUNT, GROUP_WIDTH), BF16)],
             compiler_params=params,
             name="conv_states",
         )(
@@ -293,45 +340,58 @@
             name="within",
         )(values, keys_b, query_c, step_size, log_decay, skip_wide)
 
-    def section_total(states):
+    arrived_specs = [
+        pl.BlockSpec((targets, N, width_here), lambda g: (0, 0, 0)),
+        pl.BlockSpec((targets, 8, width_here), lambda g: (0, N // 8, 0)),
+    ]
+    total_spec = pl.BlockSpec((N + 8, width_here), lambda g: (0, 0))
+
+    def section_total(half, states, first_states):
         return pl.pallas_call(
-            section_total_kernel,
+            functools.partial(section_total_kernel, half),
+            grid=(1,),
+            in_specs=arrived_specs,
+            out_specs=total_spec,
             out_shape=jax.ShapeDtypeStruct((N + 8, width_here), BF16),
             compiler_params=params,
             name="section_total",
-        )(states)
-
-    def entering_states(states, carried_in):
+        )(states, first_states)
+
+    def entering_states(half, states, first_states, carried_in):
         return pl.pallas_call(
-            entering_kernel,
+            functools.partial(entering_kernel, half),
+            grid=(1,),
+            in_specs=arrived_specs + [total_spec] * len(carried_in),
+            out_specs=pl.BlockSpec((targets, N, width_here), lambda g: (0, 0, 0)),
             out_shape=pltpu.HBM((targets, N, width_here), BF16),
             compiler_params=params,
             name="entering",
-        )(states, *carried_in)
+        )(states, first_states, *carried_in)
 
     def outputs(half, within, query_c, entering, so_far):
-        first = half * groups
+        at_once = OUTPUT_GROUPS
+        wide = at_once * GROUP_WIDTH
         carried = [] if so_far is None else [so_far]
         return pl.pallas_call(
-            functools.partial(outputs_kernel, first),
-            grid=(groups,),
+            functools.partial(outputs_kernel, half * groups),
+            grid=(groups // at_once,),
             in_specs=[
-                columns_spec(rows, GROUP_WIDTH),
-                columns_spec(rows, N),
+                columns_spec(rows, wide),
+                columns_spec(rows, at_once * N),
                 per_token,
-                entering_spec,
+                pl.BlockSpec((at_once * group_targets, N, width_here), lambda g: (g, 0, 0)),
             ]
             + [pl.BlockSpec(memory_space=pl.ANY)] * len(carried),
-            out_specs=columns_spec(rows, GROUP_WIDTH, first),
+            out_specs=columns_spec(rows, wide, half * groups // at_once),
             out_shape=jax.ShapeDtypeStruct((rows, WIDTH_X), BF16),
             input_output_aliases={4: 0} if carried else {},
+            scratch_shapes=[pltpu.VMEM((HEAD_COUNT, GROUP_WIDTH), BF16)],
             compiler_params=params,
             name="outputs",
         )(within, query_c, log_decay, entering, *carried)
 
     def exchanged(value):
-        swapped = lax.all_to_all(value, "cp", split_axis=0, concat_axis=0, tiled=True)
-        return pltpu.with_memory_space_constraint(swapped, pltpu.HBM)
+        return lax.all_to_all(value, "cp", split_axis=0, concat_axis=0, tiled=True)
 
     projected, conv_weight, bias, step_size, log_decay, skip_wide = (
         pltpu.with_memory_space_constraint(value, pltpu.HBM)
@@ -347,7 +407,8 @@
         if half:
             state, leaving = lax.optimization_barrier((state, leaving))
             arrived.append(exchanged(leaving))
-        leaving = entering_states(state, before_section(section_total(state), params))
+        total = section_total(half, state, states[0])
+        leaving = entering_states(half, state, states[0], before_section(total, params))
     if arrived:
         arrived[-1], leaving = lax.optimization_barrier((arrived[-1], leaving))
     arrived.append(exchanged(leaving))

time: 168 us -> 168 us (level)
  the two profiles are of different devices: /device:TPU:16 before, /device:TPU:48 now
where the time goes in v4:
time: 168 us; the launch traced here: 167 us
  waiting for transfers between devices  79.2 us (47%)
  starting transfers between devices  51.5 us (31%)
  Pallas kernels  31.6 us (19%)
  local copies, waits for them, and re-layouts  4.22 us (3%)
    all_to_all x4, waiting for transfers between devices, exchanged(): return lax.all_to_all(value, 'cp', split_axis=0, concat_axis=0, tiled=True)  38.8 us
    ppermute x12, waiting for transfers between devices, from_earlier(): lax.ppermute(value, 'sec', [(source, source + by) for source in range(sec...  29.1 us
    all_to_all x4, starting transfers between devices, exchanged(): return lax.all_to_all(value, 'cp', split_axis=0, concat_axis=0, tiled=True)  27.2 us
    ppermute x12, starting transfers between devices, from_earlier(): lax.ppermute(value, 'sec', [(source, source + by) for source in range(sec...  20.1 us
    pallas_call x2, Pallas kernels, within_chunk(): pl.pallas_call(functools.partial(within_kernel, first), grid=(groups,), i...  12.3 us
    ppermute x1, waiting for transfers between devices, per_device(): lax.ppermute(projected[rows - (KERNEL - 1):], ('sec', 'cp'), [(source, so...  11.3 us
    pallas_call x2, Pallas kernels, conv_states(): pl.pallas_call(functools.partial(conv_states_kernel, half * groups), grid...  10.4 us
    pallas_call x2, Pallas kernels, outputs(): pl.pallas_call(functools.partial(outputs_kernel, half * groups), grid=(gr...  5.45 us
  transfers between devices with their start and end apart: 17, of which 15 were waited for; matrix products, arithmetic and copies ran while one was open for 1% of the time, Pallas kernels for 14%

profile of v4, /device:TPU:48, one launch (start us, length us, event | category | flops | bytes accessed | tf_op | source)
XLA Modules:
  0.0 166.8 jit_solution(7235523449979226643)
XLA Ops:
  1.0 4.3 %collective-permute-start = (bf16[3,10240]{1,0:T(4,128)(2,1)S(1)}, bf16[3,10240]{1,0:T(4,128)(2,1)S(1)}, u32[]{:S(2)}, u32[]{:S(2)}) collective-permute-start(bf16[3,10240]{1,0:T(4,128)(2,1)S(1)} %slice.3), channel_id=1, source_target_pairs={{0,1},{1,2},{2,3},{3,4},{4,5},{5,6},{6,7},{7,8},{8,9},{9,10},{10,1... | collective-permute-start | bytes 184328 | tf_op jit(solution)/shard_map/ppermute | solution.py:268
  5.3 11.3 %collective-permute-done.x_rim.b_rim.c_rim = bf16[3,10240]{1,0:T(4,128)(2,1)S(1)} collective-permute-done((bf16[3,10240]{1,0:T(4,128)(2,1)S(1)}, bf16[3,10240]{1,0:T(4,128)(2,1)S(1)}, u32[]{:S(2)}, u32[]{:S(2)}) %collective-permute-start) | collective-permute-done | bytes 61472 | tf_op jit(solution)/shard_map/ppermute | solution.py:268
  16.5 5.2 %conv_states.3 = (bf16[128,4096]{1,0:T(8,128)(2,1)}, bf16[128,512]{1,0:T(8,128)(2,1)}, bf16[128,512]{1,0:T(8,128)(2,1)}, bf16[32,136,128]{2,1,0:T(8,128)(2,1)}) custom-call(bf16[128,10240]{1,0:T(8,128)(2,1)} %c_in.3, bf16[128,10240]{1,0:T(8,128)(2,1)} %c_in.3, bf16[128,10240]{1,0:T(8,128)(2,1)} %c_in.3, ...), custom_call_target="tpu_custom_call" | custom-call | tf_op jit(solution)/shard_map/conv_states/pallas_call | solution.py:297
  21.8 5.1 %all-to-all-start.1 = ((bf16[32,136,128]{2,1,0:T(8,128)(2,1)}), bf16[32,136,128]{2,1,0:T(8,128)(2,1)S(1)}, u32[]{:S(2)}, u32[]{:S(2)}) async-start(bf16[32,136,128]{2,1,0:T(8,128)(2,1)} %get-tuple-element.25), calls=%async_computation.1 | async-start | bytes 2228224 | tf_op jit(solution)/shard_map/all_to_all | solution.py:394
  26.9 5.2 %conv_states.2 = (bf16[128,4096]{1,0:T(8,128)(2,1)}, bf16[128,512]{1,0:T(8,128)(2,1)}, bf16[128,512]{1,0:T(8,128)(2,1)}, bf16[32,128,128]{2,1,0:T(8,128)(2,1)}) custom-call(bf16[128,10240]{1,0:T(8,128)(2,1)} %c_in.3, bf16[128,10240]{1,0:T(8,128)(2,1)} %c_in.3, bf16[128,10240]{1,0:T(8,128)(2,1)} %c_in.3, ...), custom_call_target="tpu_custom_call" | custom-call | tf_op jit(solution)/shard_map/conv_states/pallas_call | solution.py:297
  32.1 24.8 %all-to-all-done.1.states.decays = bf16[32,136,128]{2,1,0:T(8,128)(2,1)S(1)} async-done(((bf16[32,136,128]{2,1,0:T(8,128)(2,1)}), bf16[32,136,128]{2,1,0:T(8,128)(2,1)S(1)}, u32[]{:S(2)}, u32[]{:S(2)}) %all-to-all-start.1) | async-done | bytes 1114144 | tf_op jit(solution)/shard_map/all_to_all | solution.py:394
  56.8 5.1 %all-to-all-start = ((bf16[32,128,128]{2,1,0:T(8,128)(2,1)}), bf16[32,128,128]{2,1,0:T(8,128)(2,1)S(1)}, u32[]{:S(2)}, u32[]{:S(2)}) async-start(bf16[32,128,128]{2,1,0:T(8,128)(2,1)} %get-tuple-element.24), calls=%async_computation | async-start | bytes 2097152 | tf_op jit(solution)/shard_map/all_to_all | solution.py:394
  64.2 2.6 %collective-permute-start.2 = (bf16[136,128]{1,0:T(8,128)(2,1)S(1)}, bf16[136,128]{1,0:T(8,128)(2,1)S(1)}, u32[]{:S(2)}, u32[]{:S(2)}) collective-permute-start(bf16[136,128]{1,0:T(8,128)(2,1)S(1)} %section_total.2.own), channel_id=1, source_target_pairs={{0,64},{32,96},{64,128},{96,160},{128,192},{160,224},{192,256},{22... | collective-permute-start | bytes 104456 | tf_op jit(solution)/shard_map/ppermute | solution.py:237
  70.2 2.7 %collective-permute-done.3.parts_2_ = bf16[136,128]{1,0:T(8,128)(2,1)S(1)} collective-permute-done((bf16[136,128]{1,0:T(8,128)(2,1)S(1)}, bf16[136,128]{1,0:T(8,128)(2,1)S(1)}, u32[]{:S(2)}, u32[]{:S(2)}) %collective-permute-start.3) | collective-permute-done | bytes 34848 | tf_op jit(solution)/shard_map/ppermute | solution.py:237
  76.9 4.1 %collective-permute-done.4.parts_0_ = bf16[136,128]{1,0:T(8,128)(2,1)S(1)} collective-permute-done((bf16[136,128]{1,0:T(8,128)(2,1)S(1)}, bf16[136,128]{1,0:T(8,128)(2,1)S(1)}, u32[]{:S(2)}, u32[]{:S(2)}) %collective-permute-start.4) | collective-permute-done | bytes 34848 | tf_op jit(solution)/shard_map/ppermute | solution.py:237
  81.0 4.5 %collective-permute-done.5.parts_1_ = bf16[136,128]{1,0:T(8,128)(2,1)S(1)} collective-permute-done((bf16[136,128]{1,0:T(8,128)(2,1)S(1)}, bf16[136,128]{1,0:T(8,128)(2,1)S(1)}, u32[]{:S(2)}, u32[]{:S(2)}) %collective-permute-start.5) | collective-permute-done | bytes 34848 | tf_op jit(solution)/shard_map/ppermute | solution.py:237
  85.5 1.9 %collective-permute-done.6.parts_2_ = bf16[136,128]{1,0:T(8,128)(2,1)S(1)} collective-permute-done((bf16[136,128]{1,0:T(8,128)(2,1)S(1)}, bf16[136,128]{1,0:T(8,128)(2,1)S(1)}, u32[]{:S(2)}, u32[]{:S(2)}) %collective-permute-start.6) | collective-permute-done | bytes 34848 | tf_op jit(solution)/shard_map/ppermute | solution.py:237
  90.2 8.4 %all-to-all-start.2 = ((bf16[32,128,128]{2,1,0:T(8,128)(2,1)}), bf16[32,128,128]{2,1,0:T(8,128)(2,1)S(1)}, u32[]{:S(2)}, u32[]{:S(2)}) async-start(bf16[32,128,128]{2,1,0:T(8,128)(2,1)} %entering.2), calls=%async_computation.2 | async-start | bytes 2097152 | tf_op jit(solution)/shard_map/all_to_all | solution.py:394
  100.9 2.1 %collective-permute-start.8 = (bf16[136,128]{1,0:T(8,128)(2,1)S(1)}, bf16[136,128]{1,0:T(8,128)(2,1)S(1)}, u32[]{:S(2)}, u32[]{:S(2)}) collective-permute-start(bf16[136,128]{1,0:T(8,128)(2,1)S(1)} %section_total.3.own), channel_id=1, source_target_pairs={{0,64},{32,96},{64,128},{96,160},{128,192},{160,224},{192,256},{22... | collective-permute-start | bytes 104456 | tf_op jit(solution)/shard_map/ppermute | solution.py:237
  106.7 2.5 %collective-permute-done.9.parts_2_ = bf16[136,128]{1,0:T(8,128)(2,1)S(1)} collective-permute-done((bf16[136,128]{1,0:T(8,128)(2,1)S(1)}, bf16[136,128]{1,0:T(8,128)(2,1)S(1)}, u32[]{:S(2)}, u32[]{:S(2)}) %collective-permute-start.9) | collective-permute-done | bytes 34848 | tf_op jit(solution)/shard_map/ppermute | solution.py:237
  113.2 3.2 %collective-permute-done.10.parts_0_ = bf16[136,128]{1,0:T(8,128)(2,1)S(1)} collective-permute-done((bf16[136,128]{1,0:T(8,128)(2,1)S(1)}, bf16[136,128]{1,0:T(8,128)(2,1)S(1)}, u32[]{:S(2)}, u32[]{:S(2)}) %collective-permute-start.10) | collective-permute-done | bytes 34848 | tf_op jit(solution)/shard_map/ppermute | solution.py:237
  116.4 4.0 %collective-permute-done.11.parts_1_ = bf16[136,128]{1,0:T(8,128)(2,1)S(1)} collective-permute-done((bf16[136,128]{1,0:T(8,128)(2,1)S(1)}, bf16[136,128]{1,0:T(8,128)(2,1)S(1)}, u32[]{:S(2)}, u32[]{:S(2)}) %collective-permute-start.11) | collective-permute-done | bytes 34848 | tf_op jit(solution)/shard_map/ppermute | solution.py:237
  120.4 2.8 %collective-permute-done.12.parts_2_ = bf16[136,128]{1,0:T(8,128)(2,1)S(1)} collective-permute-done((bf16[136,128]{1,0:T(8,128)(2,1)S(1)}, bf16[136,128]{1,0:T(8,128)(2,1)S(1)}, u32[]{:S(2)}, u32[]{:S(2)}) %collective-permute-start.12) | collective-permute-done | bytes 34848 | tf_op jit(solution)/shard_map/ppermute | solution.py:237
  126.9 8.6 %all-to-all-start.3 = ((bf16[32,128,128]{2,1,0:T(8,128)(2,1)}), bf16[32,128,128]{2,1,0:T(8,128)(2,1)S(1)}, u32[]{:S(2)}, u32[]{:S(2)}) async-start(bf16[32,128,128]{2,1,0:T(8,128)(2,1)} %entering.3), calls=%async_computation.3 | async-start | bytes 2097152 | tf_op jit(solution)/shard_map/all_to_all | solution.py:394
  137.8 6.1 %within.3 = f32[128,4096]{1,0:T(8,128)} custom-call(bf16[128,4096]{1,0:T(8,128)(2,1)S(1)} %copy-done.4, bf16[128,512]{1,0:T(8,128)(2,1)S(1)} %copy-done.8, bf16[128,512]{1,0:T(8,128)(2,1)S(1)} %copy-done.7, bf16[128,128]{1,0:T(8,128)(2,1)} %step.7, bf16[128,128]{1,0:T(8,128)(2,1)} %decay.11, f32[1,8192]{1,0:T(1,128)} %reshape_reshape.3.skip), custom_call_target="tpu_custom_call" | custom-call | tf_op jit(solution)/shard_map/within/pallas_call | solution.py:325
  143.9 6.2 %within.2 = f32[128,4096]{1,0:T(8,128)} custom-call(bf16[128,4096]{1,0:T(8,128)(2,1)S(1)} %copy-done.5, bf16[128,512]{1,0:T(8,128)(2,1)S(1)} %copy-done.9, bf16[128,512]{1,0:T(8,128)(2,1)S(1)} %copy-done.6, bf16[128,128]{1,0:T(8,128)(2,1)} %step.7, bf16[128,128]{1,0:T(8,128)(2,1)} %decay.11, f32[1,8192]{1,0:T(1,128)} %reshape_reshape.3.skip), custom_call_target="tpu_custom_call" | custom-call | tf_op jit(solution)/shard_map/within/pallas_call | solution.py:325
  150.1 2.8 %outputs.2.rest_0_ = bf16[128,8192]{1,0:T(8,128)(2,1)} custom-call(f32[128,4096]{1,0:T(8,128)S(1)} %copy-done.1, bf16[128,512]{1,0:T(8,128)(2,1)S(1)} %copy-done.7, bf16[128,128]{1,0:T(8,128)(2,1)} %decay.11, bf16[32,128,128]{2,1,0:T(8,128)(2,1)S(1)} %copy-done.3), custom_call_target="tpu_custom_call" | custom-call | tf_op jit(solution)/shard_map/outputs/pallas_call | solution.py:375
  152.9 11.3 %all-to-all-done.3.entering = bf16[32,128,128]{2,1,0:T(8,128)(2,1)S(1)} async-done(((bf16[32,128,128]{2,1,0:T(8,128)(2,1)}), bf16[32,128,128]{2,1,0:T(8,128)(2,1)S(1)}, u32[]{:S(2)}, u32[]{:S(2)}) %all-to-all-start.3) | async-done | bytes 1048608 | tf_op jit(solution)/shard_map/all_to_all | solution.py:394
  164.2 2.6 %outputs.3 = bf16[128,8192]{1,0:T(8,128)(2,1)} custom-call(f32[128,4096]{1,0:T(8,128)S(1)} %copy-done, bf16[128,512]{1,0:T(8,128)(2,1)S(1)} %copy-done.6, bf16[128,128]{1,0:T(8,128)(2,1)} %decay.11, bf16[32,128,128]{2,1,0:T(8,128)(2,1)S(1)} %all-to-all-done.3.entering, bf16[128,8192]{1,0:T(8,128)(2,1)} %outputs.2.rest_0_), custom_call_target="tpu_custom_call", output_to_operand_aliasing={{}: (4, {})} | custom-call | tf_op jit(solution)/shard_map/outputs/pallas_call | solution.py:375
  (47 shorter events, 29.2 us)
Async XLA Ops:
  1.0 15.6 %collective-permute-start = (bf16[3,10240]{1,0:T(4,128)(2,1)S(1)}, bf16[3,10240]{1,0:T(4,128)(2,1)S(1)}, u32[]{:S(2)}, u32[]{:S(2)}) collective-permute-start(bf16[3,10240]{1,0:T(4,128)(2,1)S(1)} %slice.3), channel_id=1, source_target_pairs={{0,1},{1,2},{2,3},{3,4},{4,5},{5,6},{6,7},{7,8},{8,9},{9,10},{10,1... | collective-permute-start | bytes 184328 | tf_op jit(solution)/shard_map/ppermute | solution.py:268
  21.8 35.1 %all-to-all-start.1 = ((bf16[32,136,128]{2,1,0:T(8,128)(2,1)}), bf16[32,136,128]{2,1,0:T(8,128)(2,1)S(1)}, u32[]{:S(2)}, u32[]{:S(2)}) async-start(bf16[32,136,128]{2,1,0:T(8,128)(2,1)} %get-tuple-element.25), calls=%async_computation.1 | async-start | bytes 2228224 | tf_op jit(solution)/shard_map/all_to_all | solution.py:394
  56.8 33.4 %all-to-all-start = ((bf16[32,128,128]{2,1,0:T(8,128)(2,1)}), bf16[32,128,128]{2,1,0:T(8,128)(2,1)S(1)}, u32[]{:S(2)}, u32[]{:S(2)}) async-start(bf16[32,128,128]{2,1,0:T(8,128)(2,1)} %get-tuple-element.24), calls=%async_computation | async-start | bytes 2097152 | tf_op jit(solution)/shard_map/all_to_all | solution.py:394
  62.3 6.5 %collective-permute-start.1 = (bf16[136,128]{1,0:T(8,128)(2,1)S(1)}, bf16[136,128]{1,0:T(8,128)(2,1)S(1)}, u32[]{:S(2)}, u32[]{:S(2)}) collective-permute-start(bf16[136,128]{1,0:T(8,128)(2,1)S(1)} %section_total.2.own), channel_id=1, source_target_pairs={{0,32},{32,64},{64,96},{96,128},{128,160},{160,192},{192,224},{224... | collective-permute-start | bytes 104456 | tf_op jit(solution)/shard_map/ppermute | solution.py:237
  64.2 6.0 %collective-permute-start.2 = (bf16[136,128]{1,0:T(8,128)(2,1)S(1)}, bf16[136,128]{1,0:T(8,128)(2,1)S(1)}, u32[]{:S(2)}, u32[]{:S(2)}) collective-permute-start(bf16[136,128]{1,0:T(8,128)(2,1)S(1)} %section_total.2.own), channel_id=1, source_target_pairs={{0,64},{32,96},{64,128},{96,160},{128,192},{160,224},{192,256},{22... | collective-permute-start | bytes 104456 | tf_op jit(solution)/shard_map/ppermute | solution.py:237
  66.8 6.2 %collective-permute-start.3 = (bf16[136,128]{1,0:T(8,128)(2,1)S(1)}, bf16[136,128]{1,0:T(8,128)(2,1)S(1)}, u32[]{:S(2)}, u32[]{:S(2)}) collective-permute-start(bf16[136,128]{1,0:T(8,128)(2,1)S(1)} %section_total.2.own), channel_id=1, source_target_pairs={{0,96},{32,128},{64,160},{96,192},{128,224},{160,256},{192,288},{2... | collective-permute-start | bytes 104456 | tf_op jit(solution)/shard_map/ppermute | solution.py:237
  73.0 8.0 %collective-permute-start.4 = (bf16[136,128]{1,0:T(8,128)(2,1)S(1)}, bf16[136,128]{1,0:T(8,128)(2,1)S(1)}, u32[]{:S(2)}, u32[]{:S(2)}) collective-permute-start(bf16[136,128]{1,0:T(8,128)(2,1)S(1)} %get-tuple-element.27), channel_id=1, source_target_pairs={{0,128},{32,160},{64,192},{96,224},{128,256},{160,288},{192,320},{... | collective-permute-start | bytes 104456 | tf_op jit(solution)/shard_map/ppermute | solution.py:237
  74.3 11.2 %collective-permute-start.5 = (bf16[136,128]{1,0:T(8,128)(2,1)S(1)}, bf16[136,128]{1,0:T(8,128)(2,1)S(1)}, u32[]{:S(2)}, u32[]{:S(2)}) collective-permute-start(bf16[136,128]{1,0:T(8,128)(2,1)S(1)} %get-tuple-element.27), channel_id=1, source_target_pairs={{0,256},{32,288},{64,320},{96,352},{128,384},{160,416},{192,448},{... | collective-permute-start | bytes 104456 | tf_op jit(solution)/shard_map/ppermute | solution.py:237
  75.6 11.9 %collective-permute-start.6 = (bf16[136,128]{1,0:T(8,128)(2,1)S(1)}, bf16[136,128]{1,0:T(8,128)(2,1)S(1)}, u32[]{:S(2)}, u32[]{:S(2)}) collective-permute-start(bf16[136,128]{1,0:T(8,128)(2,1)S(1)} %get-tuple-element.27), channel_id=1, source_target_pairs={{0,384},{32,416},{64,448},{96,480},{1,385},{33,417},{65,449},{97,4... | collective-permute-start | bytes 104456 | tf_op jit(solution)/shard_map/ppermute | solution.py:237
  90.2 35.8 %all-to-all-start.2 = ((bf16[32,128,128]{2,1,0:T(8,128)(2,1)}), bf16[32,128,128]{2,1,0:T(8,128)(2,1)S(1)}, u32[]{:S(2)}, u32[]{:S(2)}) async-start(bf16[32,128,128]{2,1,0:T(8,128)(2,1)} %entering.2), calls=%async_computation.2 | async-start | bytes 2097152 | tf_op jit(solution)/shard_map/all_to_all | solution.py:394
  98.9 5.9 %collective-permute-start.7 = (bf16[136,128]{1,0:T(8,128)(2,1)S(1)}, bf16[136,128]{1,0:T(8,128)(2,1)S(1)}, u32[]{:S(2)}, u32[]{:S(2)}) collective-permute-start(bf16[136,128]{1,0:T(8,128)(2,1)S(1)} %section_total.3.own), channel_id=1, source_target_pairs={{0,32},{32,64},{64,96},{96,128},{128,160},{160,192},{192,224},{224... | collective-permute-start | bytes 104456 | tf_op jit(solution)/shard_map/ppermute | solution.py:237
  100.9 5.8 %collective-permute-start.8 = (bf16[136,128]{1,0:T(8,128)(2,1)S(1)}, bf16[136,128]{1,0:T(8,128)(2,1)S(1)}, u32[]{:S(2)}, u32[]{:S(2)}) collective-permute-start(bf16[136,128]{1,0:T(8,128)(2,1)S(1)} %section_total.3.own), channel_id=1, source_target_pairs={{0,64},{32,96},{64,128},{96,160},{128,192},{160,224},{192,256},{22... | collective-permute-start | bytes 104456 | tf_op jit(solution)/shard_map/ppermute | solution.py:237
  103.0 6.3 %collective-permute-start.9 = (bf16[136,128]{1,0:T(8,128)(2,1)S(1)}, bf16[136,128]{1,0:T(8,128)(2,1)S(1)}, u32[]{:S(2)}, u32[]{:S(2)}) collective-permute-start(bf16[136,128]{1,0:T(8,128)(2,1)S(1)} %section_total.3.own), channel_id=1, source_target_pairs={{0,96},{32,128},{64,160},{96,192},{128,224},{160,256},{192,288},{2... | collective-permute-start | bytes 104456 | tf_op jit(solution)/shard_map/ppermute | solution.py:237
  109.3 7.1 %collective-permute-start.10 = (bf16[136,128]{1,0:T(8,128)(2,1)S(1)}, bf16[136,128]{1,0:T(8,128)(2,1)S(1)}, u32[]{:S(2)}, u32[]{:S(2)}) collective-permute-start(bf16[136,128]{1,0:T(8,128)(2,1)S(1)} %get-tuple-element.31), channel_id=1, source_target_pairs={{0,128},{32,160},{64,192},{96,224},{128,256},{160,288},{192,320},{... | collective-permute-start | bytes 104456 | tf_op jit(solution)/shard_map/ppermute | solution.py:237
  110.6 9.8 %collective-permute-start.11 = (bf16[136,128]{1,0:T(8,128)(2,1)S(1)}, bf16[136,128]{1,0:T(8,128)(2,1)S(1)}, u32[]{:S(2)}, u32[]{:S(2)}) collective-permute-start(bf16[136,128]{1,0:T(8,128)(2,1)S(1)} %get-tuple-element.31), channel_id=1, source_target_pairs={{0,256},{32,288},{64,320},{96,352},{128,384},{160,416},{192,448},{... | collective-permute-start | bytes 104456 | tf_op jit(solution)/shard_map/ppermute | solution.py:237
  111.9 11.3 %collective-permute-start.12 = (bf16[136,128]{1,0:T(8,128)(2,1)S(1)}, bf16[136,128]{1,0:T(8,128)(2,1)S(1)}, u32[]{:S(2)}, u32[]{:S(2)}) collective-permute-start(bf16[136,128]{1,0:T(8,128)(2,1)S(1)} %get-tuple-element.31), channel_id=1, source_target_pairs={{0,384},{32,416},{64,448},{96,480},{1,385},{33,417},{65,449},{97,4... | collective-permute-start | bytes 104456 | tf_op jit(solution)/shard_map/ppermute | solution.py:237
  123.2 12.3 %copy-start.10 = (f32[128]{0:T(128)S(1)}, f32[128]{0:T(128)}, u32[]{:S(2)}) copy-start(f32[128]{0:T(128)} %param.11) | copy-start | bytes 1540
  123.2 14.6 %copy-start.7 = (bf16[128,512]{1,0:T(8,128)(2,1)S(1)}, bf16[128,512]{1,0:T(8,128)(2,1)}, u32[]{:S(2)}) copy-start(bf16[128,512]{1,0:T(8,128)(2,1)} %get-tuple-element.35.c_in) | copy-start | bytes 393220
  123.2 14.6 %copy-start.8 = (bf16[128,512]{1,0:T(8,128)(2,1)S(1)}, bf16[128,512]{1,0:T(8,128)(2,1)}, u32[]{:S(2)}) copy-start(bf16[128,512]{1,0:T(8,128)(2,1)} %get-tuple-element.34.b_in) | copy-start | bytes 393220
  124.5 13.2 %copy-start.4 = (bf16[128,4096]{1,0:T(8,128)(2,1)S(1)}, bf16[128,4096]{1,0:T(8,128)(2,1)}, u32[]{:S(2)}) copy-start(bf16[128,4096]{1,0:T(8,128)(2,1)} %get-tuple-element.33.x_in) | copy-start | bytes 3145732
  126.9 37.2 %all-to-all-start.3 = ((bf16[32,128,128]{2,1,0:T(8,128)(2,1)}), bf16[32,128,128]{2,1,0:T(8,128)(2,1)S(1)}, u32[]{:S(2)}, u32[]{:S(2)}) async-start(bf16[32,128,128]{2,1,0:T(8,128)(2,1)} %entering.3), calls=%async_computation.3 | async-start | bytes 2097152 | tf_op jit(solution)/shard_map/all_to_all | solution.py:394
  135.5 8.3 %copy-start.5 = (bf16[128,4096]{1,0:T(8,128)(2,1)S(1)}, bf16[128,4096]{1,0:T(8,128)(2,1)}, u32[]{:S(2)}) copy-start(bf16[128,4096]{1,0:T(8,128)(2,1)} %get-tuple-element.21.x_in) | copy-start | bytes 3145732
  135.5 8.3 %copy-start.6 = (bf16[128,512]{1,0:T(8,128)(2,1)S(1)}, bf16[128,512]{1,0:T(8,128)(2,1)}, u32[]{:S(2)}) copy-start(bf16[128,512]{1,0:T(8,128)(2,1)} %get-tuple-element.23.c_in) | copy-start | bytes 393220
  150.1 14.1 %copy-start = (f32[128,4096]{1,0:T(8,128)S(1)}, f32[128,4096]{1,0:T(8,128)}, u32[]{:S(2)}) copy-start(f32[128,4096]{1,0:T(8,128)} %within.2) | copy-start | bytes 6291460
  (4 other events, 19.6 us)

commit v5 on v4

--- a/solution.py
+++ b/solution.py
@@ -18,7 +18,6 @@
 F32 = jnp.float32
 BF16 = jnp.bfloat16
 HALVES = 2
-RADIX = 4
 CONV_GROUPS = 4
 OUTPUT_GROUPS = 4
 
@@ -178,33 +177,19 @@
     total[N : N + 8, :] = decay_rows(jnp.sum(sums, axis=0, keepdims=True))
 
 
-def chained(parts, at):
-    state = parts[-1][at, :].astype(F32)
-    for part in reversed(parts[:-1]):
-        gain = jnp.exp(decay_of(part[N : N + 8, :]))
-        state = part[at, :].astype(F32) + gain * state
-    return state
-
-
-def join_kernel(own, *parts):
-    *nearby, before, through = parts
-    decay_own = decay_of(own[N : N + 8, :])
-    decay_near = sum(decay_of(part[N : N + 8, :]) for part in nearby)
-    near = chained(nearby, slice(0, N))
-    before[0:N, :] = near
-    before[N : N + 8, :] = jnp.broadcast_to(decay_near, (8, near.shape[1]))
-    through[0:N, :] = (own[0:N, :].astype(F32) + jnp.exp(decay_own) * near).astype(BF16)
-    through[N : N + 8, :] = decay_rows(decay_own + decay_near)
-
-
-def entering_kernel(half, states, decays, before, *parts):
-    *earlier, entering = parts
+def entering_kernel(half, states, decays, totals, entering):
     chunks = states.shape[0]
+    sections = totals.shape[0]
+    here = lax.axis_index("sec")
     gains = jnp.exp(chunk_decays(decays, half))
-    gain_near = jnp.exp(before[N : N + 1, :])
+    section_gains = jnp.exp(chunk_decays(totals[:, N : N + 8, :], 0))
     for part in range(N // 32):
         at = slice(part * 32, (part + 1) * 32)
-        carried = before[at, :] + gain_near * chained(earlier, at)
+        carried = jnp.zeros((32, states.shape[2]), F32)
+        for section in range(sections - 1):
+            after = section_gains[section : section + 1, :] * carried
+            after = after + totals[section, at, :].astype(F32)
+            carried = jnp.where(section < here, after, carried)
         for chunk in range(chunks):
             entering[chunk, at, :] = carried.astype(BF16)
             carried = gains[chunk : chunk + 1, :] * carried + states[chunk, at, :].astype(F32)
@@ -231,32 +216,9 @@
             out[:, wide] = (within[:, wide] + growth[:, lanes] * carried).astype(BF16)
 
 
-def from_earlier(value, step, count):
-    sections = lax.axis_size("sec")
-    return [
-        lax.ppermute(value, "sec", [(source, source + by) for source in range(sections - by)])
-        for by in range(step, step * count, step)
-        if by < sections
-    ]
-
-
-def before_section(total, params):
-    before, through = pl.pallas_call(
-        join_kernel,
-        out_shape=[
-            jax.ShapeDtypeStruct(total.shape, F32),
-            jax.ShapeDtypeStruct(total.shape, BF16),
-        ],
-        compiler_params=params,
-        name="join",
-    )(total, *from_earlier(total, 1, RADIX))
-    return before, *from_earlier(through, RADIX, RADIX)
-
-
 def per_device(projected, conv_weight, conv_bias, step_size, log_decay, skip_gain):
     targets = lax.axis_size("cp")
     sections = lax.axis_size("sec")
-    assert sections <= RADIX * RADIX
     rows = projected.shape[0]
     width_all = projected.shape[1]
     devices = targets * sections
@@ -357,16 +319,17 @@
             name="section_total",
         )(states, first_states)
 
-    def entering_states(half, states, first_states, carried_in):
+    def entering_states(half, states, first_states, totals):
         return pl.pallas_call(
             functools.partial(entering_kernel, half),
             grid=(1,),
-            in_specs=arrived_specs + [total_spec] * len(carried_in),
+            in_specs=arrived_specs
+            + [pl.BlockSpec((sections, N + 8, width_here), lambda g: (0, 0, 0))],
             out_specs=pl.BlockSpec((targets, N, width_here), lambda g: (0, 0, 0)),
             out_shape=pltpu.HBM((targets, N, width_here), BF16),
             compiler_params=params,
             name="entering",
-        )(states, first_states, *carried_in)
+        )(states, first_states, totals)
 
     def outputs(half, within, query_c, entering, so_far):
         at_once = OUTPUT_GROUPS
@@ -407,8 +370,8 @@
         if half:
             state, leaving = lax.optimization_barrier((state, leaving))
             arrived.append(exchanged(leaving))
-        total = section_total(half, state, states[0])
-        leaving = entering_states(half, state, states[0], before_section(total, params))
+        totals = lax.all_gather(section_total(half, state, states[0]), "sec")
+        leaving = entering_states(half, state, states[0], totals)
     if arrived:
         arrived[-1], leaving = lax.optimization_barrier((arrived[-1], leaving))
     arrived.append(exchanged(leaving))

time: 168 us -> 161 us (0.958)
  the two profiles are of different devices: /device:TPU:48 before, /device:TPU:40 now
where the time goes in v5:
time: 161 us; the launch traced here: 160 us
  waiting for transfers between devices  67.3 us (42%)
  blocking collectives  32.3 us (20%)
  Pallas kernels  31.8 us (20%)
  starting transfers between devices  24.4 us (15%)
  local copies, waits for them, and re-layouts  4.23 us (3%)
    all_to_all x4, waiting for transfers between devices, exchanged(): return lax.all_to_all(value, 'cp', split_axis=0, concat_axis=0, tiled=True)  56 us
    all_gather x2, blocking collectives, per_device(): totals = lax.all_gather(section_total(half, state, states[0]), 'sec')  32.3 us
    all_to_all x4, starting transfers between devices, exchanged(): return lax.all_to_all(value, 'cp', split_axis=0, concat_axis=0, tiled=True)  20.2 us
    pallas_call x2, Pallas kernels, within_chunk(): pl.pallas_call(functools.partial(within_kernel, first), grid=(groups,), i...  12.3 us
    ppermute x1, waiting for transfers between devices, per_device(): lax.ppermute(projected[rows - (KERNEL - 1):], ('sec', 'cp'), [(source, so...  11.3 us
    pallas_call x2, Pallas kernels, conv_states(): pl.pallas_call(functools.partial(conv_states_kernel, half * groups), grid...  10.4 us
    pallas_call x2, Pallas kernels, outputs(): pl.pallas_call(functools.partial(outputs_kernel, half * groups), grid=(gr...  5.45 us
    ppermute x1, starting transfers between devices, per_device(): lax.ppermute(projected[rows - (KERNEL - 1):], ('sec', 'cp'), [(source, so...  4.28 us
  transfers between devices with their start and end apart: 5, of which 5 were waited for; matrix products, arithmetic and copies ran while one was open for 1% of the time, Pallas kernels for 15%

profile of v5, /device:TPU:40, one launch (start us, length us, event | category | flops | bytes accessed | tf_op | source)
XLA Modules:
  0.0 160.3 jit_solution(8656378459955927070)
XLA Ops:
  0.0 1.0 slice.3
  1.0 4.3 %collective-permute-start = (bf16[3,10240]{1,0:T(4,128)(2,1)S(1)}, bf16[3,10240]{1,0:T(4,128)(2,1)S(1)}, u32[]{:S(2)}, u32[]{:S(2)}) collective-permute-start(bf16[3,10240]{1,0:T(4,128)(2,1)S(1)} %slice.3), channel_id=1, source_target_pairs={{0,1},{1,2},{2,3},{3,4},{4,5},{5,6},{6,7},{7,8},{8,9},{9,10},{10,1... | collective-permute-start | bytes 184328 | tf_op jit(solution)/shard_map/ppermute | solution.py:230
  5.3 11.3 %collective-permute-done.x_rim.b_rim.c_rim = bf16[3,10240]{1,0:T(4,128)(2,1)S(1)} collective-permute-done((bf16[3,10240]{1,0:T(4,128)(2,1)S(1)}, bf16[3,10240]{1,0:T(4,128)(2,1)S(1)}, u32[]{:S(2)}, u32[]{:S(2)}) %collective-permute-start) | collective-permute-done | bytes 61472 | tf_op jit(solution)/shard_map/ppermute | solution.py:230
  16.5 5.2 %conv_states.3 = (bf16[128,4096]{1,0:T(8,128)(2,1)}, bf16[128,512]{1,0:T(8,128)(2,1)}, bf16[128,512]{1,0:T(8,128)(2,1)}, bf16[32,136,128]{2,1,0:T(8,128)(2,1)}) custom-call(bf16[128,10240]{1,0:T(8,128)(2,1)} %c_in.3, bf16[128,10240]{1,0:T(8,128)(2,1)} %c_in.3, bf16[128,10240]{1,0:T(8,128)(2,1)} %c_in.3, ...), custom_call_target="tpu_custom_call" | custom-call | tf_op jit(solution)/shard_map/conv_states/pallas_call | solution.py:259
  21.8 5.1 %all-to-all-start.1 = ((bf16[32,136,128]{2,1,0:T(8,128)(2,1)}), bf16[32,136,128]{2,1,0:T(8,128)(2,1)S(1)}, u32[]{:S(2)}, u32[]{:S(2)}) async-start(bf16[32,136,128]{2,1,0:T(8,128)(2,1)} %get-tuple-element.21), calls=%async_computation.1 | async-start | bytes 2228224 | tf_op jit(solution)/shard_map/all_to_all | solution.py:357
  26.9 5.2 %conv_states.2 = (bf16[128,4096]{1,0:T(8,128)(2,1)}, bf16[128,512]{1,0:T(8,128)(2,1)}, bf16[128,512]{1,0:T(8,128)(2,1)}, bf16[32,128,128]{2,1,0:T(8,128)(2,1)}) custom-call(bf16[128,10240]{1,0:T(8,128)(2,1)} %c_in.3, bf16[128,10240]{1,0:T(8,128)(2,1)} %c_in.3, bf16[128,10240]{1,0:T(8,128)(2,1)} %c_in.3, ...), custom_call_target="tpu_custom_call" | custom-call | tf_op jit(solution)/shard_map/conv_states/pallas_call | solution.py:259
  32.1 24.7 %all-to-all-done.1.states.decays = bf16[32,136,128]{2,1,0:T(8,128)(2,1)S(1)} async-done(((bf16[32,136,128]{2,1,0:T(8,128)(2,1)}), bf16[32,136,128]{2,1,0:T(8,128)(2,1)S(1)}, u32[]{:S(2)}, u32[]{:S(2)}) %all-to-all-start.1) | async-done | bytes 1114144 | tf_op jit(solution)/shard_map/all_to_all | solution.py:357
  56.8 5.1 %all-to-all-start = ((bf16[32,128,128]{2,1,0:T(8,128)(2,1)}), bf16[32,128,128]{2,1,0:T(8,128)(2,1)S(1)}, u32[]{:S(2)}, u32[]{:S(2)}) async-start(bf16[32,128,128]{2,1,0:T(8,128)(2,1)} %get-tuple-element.20), calls=%async_computation | async-start | bytes 2097152 | tf_op jit(solution)/shard_map/all_to_all | solution.py:357
  62.3 16.2 %all-gather = bf16[2176,128]{1,0:T(8,128)(2,1)S(1)} all-gather(bf16[136,128]{1,0:T(8,128)(2,1)S(1)} %section_total.2), channel_id=2, replica_groups=mesh['sec'=16,'cp'=32] {'sec'}, dimensions={0}, use_global_device_ids=true | all-gather | bytes 591872 | tf_op jit(solution)/shard_map/all_gather | solution.py:373
  78.5 1.5 entering.2
  80.0 10.2 %all-to-all-done.states = bf16[32,128,128]{2,1,0:T(8,128)(2,1)S(1)} async-done(((bf16[32,128,128]{2,1,0:T(8,128)(2,1)}), bf16[32,128,128]{2,1,0:T(8,128)(2,1)S(1)}, u32[]{:S(2)}, u32[]{:S(2)}) %all-to-all-start) | async-done | bytes 1048608 | tf_op jit(solution)/shard_map/all_to_all | solution.py:357
  90.2 4.9 %all-to-all-start.2 = ((bf16[32,128,128]{2,1,0:T(8,128)(2,1)}), bf16[32,128,128]{2,1,0:T(8,128)(2,1)S(1)}, u32[]{:S(2)}, u32[]{:S(2)}) async-start(bf16[32,128,128]{2,1,0:T(8,128)(2,1)} %entering.2), calls=%async_computation.2 | async-start | bytes 2097152 | tf_op jit(solution)/shard_map/all_to_all | solution.py:357
  95.4 16.1 %all-gather.1 = bf16[2176,128]{1,0:T(8,128)(2,1)S(1)} all-gather(bf16[136,128]{1,0:T(8,128)(2,1)S(1)} %section_total.3), channel_id=3, replica_groups=mesh['sec'=16,'cp'=32] {'sec'}, dimensions={0}, use_global_device_ids=true | all-gather | bytes 591872 | tf_op jit(solution)/shard_map/all_gather | solution.py:373
  111.6 1.5 entering.3
  113.0 10.4 %all-to-all-done.2.entering = bf16[32,128,128]{2,1,0:T(8,128)(2,1)S(1)} async-done(((bf16[32,128,128]{2,1,0:T(8,128)(2,1)}), bf16[32,128,128]{2,1,0:T(8,128)(2,1)S(1)}, u32[]{:S(2)}, u32[]{:S(2)}) %all-to-all-start.2) | async-done | bytes 1048608 | tf_op jit(solution)/shard_map/all_to_all | solution.py:357
  123.4 1.0 copy-done.2
  124.4 5.1 %all-to-all-start.3 = ((bf16[32,128,128]{2,1,0:T(8,128)(2,1)}), bf16[32,128,128]{2,1,0:T(8,128)(2,1)S(1)}, u32[]{:S(2)}, u32[]{:S(2)}) async-start(bf16[32,128,128]{2,1,0:T(8,128)(2,1)} %entering.3), calls=%async_computation.3 | async-start | bytes 2097152 | tf_op jit(solution)/shard_map/all_to_all | solution.py:357
  129.5 0.7 broadcast_in_dim.3
  130.2 1.5 reshape_reshape.3.skip
  131.8 6.1 %within.3 = f32[128,4096]{1,0:T(8,128)} custom-call(bf16[128,4096]{1,0:T(8,128)(2,1)S(1)} %copy-done.4, bf16[128,512]{1,0:T(8,128)(2,1)S(1)} %copy-done.8, bf16[128,512]{1,0:T(8,128)(2,1)S(1)} %copy-done.7, bf16[128,128]{1,0:T(8,128)(2,1)} %step.7, bf16[128,128]{1,0:T(8,128)(2,1)} %decay.11, f32[1,8192]{1,0:T(1,128)} %reshape_reshape.3.skip), custom_call_target="tpu_custom_call" | custom-call | tf_op jit(solution)/shard_map/within/pallas_call | solution.py:287
  137.9 6.2 %within.2 = f32[128,4096]{1,0:T(8,128)} custom-call(bf16[128,4096]{1,0:T(8,128)(2,1)S(1)} %copy-done.5, bf16[128,512]{1,0:T(8,128)(2,1)S(1)} %copy-done.9, bf16[128,512]{1,0:T(8,128)(2,1)S(1)} %copy-done.6, bf16[128,128]{1,0:T(8,128)(2,1)} %step.7, bf16[128,128]{1,0:T(8,128)(2,1)} %decay.11, f32[1,8192]{1,0:T(1,128)} %reshape_reshape.3.skip), custom_call_target="tpu_custom_call" | custom-call | tf_op jit(solution)/shard_map/within/pallas_call | solution.py:287
  144.1 2.8 %outputs.2.rest_0_ = bf16[128,8192]{1,0:T(8,128)(2,1)} custom-call(f32[128,4096]{1,0:T(8,128)S(1)} %copy-done.1, bf16[128,512]{1,0:T(8,128)(2,1)S(1)} %copy-done.7, bf16[128,128]{1,0:T(8,128)(2,1)} %decay.11, bf16[32,128,128]{2,1,0:T(8,128)(2,1)S(1)} %copy-done.3), custom_call_target="tpu_custom_call" | custom-call | tf_op jit(solution)/shard_map/outputs/pallas_call | solution.py:338
  146.9 10.7 %all-to-all-done.3.entering = bf16[32,128,128]{2,1,0:T(8,128)(2,1)S(1)} async-done(((bf16[32,128,128]{2,1,0:T(8,128)(2,1)}), bf16[32,128,128]{2,1,0:T(8,128)(2,1)S(1)}, u32[]{:S(2)}, u32[]{:S(2)}) %all-to-all-start.3) | async-done | bytes 1048608 | tf_op jit(solution)/shard_map/all_to_all | solution.py:357
  157.6 2.6 %outputs.3 = bf16[128,8192]{1,0:T(8,128)(2,1)} custom-call(f32[128,4096]{1,0:T(8,128)S(1)} %copy-done, bf16[128,512]{1,0:T(8,128)(2,1)S(1)} %copy-done.6, bf16[128,128]{1,0:T(8,128)(2,1)} %decay.11, bf16[32,128,128]{2,1,0:T(8,128)(2,1)S(1)} %all-to-all-done.3.entering, bf16[128,8192]{1,0:T(8,128)(2,1)} %outputs.2.rest_0_), custom_call_target="tpu_custom_call", output_to_operand_aliasing={{}: (4, {})} | custom-call | tf_op jit(solution)/shard_map/outputs/pallas_call | solution.py:338
  (23 shorter events, 0.7 us)
Async XLA Ops:
  1.0 15.6 %collective-permute-start = (bf16[3,10240]{1,0:T(4,128)(2,1)S(1)}, bf16[3,10240]{1,0:T(4,128)(2,1)S(1)}, u32[]{:S(2)}, u32[]{:S(2)}) collective-permute-start(bf16[3,10240]{1,0:T(4,128)(2,1)S(1)} %slice.3), channel_id=1, source_target_pairs={{0,1},{1,2},{2,3},{3,4},{4,5},{5,6},{6,7},{7,8},{8,9},{9,10},{10,1... | collective-permute-start | bytes 184328 | tf_op jit(solution)/shard_map/ppermute | solution.py:230
  21.8 35.1 %all-to-all-start.1 = ((bf16[32,136,128]{2,1,0:T(8,128)(2,1)}), bf16[32,136,128]{2,1,0:T(8,128)(2,1)S(1)}, u32[]{:S(2)}, u32[]{:S(2)}) async-start(bf16[32,136,128]{2,1,0:T(8,128)(2,1)} %get-tuple-element.21), calls=%async_computation.1 | async-start | bytes 2228224 | tf_op jit(solution)/shard_map/all_to_all | solution.py:357
  56.8 33.4 %all-to-all-start = ((bf16[32,128,128]{2,1,0:T(8,128)(2,1)}), bf16[32,128,128]{2,1,0:T(8,128)(2,1)S(1)}, u32[]{:S(2)}, u32[]{:S(2)}) async-start(bf16[32,128,128]{2,1,0:T(8,128)(2,1)} %get-tuple-element.20), calls=%async_computation | async-start | bytes 2097152 | tf_op jit(solution)/shard_map/all_to_all | solution.py:357
  90.2 33.2 %all-to-all-start.2 = ((bf16[32,128,128]{2,1,0:T(8,128)(2,1)}), bf16[32,128,128]{2,1,0:T(8,128)(2,1)S(1)}, u32[]{:S(2)}, u32[]{:S(2)}) async-start(bf16[32,128,128]{2,1,0:T(8,128)(2,1)} %entering.2), calls=%async_computation.2 | async-start | bytes 2097152 | tf_op jit(solution)/shard_map/all_to_all | solution.py:357
  111.6 17.9 %copy-start.10 = (f32[128]{0:T(128)S(1)}, f32[128]{0:T(128)}, u32[]{:S(2)}) copy-start(f32[128]{0:T(128)} %param.11) | copy-start | bytes 1540
  111.6 20.2 %copy-start.7 = (bf16[128,512]{1,0:T(8,128)(2,1)S(1)}, bf16[128,512]{1,0:T(8,128)(2,1)}, u32[]{:S(2)}) copy-start(bf16[128,512]{1,0:T(8,128)(2,1)} %get-tuple-element.27.c_in) | copy-start | bytes 393220
  111.6 20.2 %copy-start.8 = (bf16[128,512]{1,0:T(8,128)(2,1)S(1)}, bf16[128,512]{1,0:T(8,128)(2,1)}, u32[]{:S(2)}) copy-start(bf16[128,512]{1,0:T(8,128)(2,1)} %get-tuple-element.26.b_in) | copy-start | bytes 393220
  113.0 18.8 %copy-start.4 = (bf16[128,4096]{1,0:T(8,128)(2,1)S(1)}, bf16[128,4096]{1,0:T(8,128)(2,1)}, u32[]{:S(2)}) copy-start(bf16[128,4096]{1,0:T(8,128)(2,1)} %get-tuple-element.25.x_in) | copy-start | bytes 3145732
  123.4 1.0 copy-start.2
  124.4 33.2 %all-to-all-start.3 = ((bf16[32,128,128]{2,1,0:T(8,128)(2,1)}), bf16[32,128,128]{2,1,0:T(8,128)(2,1)S(1)}, u32[]{:S(2)}, u32[]{:S(2)}) async-start(bf16[32,128,128]{2,1,0:T(8,128)(2,1)} %entering.3), calls=%async_computation.3 | async-start | bytes 2097152 | tf_op jit(solution)/shard_map/all_to_all | solution.py:357
  129.5 8.4 %copy-start.5 = (bf16[128,4096]{1,0:T(8,128)(2,1)S(1)}, bf16[128,4096]{1,0:T(8,128)(2,1)}, u32[]{:S(2)}) copy-start(bf16[128,4096]{1,0:T(8,128)(2,1)} %get-tuple-element.17.x_in) | copy-start | bytes 3145732
  129.5 8.3 %copy-start.6 = (bf16[128,512]{1,0:T(8,128)(2,1)S(1)}, bf16[128,512]{1,0:T(8,128)(2,1)}, u32[]{:S(2)}) copy-start(bf16[128,512]{1,0:T(8,128)(2,1)} %get-tuple-element.19.c_in) | copy-start | bytes 393220
  131.8 6.1 %copy-start.9 = (bf16[128,512]{1,0:T(8,128)(2,1)S(1)}, bf16[128,512]{1,0:T(8,128)(2,1)}, u32[]{:S(2)}) copy-start(bf16[128,512]{1,0:T(8,128)(2,1)} %get-tuple-element.18.b_in) | copy-start | bytes 393220
  137.8 6.3 %copy-start.1 = (f32[128,4096]{1,0:T(8,128)S(1)}, f32[128,4096]{1,0:T(8,128)}, u32[]{:S(2)}) copy-start(f32[128,4096]{1,0:T(8,128)} %within.3) | copy-start | bytes 6291460
  137.8 6.3 %copy-start.3 = (bf16[32,128,128]{2,1,0:T(8,128)(2,1)S(1)}, bf16[32,128,128]{2,1,0:T(8,128)(2,1)}, u32[]{:S(2)}) copy-start(bf16[32,128,128]{2,1,0:T(8,128)(2,1)} %copy-done.2) | copy-start | bytes 3145732
  144.1 13.5 %copy-start = (f32[128,4096]{1,0:T(8,128)S(1)}, f32[128,4096]{1,0:T(8,128)}, u32[]{:S(2)}) copy-start(f32[128,4096]{1,0:T(8,128)} %within.2) | copy-start | bytes 6291460

commit v6 on v5

--- a/solution.py
+++ b/solution.py
@@ -356,11 +356,13 @@
     def exchanged(value):
         return lax.all_to_all(value, "cp", split_axis=0, concat_axis=0, tiled=True)
 
-    projected, conv_weight, bias, step_size, log_decay, skip_wide = (
-        pltpu.with_memory_space_constraint(value, pltpu.HBM)
-        for value in (projected, conv_weight, bias, step_size, log_decay, skip_wide)
-    )
-    convs = [conv_states(half) for half in range(HALVES)]
+    def in_hbm(values):
+        return [pltpu.with_memory_space_constraint(value, pltpu.HBM) for value in values]
+
+    projected, conv_weight, bias, step_size, log_decay, skip_wide = in_hbm(
+        (projected, conv_weight, bias, step_size, log_decay, skip_wide)
+    )
+    convs = [in_hbm(conv_states(half)) for half in range(HALVES)]
     states = [exchanged(conv[3]) for conv in convs]
     withins = [within_chunk(half, *convs[half][:3]) for half in range(HALVES)]
     arrived = []

time: 161 us -> 161 us (level)
  the two profiles are of different devices: /device:TPU:40 before, /device:TPU:64 now
where the time goes in v6:
time: 161 us; the launch traced here: 160 us
  waiting for transfers between devices  49 us (30%)
  blocking collectives  39.1 us (24%)
  Pallas kernels  37.3 us (23%)
  starting transfers between devices  32.4 us (20%)
  local copies, waits for them, and re-layouts  1.78 us (1%)
    all_to_all x4, waiting for transfers between devices, exchanged(): return lax.all_to_all(value, 'cp', split_axis=0, concat_axis=0, tiled=True)  44.6 us
    all_gather x2, blocking collectives, per_device(): totals = lax.all_gather(section_total(half, state, states[0]), 'sec')  39.1 us
    all_to_all x4, starting transfers between devices, exchanged(): return lax.all_to_all(value, 'cp', split_axis=0, concat_axis=0, tiled=True)  28.1 us
    pallas_call x2, Pallas kernels, within_chunk(): pl.pallas_call(functools.partial(within_kernel, first), grid=(groups,), i...  12.6 us
    pallas_call x2, Pallas kernels, conv_states(): pl.pallas_call(functools.partial(conv_states_kernel, half * groups), grid...  10.5 us
    pallas_call x2, Pallas kernels, outputs(): pl.pallas_call(functools.partial(outputs_kernel, half * groups), grid=(gr...  5.74 us
    pallas_call x2, Pallas kernels, entering_states(): pl.pallas_call(functools.partial(entering_kernel, half), grid=(1,), in_sp...  5.4 us
    ppermute x1, waiting for transfers between devices, per_device(): lax.ppermute(projected[rows - (KERNEL - 1):], ('sec', 'cp'), [(source, so...  4.43 us
  transfers between devices with their start and end apart: 5, of which 5 were waited for; matrix products, arithmetic and copies ran while one was open for 0% of the time, Pallas kernels for 18%

profile of v6, /device:TPU:64, one launch (start us, length us, event | category | flops | bytes accessed | tf_op | source)
XLA Modules:
  0.0 159.7 jit_solution(15837220513979634457)
XLA Ops:
  0.0 1.0 slice.3
  1.0 4.3 %collective-permute-start = (bf16[3,10240]{1,0:T(4,128)(2,1)S(1)}, bf16[3,10240]{1,0:T(4,128)(2,1)S(1)}, u32[]{:S(2)}, u32[]{:S(2)}) collective-permute-start(bf16[3,10240]{1,0:T(4,128)(2,1)S(1)} %slice.3), channel_id=1, source_target_pairs={{0,1},{1,2},{2,3},{3,4},{4,5},{5,6},{6,7},{7,8},{8,9},{9,10},{10,1... | collective-permute-start | bytes 184328 | tf_op jit(solution)/shard_map/ppermute | solution.py:230
  5.3 4.4 %collective-permute-done.x_rim.b_rim.c_rim = bf16[3,10240]{1,0:T(4,128)(2,1)S(1)} collective-permute-done((bf16[3,10240]{1,0:T(4,128)(2,1)S(1)}, bf16[3,10240]{1,0:T(4,128)(2,1)S(1)}, u32[]{:S(2)}, u32[]{:S(2)}) %collective-permute-start) | collective-permute-done | bytes 61472 | tf_op jit(solution)/shard_map/ppermute | solution.py:230
  9.7 5.3 %conv_states.3 = (bf16[128,4096]{1,0:T(8,128)(2,1)}, bf16[128,512]{1,0:T(8,128)(2,1)}, bf16[128,512]{1,0:T(8,128)(2,1)}, bf16[32,136,128]{2,1,0:T(8,128)(2,1)}) custom-call(bf16[128,10240]{1,0:T(8,128)(2,1)} %c_in.3, bf16[128,10240]{1,0:T(8,128)(2,1)} %c_in.3, bf16[128,10240]{1,0:T(8,128)(2,1)} %c_in.3, ...), custom_call_target="tpu_custom_call" | custom-call | tf_op jit(solution)/shard_map/conv_states/pallas_call | solution.py:259
  15.0 11.4 %all-to-all-start.1 = ((bf16[32,136,128]{2,1,0:T(8,128)(2,1)}), bf16[32,136,128]{2,1,0:T(8,128)(2,1)S(1)}, u32[]{:S(2)}, u32[]{:S(2)}) async-start(bf16[32,136,128]{2,1,0:T(8,128)(2,1)} %get-tuple-element.21), calls=%async_computation.1 | async-start | bytes 2228224 | tf_op jit(solution)/shard_map/all_to_all | solution.py:357
  26.3 5.3 %conv_states.2 = (bf16[128,4096]{1,0:T(8,128)(2,1)}, bf16[128,512]{1,0:T(8,128)(2,1)}, bf16[128,512]{1,0:T(8,128)(2,1)}, bf16[32,128,128]{2,1,0:T(8,128)(2,1)}) custom-call(bf16[128,10240]{1,0:T(8,128)(2,1)} %c_in.3, bf16[128,10240]{1,0:T(8,128)(2,1)} %c_in.3, bf16[128,10240]{1,0:T(8,128)(2,1)} %c_in.3, ...), custom_call_target="tpu_custom_call" | custom-call | tf_op jit(solution)/shard_map/conv_states/pallas_call | solution.py:259
  31.6 23.7 %all-to-all-done.1.states.decays = bf16[32,136,128]{2,1,0:T(8,128)(2,1)S(1)} async-done(((bf16[32,136,128]{2,1,0:T(8,128)(2,1)}), bf16[32,136,128]{2,1,0:T(8,128)(2,1)S(1)}, u32[]{:S(2)}, u32[]{:S(2)}) %all-to-all-start.1) | async-done | bytes 1114144 | tf_op jit(solution)/shard_map/all_to_all | solution.py:357
  55.3 5.2 %all-to-all-start = ((bf16[32,128,128]{2,1,0:T(8,128)(2,1)}), bf16[32,128,128]{2,1,0:T(8,128)(2,1)S(1)}, u32[]{:S(2)}, u32[]{:S(2)}) async-start(bf16[32,128,128]{2,1,0:T(8,128)(2,1)} %get-tuple-element.20), calls=%async_computation | async-start | bytes 2097152 | tf_op jit(solution)/shard_map/all_to_all | solution.py:357
  60.6 1.5 section_total.2
  62.1 19.9 %all-gather = bf16[2176,128]{1,0:T(8,128)(2,1)S(1)} all-gather(bf16[136,128]{1,0:T(8,128)(2,1)S(1)} %section_total.2), channel_id=2, replica_groups=mesh['sec'=16,'cp'=32] {'sec'}, dimensions={0}, use_global_device_ids=true | all-gather | bytes 591872 | tf_op jit(solution)/shard_map/all_gather | solution.py:375
  82.0 2.7 %entering.2 = bf16[32,128,128]{2,1,0:T(8,128)(2,1)} custom-call(bf16[32,136,128]{2,1,0:T(8,128)(2,1)} %copy-done.4, bf16[32,136,128]{2,1,0:T(8,128)(2,1)} %copy-done.4, bf16[16,136,128]{2,1,0:T(8,128)(2,1)S(1)} %bitcast.4), custom_call_target="tpu_custom_call" | custom-call | tf_op jit(solution)/shard_map/entering/pallas_call | solution.py:323
  84.7 3.9 %all-to-all-done.states = bf16[32,128,128]{2,1,0:T(8,128)(2,1)S(1)} async-done(((bf16[32,128,128]{2,1,0:T(8,128)(2,1)}), bf16[32,128,128]{2,1,0:T(8,128)(2,1)S(1)}, u32[]{:S(2)}, u32[]{:S(2)}) %all-to-all-start) | async-done | bytes 1048608 | tf_op jit(solution)/shard_map/all_to_all | solution.py:357
  88.5 5.9 %all-to-all-start.2 = ((bf16[32,128,128]{2,1,0:T(8,128)(2,1)}), bf16[32,128,128]{2,1,0:T(8,128)(2,1)S(1)}, u32[]{:S(2)}, u32[]{:S(2)}) async-start(bf16[32,128,128]{2,1,0:T(8,128)(2,1)} %entering.2), calls=%async_computation.2 | async-start | bytes 2097152 | tf_op jit(solution)/shard_map/all_to_all | solution.py:357
  94.5 1.5 section_total.3
  96.0 19.2 %all-gather.1 = bf16[2176,128]{1,0:T(8,128)(2,1)S(1)} all-gather(bf16[136,128]{1,0:T(8,128)(2,1)S(1)} %section_total.3), channel_id=3, replica_groups=mesh['sec'=16,'cp'=32] {'sec'}, dimensions={0}, use_global_device_ids=true | all-gather | bytes 591872 | tf_op jit(solution)/shard_map/all_gather | solution.py:375
  115.2 2.7 %entering.3 = bf16[32,128,128]{2,1,0:T(8,128)(2,1)} custom-call(bf16[32,128,128]{2,1,0:T(8,128)(2,1)} %copy-done.5, bf16[32,136,128]{2,1,0:T(8,128)(2,1)} %copy-done.4, bf16[16,136,128]{2,1,0:T(8,128)(2,1)S(1)} %bitcast.3), custom_call_target="tpu_custom_call" | custom-call | tf_op jit(solution)/shard_map/entering/pallas_call | solution.py:323
  117.9 5.1 %all-to-all-done.2.entering = bf16[32,128,128]{2,1,0:T(8,128)(2,1)S(1)} async-done(((bf16[32,128,128]{2,1,0:T(8,128)(2,1)}), bf16[32,128,128]{2,1,0:T(8,128)(2,1)S(1)}, u32[]{:S(2)}, u32[]{:S(2)}) %all-to-all-start.2) | async-done | bytes 1048608 | tf_op jit(solution)/shard_map/all_to_all | solution.py:357
  123.1 5.6 %all-to-all-start.3 = ((bf16[32,128,128]{2,1,0:T(8,128)(2,1)}), bf16[32,128,128]{2,1,0:T(8,128)(2,1)S(1)}, u32[]{:S(2)}, u32[]{:S(2)}) async-start(bf16[32,128,128]{2,1,0:T(8,128)(2,1)} %entering.3), calls=%async_computation.3 | async-start | bytes 2097152 | tf_op jit(solution)/shard_map/all_to_all | solution.py:357
  128.8 0.7 reshape_reshape.3.skip
  129.5 6.2 %within.3 = f32[128,4096]{1,0:T(8,128)} custom-call(bf16[128,4096]{1,0:T(8,128)(2,1)} %get-tuple-element.25.x_in, bf16[128,512]{1,0:T(8,128)(2,1)} %get-tuple-element.26.b_in, bf16[128,512]{1,0:T(8,128)(2,1)} %get-tuple-element.27.c_in, bf16[128,128]{1,0:T(8,128)(2,1)} %step.7, bf16[128,128]{1,0:T(8,128)(2,1)} %decay.11, f32[1,8192]{1,0:T(1,128)} %reshape_reshape.3.skip), custom_call_target="tpu_custom_call" | custom-call | tf_op jit(solution)/shard_map/within/pallas_call | solution.py:287
  135.8 6.4 %within.2 = f32[128,4096]{1,0:T(8,128)} custom-call(bf16[128,4096]{1,0:T(8,128)(2,1)} %get-tuple-element.17.x_in, bf16[128,512]{1,0:T(8,128)(2,1)} %get-tuple-element.18.b_in, bf16[128,512]{1,0:T(8,128)(2,1)} %get-tuple-element.19.c_in, bf16[128,128]{1,0:T(8,128)(2,1)} %step.7, bf16[128,128]{1,0:T(8,128)(2,1)} %decay.11, f32[1,8192]{1,0:T(1,128)} %reshape_reshape.3.skip), custom_call_target="tpu_custom_call" | custom-call | tf_op jit(solution)/shard_map/within/pallas_call | solution.py:287
  142.2 2.9 %outputs.2.rest_0_ = bf16[128,8192]{1,0:T(8,128)(2,1)} custom-call(f32[128,4096]{1,0:T(8,128)S(1)} %copy-done.1, bf16[128,512]{1,0:T(8,128)(2,1)} %get-tuple-element.27.c_in, bf16[128,128]{1,0:T(8,128)(2,1)} %decay.11, bf16[32,128,128]{2,1,0:T(8,128)(2,1)S(1)} %copy-done.3), custom_call_target="tpu_custom_call" | custom-call | tf_op jit(solution)/shard_map/outputs/pallas_call | solution.py:338
  145.1 11.8 %all-to-all-done.3.entering = bf16[32,128,128]{2,1,0:T(8,128)(2,1)S(1)} async-done(((bf16[32,128,128]{2,1,0:T(8,128)(2,1)}), bf16[32,128,128]{2,1,0:T(8,128)(2,1)S(1)}, u32[]{:S(2)}, u32[]{:S(2)}) %all-to-all-start.3) | async-done | bytes 1048608 | tf_op jit(solution)/shard_map/all_to_all | solution.py:357
  156.9 2.8 %outputs.3 = bf16[128,8192]{1,0:T(8,128)(2,1)} custom-call(f32[128,4096]{1,0:T(8,128)S(1)} %copy-done, bf16[128,512]{1,0:T(8,128)(2,1)} %get-tuple-element.19.c_in, bf16[128,128]{1,0:T(8,128)(2,1)} %decay.11, bf16[32,128,128]{2,1,0:T(8,128)(2,1)S(1)} %all-to-all-done.3.entering, bf16[128,8192]{1,0:T(8,128)(2,1)} %outputs.2.rest_0_), custom_call_target="tpu_custom_call", output_to_operand_aliasing={{}: (4, {})} | custom-call | tf_op jit(solution)/shard_map/outputs/pallas_call | solution.py:338
  (15 shorter events, 0.1 us)
Async XLA Ops:
  1.0 8.7 %collective-permute-start = (bf16[3,10240]{1,0:T(4,128)(2,1)S(1)}, bf16[3,10240]{1,0:T(4,128)(2,1)S(1)}, u32[]{:S(2)}, u32[]{:S(2)}) collective-permute-start(bf16[3,10240]{1,0:T(4,128)(2,1)S(1)} %slice.3), channel_id=1, source_target_pairs={{0,1},{1,2},{2,3},{3,4},{4,5},{5,6},{6,7},{7,8},{8,9},{9,10},{10,1... | collective-permute-start | bytes 184328 | tf_op jit(solution)/shard_map/ppermute | solution.py:230
  15.0 40.4 %all-to-all-start.1 = ((bf16[32,136,128]{2,1,0:T(8,128)(2,1)}), bf16[32,136,128]{2,1,0:T(8,128)(2,1)S(1)}, u32[]{:S(2)}, u32[]{:S(2)}) async-start(bf16[32,136,128]{2,1,0:T(8,128)(2,1)} %get-tuple-element.21), calls=%async_computation.1 | async-start | bytes 2228224 | tf_op jit(solution)/shard_map/all_to_all | solution.py:357
  55.3 5.2 %copy-start.4 = (bf16[32,136,128]{2,1,0:T(8,128)(2,1)}, bf16[32,136,128]{2,1,0:T(8,128)(2,1)S(1)}, u32[]{:S(2)}) copy-start(bf16[32,136,128]{2,1,0:T(8,128)(2,1)S(1)} %all-to-all-done.1.states.decays) | copy-start | bytes 3342340
  55.3 33.2 %all-to-all-start = ((bf16[32,128,128]{2,1,0:T(8,128)(2,1)}), bf16[32,128,128]{2,1,0:T(8,128)(2,1)S(1)}, u32[]{:S(2)}, u32[]{:S(2)}) async-start(bf16[32,128,128]{2,1,0:T(8,128)(2,1)} %get-tuple-element.20), calls=%async_computation | async-start | bytes 2097152 | tf_op jit(solution)/shard_map/all_to_all | solution.py:357
  88.5 5.9 %copy-start.5 = (bf16[32,128,128]{2,1,0:T(8,128)(2,1)}, bf16[32,128,128]{2,1,0:T(8,128)(2,1)S(1)}, u32[]{:S(2)}) copy-start(bf16[32,128,128]{2,1,0:T(8,128)(2,1)S(1)} %all-to-all-done.states) | copy-start | bytes 3145732
  88.5 34.5 %all-to-all-start.2 = ((bf16[32,128,128]{2,1,0:T(8,128)(2,1)}), bf16[32,128,128]{2,1,0:T(8,128)(2,1)S(1)}, u32[]{:S(2)}, u32[]{:S(2)}) async-start(bf16[32,128,128]{2,1,0:T(8,128)(2,1)} %entering.2), calls=%async_computation.2 | async-start | bytes 2097152 | tf_op jit(solution)/shard_map/all_to_all | solution.py:357
  115.2 13.5 %copy-start.6 = (f32[128]{0:T(128)S(1)}, f32[128]{0:T(128)}, u32[]{:S(2)}) copy-start(f32[128]{0:T(128)} %param.11) | copy-start | bytes 1540
  123.1 12.7 %copy-start.2 = (bf16[32,128,128]{2,1,0:T(8,128)(2,1)}, bf16[32,128,128]{2,1,0:T(8,128)(2,1)S(1)}, u32[]{:S(2)}) copy-start(bf16[32,128,128]{2,1,0:T(8,128)(2,1)S(1)} %all-to-all-done.2.entering) | copy-start | bytes 3145732
  123.1 33.9 %all-to-all-start.3 = ((bf16[32,128,128]{2,1,0:T(8,128)(2,1)}), bf16[32,128,128]{2,1,0:T(8,128)(2,1)S(1)}, u32[]{:S(2)}, u32[]{:S(2)}) async-start(bf16[32,128,128]{2,1,0:T(8,128)(2,1)} %entering.3), calls=%async_computation.3 | async-start | bytes 2097152 | tf_op jit(solution)/shard_map/all_to_all | solution.py:357
  135.7 6.4 %copy-start.1 = (f32[128,4096]{1,0:T(8,128)S(1)}, f32[128,4096]{1,0:T(8,128)}, u32[]{:S(2)}) copy-start(f32[128,4096]{1,0:T(8,128)} %within.3) | copy-start | bytes 6291460
  135.7 6.4 %copy-start.3 = (bf16[32,128,128]{2,1,0:T(8,128)(2,1)S(1)}, bf16[32,128,128]{2,1,0:T(8,128)(2,1)}, u32[]{:S(2)}) copy-start(bf16[32,128,128]{2,1,0:T(8,128)(2,1)} %copy-done.2) | copy-start | bytes 3145732
  142.1 14.8 %copy-start = (f32[128,4096]{1,0:T(8,128)S(1)}, f32[128,4096]{1,0:T(8,128)}, u32[]{:S(2)}) copy-start(f32[128,4096]{1,0:T(8,128)} %within.2) | copy-start | bytes 6291460

commit v7 on v6

--- a/solution.py
+++ b/solution.py
@@ -66,15 +66,34 @@
     return dot(picked.astype(BF16), spread, 1, 0)
 
 
-def conv_silu(columns, rim, weights, biases):
-    rows, width = columns.shape
-    shape = (8 - (KERNEL - 1), width)
-    extended = jnp.concatenate([jnp.zeros(shape, F32), rim.astype(F32), columns.astype(F32)], axis=0)
+def taps(extended, weights):
     before = pltpu.roll(extended, 1, 0)
     earlier = pltpu.roll(weights[1:2, :] * extended + weights[0:1, :] * before, 2, 0)
-    summed = biases + (weights[3:4, :] * extended + weights[2:3, :] * before) + earlier
-    summed = summed[8:, :]
+    return (weights[3:4, :] * extended + weights[2:3, :] * before + earlier)[8:, :]
+
+
+def conv_silu(columns, rim, weights, biases):
+    width = columns.shape[1]
+    top = jnp.concatenate([jnp.zeros((8 - (KERNEL - 1), width), F32), rim.astype(F32)], axis=0)
+    if columns.dtype == F32:
+        added = taps(jnp.concatenate([top, jnp.zeros((8, width), F32)], axis=0), weights)
+        summed = jnp.concatenate([columns[:8, :] + added, columns[8:, :]], axis=0)
+    else:
+        summed = biases + taps(jnp.concatenate([top, columns.astype(F32)], axis=0), weights)
     return (summed / (1.0 + jnp.exp(-summed))).astype(BF16)
+
+
+def conv_sums_kernel(x_in, b_in, c_in, x_w, b_w, c_w, x_bias, b_bias, c_bias, x_out, b_out, c_out):
+    for columns, weights, biases, out in (
+        (x_in, x_w, x_bias, x_out),
+        (b_in, b_w, b_bias, b_out),
+        (c_in, c_w, c_bias, c_out),
+    ):
+        for first in range(0, out.shape[1], N):
+            at = slice(first, first + N)
+            top = jnp.zeros((8, N), F32)
+            extended = jnp.concatenate([top, columns[:, at].astype(F32)], axis=0)
+            out[:, at] = biases[:, at] + taps(extended, weights[:, at])
 
 
 def decay_rows(*totals):
@@ -256,10 +275,28 @@
                 columns_spec(height, narrow, c_first // at_once + first),
             ]
 
+        tokens, token_specs = [projected] * 3, three(rows)
+        if not half:
+            token_specs = [
+                columns_spec(rows, wide), columns_spec(rows, narrow), columns_spec(rows, narrow)
+            ]
+            tokens = pl.pallas_call(
+                conv_sums_kernel,
+                grid=(groups // at_once,),
+                in_specs=three(rows) + three(KERNEL) + three(1),
+                out_specs=token_specs,
+                out_shape=[
+                    jax.ShapeDtypeStruct((rows, width_half), F32),
+                    jax.ShapeDtypeStruct((rows, groups * N), F32),
+                    jax.ShapeDtypeStruct((rows, groups * N), F32),
+                ],
+                compiler_params=params,
+                name="conv_sums",
+            )(*[projected] * 3, *[conv_weight] * 3, *[bias] * 3)
         return pl.pallas_call(
             functools.partial(conv_states_kernel, half * groups),
             grid=(groups // at_once,),
-            in_specs=three(rows) + three(KERNEL - 1) + three(KERNEL) + three(1) + [per_token] * 2,
+            in_specs=token_specs + three(KERNEL - 1) + three(KERNEL) + three(1) + [per_token] * 2,
             out_specs=[
                 columns_spec(rows, wide),
                 columns_spec(rows, narrow),
@@ -278,8 +315,7 @@
             compiler_params=params,
             name="conv_states",
         )(
-            projected, projected, projected, rim, rim, rim, conv_weight, conv_weight, conv_weight,
-            bias, bias, bias, step_size, log_decay,
+            *tokens, *[rim] * 3, *[conv_weight] * 3, *[bias] * 3, step_size, log_decay
         )
 
     def within_chunk(half, values, keys_b, query_c):

time: 161 us -> 159 us (0.988)
  waiting for transfers between devices: 49 us -> 46.4 us
    ppermute x1, waiting for transfers between devices: 4.43 us -> 1.91 us  [per_device(): lax.ppermute(projected[rows - (KERNEL - 1):], ('sec', 'cp'), [(source, so...]
    pallas_call x0 -> x1, Pallas kernels: none -> 2.52 us  [conv_states(): pl.pallas_call(conv_sums_kernel, grid=(groups // at_once,), in_specs=thre...]
  transfers between devices with their start and end apart: 5 -> 5, of which waited for: 5 -> 5; matrix products, arithmetic and copies ran while one was open for 0% -> 1% of each run, Pallas kernels for 18% -> 20%
where the time goes in v7:
time: 159 us; the launch traced here: 158 us
  waiting for transfers between devices  46.4 us (29%)
  blocking collectives  39.1 us (25%)
  Pallas kernels  38.4 us (24%)
  starting transfers between devices  32.4 us (20%)
  local copies, waits for them, and re-layouts  1.8 us (1%)
    all_to_all x4, waiting for transfers between devices, exchanged(): return lax.all_to_all(value, 'cp', split_axis=0, concat_axis=0, tiled=True)  44.5 us
    all_gather x2, blocking collectives, per_device(): totals = lax.all_gather(section_total(half, state, states[0]), 'sec')  39.1 us
    all_to_all x4, starting transfers between devices, exchanged(): return lax.all_to_all(value, 'cp', split_axis=0, concat_axis=0, tiled=True)  28.1 us
    pallas_call x2, Pallas kernels, within_chunk(): pl.pallas_call(functools.partial(within_kernel, first), grid=(groups,), i...  12.7 us
    pallas_call x2, Pallas kernels, conv_states(): pl.pallas_call(functools.partial(conv_states_kernel, half * groups), grid...  9.09 us
    pallas_call x2, Pallas kernels, outputs(): pl.pallas_call(functools.partial(outputs_kernel, half * groups), grid=(gr...  5.73 us
    pallas_call x2, Pallas kernels, entering_states(): pl.pallas_call(functools.partial(entering_kernel, half), grid=(1,), in_sp...  5.38 us
    ppermute x1, starting transfers between devices, per_device(): lax.ppermute(projected[rows - (KERNEL - 1):], ('sec', 'cp'), [(source, so...  4.28 us
  transfers between devices with their start and end apart: 5, of which 5 were waited for; matrix products, arithmetic and copies ran while one was open for 1% of the time, Pallas kernels for 20%

profile of v7, /device:TPU:64, one launch (start us, length us, event | category | flops | bytes accessed | tf_op | source)
XLA Modules:
  0.0 158.3 jit_solution(1974553741951969588)
XLA Ops:
  0.0 1.0 slice.3
  1.0 4.3 %collective-permute-start = (bf16[3,10240]{1,0:T(4,128)(2,1)S(1)}, bf16[3,10240]{1,0:T(4,128)(2,1)S(1)}, u32[]{:S(2)}, u32[]{:S(2)}) collective-permute-start(bf16[3,10240]{1,0:T(4,128)(2,1)S(1)} %slice.3), channel_id=1, source_target_pairs={{0,1},{1,2},{2,3},{3,4},{4,5},{5,6},{6,7},{7,8},{8,9},{9,10},{10,1... | collective-permute-start | bytes 184328 | tf_op jit(solution)/shard_map/ppermute | solution.py:249
  5.3 2.5 %conv_sums.1 = (f32[128,4096]{1,0:T(8,128)S(1)}, f32[128,512]{1,0:T(8,128)S(1)}, f32[128,512]{1,0:T(8,128)S(1)}) custom-call(bf16[128,10240]{1,0:T(8,128)(2,1)} %c_in.3, bf16[128,10240]{1,0:T(8,128)(2,1)} %c_in.3, bf16[128,10240]{1,0:T(8,128)(2,1)} %c_in.3, f32[4,10240]{1,0:T(4,128)} %c_w.5, f32[4,10240]{1,0:T(4,128)} %c_w.5, f32[4,10240]{1,0:T(4,128)} %c_w.5, ...), custom_call_target="tpu_custom_call" | custom-call | tf_op jit(solution)/shard_map/conv_sums/pallas_call | solution.py:283
  7.8 1.9 %collective-permute-done.x_rim.b_rim.c_rim = bf16[3,10240]{1,0:T(4,128)(2,1)S(1)} collective-permute-done((bf16[3,10240]{1,0:T(4,128)(2,1)S(1)}, bf16[3,10240]{1,0:T(4,128)(2,1)S(1)}, u32[]{:S(2)}, u32[]{:S(2)}) %collective-permute-start) | collective-permute-done | bytes 61472 | tf_op jit(solution)/shard_map/ppermute | solution.py:249
  9.7 3.9 %conv_states.3 = (bf16[128,4096]{1,0:T(8,128)(2,1)}, bf16[128,512]{1,0:T(8,128)(2,1)}, bf16[128,512]{1,0:T(8,128)(2,1)}, bf16[32,136,128]{2,1,0:T(8,128)(2,1)}) custom-call(f32[128,4096]{1,0:T(8,128)S(1)} %get-tuple-element.24.x_in, f32[128,512]{1,0:T(8,128)S(1)} %get-tuple-element.25.b_in, f32[128,512]{1,0:T(8,128)S(1)} %get-tuple-element.26.c_in, ...), custom_call_target="tpu_custom_call" | custom-call | tf_op jit(solution)/shard_map/conv_states/pallas_call | solution.py:296
  13.5 11.4 %all-to-all-start.1 = ((bf16[32,136,128]{2,1,0:T(8,128)(2,1)}), bf16[32,136,128]{2,1,0:T(8,128)(2,1)S(1)}, u32[]{:S(2)}, u32[]{:S(2)}) async-start(bf16[32,136,128]{2,1,0:T(8,128)(2,1)} %get-tuple-element.27), calls=%async_computation.1 | async-start | bytes 2228224 | tf_op jit(solution)/shard_map/all_to_all | solution.py:393
  24.9 5.2 %conv_states.2 = (bf16[128,4096]{1,0:T(8,128)(2,1)}, bf16[128,512]{1,0:T(8,128)(2,1)}, bf16[128,512]{1,0:T(8,128)(2,1)}, bf16[32,128,128]{2,1,0:T(8,128)(2,1)}) custom-call(bf16[128,10240]{1,0:T(8,128)(2,1)} %c_in.3, bf16[128,10240]{1,0:T(8,128)(2,1)} %c_in.3, bf16[128,10240]{1,0:T(8,128)(2,1)} %c_in.3, ...), custom_call_target="tpu_custom_call" | custom-call | tf_op jit(solution)/shard_map/conv_states/pallas_call | solution.py:296
  30.2 23.8 %all-to-all-done.1.states.decays = bf16[32,136,128]{2,1,0:T(8,128)(2,1)S(1)} async-done(((bf16[32,136,128]{2,1,0:T(8,128)(2,1)}), bf16[32,136,128]{2,1,0:T(8,128)(2,1)S(1)}, u32[]{:S(2)}, u32[]{:S(2)}) %all-to-all-start.1) | async-done | bytes 1114144 | tf_op jit(solution)/shard_map/all_to_all | solution.py:393
  53.9 5.2 %all-to-all-start = ((bf16[32,128,128]{2,1,0:T(8,128)(2,1)}), bf16[32,128,128]{2,1,0:T(8,128)(2,1)S(1)}, u32[]{:S(2)}, u32[]{:S(2)}) async-start(bf16[32,128,128]{2,1,0:T(8,128)(2,1)} %get-tuple-element.23), calls=%async_computation | async-start | bytes 2097152 | tf_op jit(solution)/shard_map/all_to_all | solution.py:393
  59.1 1.5 section_total.2
  60.7 19.9 %all-gather = bf16[2176,128]{1,0:T(8,128)(2,1)S(1)} all-gather(bf16[136,128]{1,0:T(8,128)(2,1)S(1)} %section_total.2), channel_id=2, replica_groups=mesh['sec'=16,'cp'=32] {'sec'}, dimensions={0}, use_global_device_ids=true | all-gather | bytes 591872 | tf_op jit(solution)/shard_map/all_gather | solution.py:411
  80.6 2.7 %entering.2 = bf16[32,128,128]{2,1,0:T(8,128)(2,1)} custom-call(bf16[32,136,128]{2,1,0:T(8,128)(2,1)} %copy-done.4, bf16[32,136,128]{2,1,0:T(8,128)(2,1)} %copy-done.4, bf16[16,136,128]{2,1,0:T(8,128)(2,1)S(1)} %bitcast.4), custom_call_target="tpu_custom_call" | custom-call | tf_op jit(solution)/shard_map/entering/pallas_call | solution.py:359
  83.2 3.9 %all-to-all-done.states = bf16[32,128,128]{2,1,0:T(8,128)(2,1)S(1)} async-done(((bf16[32,128,128]{2,1,0:T(8,128)(2,1)}), bf16[32,128,128]{2,1,0:T(8,128)(2,1)S(1)}, u32[]{:S(2)}, u32[]{:S(2)}) %all-to-all-start) | async-done | bytes 1048608 | tf_op jit(solution)/shard_map/all_to_all | solution.py:393
  87.1 5.9 %all-to-all-start.2 = ((bf16[32,128,128]{2,1,0:T(8,128)(2,1)}), bf16[32,128,128]{2,1,0:T(8,128)(2,1)S(1)}, u32[]{:S(2)}, u32[]{:S(2)}) async-start(bf16[32,128,128]{2,1,0:T(8,128)(2,1)} %entering.2), calls=%async_computation.2 | async-start | bytes 2097152 | tf_op jit(solution)/shard_map/all_to_all | solution.py:393
  93.1 1.5 section_total.3
  94.6 19.2 %all-gather.1 = bf16[2176,128]{1,0:T(8,128)(2,1)S(1)} all-gather(bf16[136,128]{1,0:T(8,128)(2,1)S(1)} %section_total.3), channel_id=3, replica_groups=mesh['sec'=16,'cp'=32] {'sec'}, dimensions={0}, use_global_device_ids=true | all-gather | bytes 591872 | tf_op jit(solution)/shard_map/all_gather | solution.py:411
  113.8 2.7 %entering.3 = bf16[32,128,128]{2,1,0:T(8,128)(2,1)} custom-call(bf16[32,128,128]{2,1,0:T(8,128)(2,1)} %copy-done.5, bf16[32,136,128]{2,1,0:T(8,128)(2,1)} %copy-done.4, bf16[16,136,128]{2,1,0:T(8,128)(2,1)S(1)} %bitcast.3), custom_call_target="tpu_custom_call" | custom-call | tf_op jit(solution)/shard_map/entering/pallas_call | solution.py:359
  116.5 5.1 %all-to-all-done.2.entering = bf16[32,128,128]{2,1,0:T(8,128)(2,1)S(1)} async-done(((bf16[32,128,128]{2,1,0:T(8,128)(2,1)}), bf16[32,128,128]{2,1,0:T(8,128)(2,1)S(1)}, u32[]{:S(2)}, u32[]{:S(2)}) %all-to-all-start.2) | async-done | bytes 1048608 | tf_op jit(solution)/shard_map/all_to_all | solution.py:393
  121.6 5.6 %all-to-all-start.3 = ((bf16[32,128,128]{2,1,0:T(8,128)(2,1)}), bf16[32,128,128]{2,1,0:T(8,128)(2,1)S(1)}, u32[]{:S(2)}, u32[]{:S(2)}) async-start(bf16[32,128,128]{2,1,0:T(8,128)(2,1)} %entering.3), calls=%async_computation.3 | async-start | bytes 2097152 | tf_op jit(solution)/shard_map/all_to_all | solution.py:393
  128.1 6.2 %within.3 = f32[128,4096]{1,0:T(8,128)} custom-call(bf16[128,4096]{1,0:T(8,128)(2,1)} %get-tuple-element.31.x_in, bf16[128,512]{1,0:T(8,128)(2,1)} %get-tuple-element.32.b_in, bf16[128,512]{1,0:T(8,128)(2,1)} %get-tuple-element.33.c_in, bf16[128,128]{1,0:T(8,128)(2,1)} %step.7, bf16[128,128]{1,0:T(8,128)(2,1)} %decay.11, f32[1,8192]{1,0:T(1,128)} %reshape_reshape.3.skip), custom_call_target="tpu_custom_call" | custom-call | tf_op jit(solution)/shard_map/within/pallas_call | solution.py:323
  134.4 6.4 %within.2 = f32[128,4096]{1,0:T(8,128)} custom-call(bf16[128,4096]{1,0:T(8,128)(2,1)} %get-tuple-element.20.x_in, bf16[128,512]{1,0:T(8,128)(2,1)} %get-tuple-element.21.b_in, bf16[128,512]{1,0:T(8,128)(2,1)} %get-tuple-element.22.c_in, bf16[128,128]{1,0:T(8,128)(2,1)} %step.7, bf16[128,128]{1,0:T(8,128)(2,1)} %decay.11, f32[1,8192]{1,0:T(1,128)} %reshape_reshape.3.skip), custom_call_target="tpu_custom_call" | custom-call | tf_op jit(solution)/shard_map/within/pallas_call | solution.py:323
  140.8 2.9 %outputs.2.rest_0_ = bf16[128,8192]{1,0:T(8,128)(2,1)} custom-call(f32[128,4096]{1,0:T(8,128)S(1)} %copy-done.1, bf16[128,512]{1,0:T(8,128)(2,1)} %get-tuple-element.33.c_in, bf16[128,128]{1,0:T(8,128)(2,1)} %decay.11, bf16[32,128,128]{2,1,0:T(8,128)(2,1)S(1)} %copy-done.3), custom_call_target="tpu_custom_call" | custom-call | tf_op jit(solution)/shard_map/outputs/pallas_call | solution.py:374
  143.8 11.8 %all-to-all-done.3.entering = bf16[32,128,128]{2,1,0:T(8,128)(2,1)S(1)} async-done(((bf16[32,128,128]{2,1,0:T(8,128)(2,1)}), bf16[32,128,128]{2,1,0:T(8,128)(2,1)S(1)}, u32[]{:S(2)}, u32[]{:S(2)}) %all-to-all-start.3) | async-done | bytes 1048608 | tf_op jit(solution)/shard_map/all_to_all | solution.py:393
  155.5 2.8 %outputs.3 = bf16[128,8192]{1,0:T(8,128)(2,1)} custom-call(f32[128,4096]{1,0:T(8,128)S(1)} %copy-done, bf16[128,512]{1,0:T(8,128)(2,1)} %get-tuple-element.22.c_in, bf16[128,128]{1,0:T(8,128)(2,1)} %decay.11, bf16[32,128,128]{2,1,0:T(8,128)(2,1)S(1)} %all-to-all-done.3.entering, bf16[128,8192]{1,0:T(8,128)(2,1)} %outputs.2.rest_0_), custom_call_target="tpu_custom_call", output_to_operand_aliasing={{}: (4, {})} | custom-call | tf_op jit(solution)/shard_map/outputs/pallas_call | solution.py:374
  (16 shorter events, 0.8 us)
Async XLA Ops:
  1.0 8.7 %collective-permute-start = (bf16[3,10240]{1,0:T(4,128)(2,1)S(1)}, bf16[3,10240]{1,0:T(4,128)(2,1)S(1)}, u32[]{:S(2)}, u32[]{:S(2)}) collective-permute-start(bf16[3,10240]{1,0:T(4,128)(2,1)S(1)} %slice.3), channel_id=1, source_target_pairs={{0,1},{1,2},{2,3},{3,4},{4,5},{5,6},{6,7},{7,8},{8,9},{9,10},{10,1... | collective-permute-start | bytes 184328 | tf_op jit(solution)/shard_map/ppermute | solution.py:249
  13.5 40.4 %all-to-all-start.1 = ((bf16[32,136,128]{2,1,0:T(8,128)(2,1)}), bf16[32,136,128]{2,1,0:T(8,128)(2,1)S(1)}, u32[]{:S(2)}, u32[]{:S(2)}) async-start(bf16[32,136,128]{2,1,0:T(8,128)(2,1)} %get-tuple-element.27), calls=%async_computation.1 | async-start | bytes 2228224 | tf_op jit(solution)/shard_map/all_to_all | solution.py:393
  53.9 5.2 %copy-start.4 = (bf16[32,136,128]{2,1,0:T(8,128)(2,1)}, bf16[32,136,128]{2,1,0:T(8,128)(2,1)S(1)}, u32[]{:S(2)}) copy-start(bf16[32,136,128]{2,1,0:T(8,128)(2,1)S(1)} %all-to-all-done.1.states.decays) | copy-start | bytes 3342340
  53.9 33.2 %all-to-all-start = ((bf16[32,128,128]{2,1,0:T(8,128)(2,1)}), bf16[32,128,128]{2,1,0:T(8,128)(2,1)S(1)}, u32[]{:S(2)}, u32[]{:S(2)}) async-start(bf16[32,128,128]{2,1,0:T(8,128)(2,1)} %get-tuple-element.23), calls=%async_computation | async-start | bytes 2097152 | tf_op jit(solution)/shard_map/all_to_all | solution.py:393
  87.1 5.9 %copy-start.5 = (bf16[32,128,128]{2,1,0:T(8,128)(2,1)}, bf16[32,128,128]{2,1,0:T(8,128)(2,1)S(1)}, u32[]{:S(2)}) copy-start(bf16[32,128,128]{2,1,0:T(8,128)(2,1)S(1)} %all-to-all-done.states) | copy-start | bytes 3145732
  87.1 34.5 %all-to-all-start.2 = ((bf16[32,128,128]{2,1,0:T(8,128)(2,1)}), bf16[32,128,128]{2,1,0:T(8,128)(2,1)S(1)}, u32[]{:S(2)}, u32[]{:S(2)}) async-start(bf16[32,128,128]{2,1,0:T(8,128)(2,1)} %entering.2), calls=%async_computation.2 | async-start | bytes 2097152 | tf_op jit(solution)/shard_map/all_to_all | solution.py:393
  113.8 13.5 %copy-start.6 = (f32[128]{0:T(128)S(1)}, f32[128]{0:T(128)}, u32[]{:S(2)}) copy-start(f32[128]{0:T(128)} %param.11) | copy-start | bytes 1540
  121.6 12.7 %copy-start.2 = (bf16[32,128,128]{2,1,0:T(8,128)(2,1)}, bf16[32,128,128]{2,1,0:T(8,128)(2,1)S(1)}, u32[]{:S(2)}) copy-start(bf16[32,128,128]{2,1,0:T(8,128)(2,1)S(1)} %all-to-all-done.2.entering) | copy-start | bytes 3145732
  121.6 33.9 %all-to-all-start.3 = ((bf16[32,128,128]{2,1,0:T(8,128)(2,1)}), bf16[32,128,128]{2,1,0:T(8,128)(2,1)S(1)}, u32[]{:S(2)}, u32[]{:S(2)}) async-start(bf16[32,128,128]{2,1,0:T(8,128)(2,1)} %entering.3), calls=%async_computation.3 | async-start | bytes 2097152 | tf_op jit(solution)/shard_map/all_to_all | solution.py:393
  134.3 6.4 %copy-start.1 = (f32[128,4096]{1,0:T(8,128)S(1)}, f32[128,4096]{1,0:T(8,128)}, u32[]{:S(2)}) copy-start(f32[128,4096]{1,0:T(8,128)} %within.3) | copy-start | bytes 6291460
  134.4 6.4 %copy-start.3 = (bf16[32,128,128]{2,1,0:T(8,128)(2,1)S(1)}, bf16[32,128,128]{2,1,0:T(8,128)(2,1)}, u32[]{:S(2)}) copy-start(bf16[32,128,128]{2,1,0:T(8,128)(2,1)} %copy-done.2) | copy-start | bytes 3145732
  140.8 14.7 %copy-start = (f32[128,4096]{1,0:T(8,128)S(1)}, f32[128,4096]{1,0:T(8,128)}, u32[]{:S(2)}) copy-start(f32[128,4096]{1,0:T(8,128)} %within.2) | copy-start | bytes 6291460

commit v8 on v7

--- a/solution.py
+++ b/solution.py
@@ -133,9 +133,10 @@
         values = conv_silu(x_in[:, wide], x_rim[:, wide], x_w[:, wide], x_bias[:, wide])
         keys_b = conv_silu(b_in[:, narrow], b_rim[:, narrow], b_w[:, narrow], b_bias[:, narrow])
         query_c = conv_silu(c_in[:, narrow], c_rim[:, narrow], c_w[:, narrow], c_bias[:, narrow])
-        x_out[:, wide] = values
-        b_out[:, narrow] = keys_b
-        c_out[:, narrow] = query_c
+        if x_out is not None:
+            x_out[:, wide] = values
+            b_out[:, narrow] = keys_b
+            c_out[:, narrow] = query_c
         weighted = (values.astype(F32) * over_heads(weight_parts, group, spread[...])).astype(BF16)
         summed = dot(keys_b, weighted, 0, 0).astype(BF16)
         here = range(targets // groups)
@@ -152,6 +153,23 @@
             for at in here:
                 lanes = slice(at * width, (at + 1) * width)
                 states[local * len(here) + at, N:height, :] = pieces[:, lanes]
+
+
+def states_only_kernel(first_group, *refs):
+    conv_states_kernel(first_group, *refs[:-2], None, None, None, *refs[-2:])
+
+
+def conv_kernel(
+    x_in, b_in, c_in, x_rim, b_rim, c_rim, x_w, b_w, c_w, x_bias, b_bias, c_bias, x_out, b_out, c_out
+):
+    for columns, rim, weights, biases, out in (
+        (x_in, x_rim, x_w, x_bias, x_out),
+        (b_in, b_rim, b_w, b_bias, b_out),
+        (c_in, c_rim, c_w, c_bias, c_out),
+    ):
+        for first in range(0, out.shape[1], N):
+            at = slice(first, first + N)
+            out[:, at] = conv_silu(columns[:, at], rim[:, at], weights[:, at], biases[:, at])
 
 
 def within_kernel(first_group, x_in, b_in, c_in, step, decay, skip, out, running_all, steps_all):
@@ -293,30 +311,45 @@
                 compiler_params=params,
                 name="conv_sums",
             )(*[projected] * 3, *[conv_weight] * 3, *[bias] * 3)
-        return pl.pallas_call(
-            functools.partial(conv_states_kernel, half * groups),
+        conv_specs = [
+            columns_spec(rows, wide), columns_spec(rows, narrow), columns_spec(rows, narrow)
+        ]
+        conv_shapes = [
+            pltpu.HBM((rows, width_half), BF16),
+            pltpu.HBM((rows, groups * N), BF16),
+            pltpu.HBM((rows, groups * N), BF16),
+        ]
+        around_specs = three(KERNEL - 1) + three(KERNEL) + three(1)
+        around = [*[rim] * 3, *[conv_weight] * 3, *[bias] * 3]
+        convolved = []
+        if not half:
+            convolved = pl.pallas_call(
+                conv_kernel,
+                grid=(groups // at_once,),
+                in_specs=three(rows) + around_specs,
+                out_specs=conv_specs,
+                out_shape=conv_shapes,
+                compiler_params=params,
+                name="conv",
+            )(*[projected] * 3, *around)
+        kernel = conv_states_kernel if half else states_only_kernel
+        results = pl.pallas_call(
+            functools.partial(kernel, half * groups),
             grid=(groups // at_once,),
-            in_specs=token_specs + three(KERNEL - 1) + three(KERNEL) + three(1) + [per_token] * 2,
-            out_specs=[
-                columns_spec(rows, wide),
-                columns_spec(rows, narrow),
-                columns_spec(rows, narrow),
+            in_specs=token_specs + around_specs + [per_token] * 2,
+            out_specs=(conv_specs if half else [])
+            + [
                 pl.BlockSpec(
                     (at_once * group_targets, state_rows, width_here), lambda g: (g, 0, 0)
                 ),
             ],
-            out_shape=[
-                pltpu.HBM((rows, width_half), BF16),
-                pltpu.HBM((rows, groups * N), BF16),
-                pltpu.HBM((rows, groups * N), BF16),
-                pltpu.HBM((targets, state_rows, width_here), BF16),
-            ],
+            out_shape=(conv_shapes if half else [])
+            + [pltpu.HBM((targets, state_rows, width_here), BF16)],
             scratch_shapes=[pltpu.VMEM((HEAD_COUNT, GROUP_WIDTH), BF16)],
             compiler_params=params,
             name="conv_states",
-        )(
-            *tokens, *[rim] * 3, *[conv_weight] * 3, *[bias] * 3, step_size, log_decay
-        )
+        )(*tokens, *around, step_size, log_decay)
+        return [*convolved, *results]
 
     def within_chunk(half, values, keys_b, query_c):
         first = half * groups

time: 159 us -> 159 us (level)
  waiting for transfers between devices: 46.4 us -> 42.5 us
  Pallas kernels: 38.4 us -> 42.2 us
    all_to_all x4, waiting for transfers between devices: 44.5 us -> 40.5 us  [exchanged(): return lax.all_to_all(value, 'cp', split_axis=0, concat_axis=0, tiled=True)]
    pallas_call x2 -> x3, Pallas kernels: 9.09 us -> 12.9 us  [the longest x2 8.84 us: conv_states(): pl.pallas_call(functools.partial(kernel, half * groups), grid=(groups //...]
  transfers between devices with their start and end apart: 5 -> 5, of which waited for: 5 -> 5; matrix products, arithmetic and copies ran while one was open for 1% -> 1% of each run, Pallas kernels for 20% -> 23%
where the time goes in v8:
time: 159 us; the launch traced here: 158 us
  waiting for transfers between devices  42.5 us (27%)
  Pallas kernels  42.2 us (27%)
  blocking collectives  39.1 us (25%)
  starting transfers between devices  32.4 us (20%)
  local copies, waits for them, and re-layouts  1.78 us (1%)
    all_to_all x4, waiting for transfers between devices, exchanged(): return lax.all_to_all(value, 'cp', split_axis=0, concat_axis=0, tiled=True)  40.5 us
    all_gather x2, blocking collectives, per_device(): totals = lax.all_gather(section_total(half, state, states[0]), 'sec')  39.1 us
    all_to_all x4, starting transfers between devices, exchanged(): return lax.all_to_all(value, 'cp', split_axis=0, concat_axis=0, tiled=True)  28.1 us
    pallas_call x2, Pallas kernels, within_chunk(): pl.pallas_call(functools.partial(within_kernel, first), grid=(groups,), i...  12.7 us
    pallas_call x2, Pallas kernels, conv_states(): pl.pallas_call(functools.partial(kernel, half * groups), grid=(groups //...  8.84 us
    pallas_call x2, Pallas kernels, outputs(): pl.pallas_call(functools.partial(outputs_kernel, half * groups), grid=(gr...  5.74 us
    pallas_call x2, Pallas kernels, entering_states(): pl.pallas_call(functools.partial(entering_kernel, half), grid=(1,), in_sp...  5.41 us
    ppermute x1, starting transfers between devices, per_device(): lax.ppermute(projected[rows - (KERNEL - 1):], ('sec', 'cp'), [(source, so...  4.28 us
  transfers between devices with their start and end apart: 5, of which 5 were waited for; matrix products, arithmetic and copies ran while one was open for 1% of the time, Pallas kernels for 23%

profile of v8, /device:TPU:64, one launch (start us, length us, event | category | flops | bytes accessed | tf_op | source)
XLA Modules:
  0.0 158.1 jit_solution(7151311463737694988)
XLA Ops:
  1.0 4.3 %collective-permute-start = (bf16[3,10240]{1,0:T(4,128)(2,1)S(1)}, bf16[3,10240]{1,0:T(4,128)(2,1)S(1)}, u32[]{:S(2)}, u32[]{:S(2)}) collective-permute-start(bf16[3,10240]{1,0:T(4,128)(2,1)S(1)} %slice.3), channel_id=1, source_target_pairs={{0,1},{1,2},{2,3},{3,4},{4,5},{5,6},{6,7},{7,8},{8,9},{9,10},{10,1... | collective-permute-start | bytes 184328 | tf_op jit(solution)/shard_map/ppermute | solution.py:267
  5.3 2.5 %conv_sums.1 = (f32[128,4096]{1,0:T(8,128)S(1)}, f32[128,512]{1,0:T(8,128)S(1)}, f32[128,512]{1,0:T(8,128)S(1)}) custom-call(bf16[128,10240]{1,0:T(8,128)(2,1)} %c_in.5, bf16[128,10240]{1,0:T(8,128)(2,1)} %c_in.5, bf16[128,10240]{1,0:T(8,128)(2,1)} %c_in.5, f32[4,10240]{1,0:T(4,128)} %c_w.5, f32[4,10240]{1,0:T(4,128)} %c_w.5, f32[4,10240]{1,0:T(4,128)} %c_w.5, ...), custom_call_target="tpu_custom_call" | custom-call | tf_op jit(solution)/shard_map/conv_sums/pallas_call | solution.py:301
  7.8 1.9 %collective-permute-done.x_rim.b_rim.c_rim.refs_3_.refs_4_.refs_5_ = bf16[3,10240]{1,0:T(4,128)(2,1)S(1)} collective-permute-done((bf16[3,10240]{1,0:T(4,128)(2,1)S(1)}, bf16[3,10240]{1,0:T(4,128)(2,1)S(1)}, u32[]{:S(2)}, u32[]{:S(2)}) %collective-permute-start) | collective-permute-done | bytes 61472 | tf_op jit(solution)/shard_map/ppermute | solution.py:267
  9.7 3.6 %conv_states.3 = bf16[32,136,128]{2,1,0:T(8,128)(2,1)} custom-call(f32[128,4096]{1,0:T(8,128)S(1)} %get-tuple-element.23.refs_0_, f32[128,512]{1,0:T(8,128)S(1)} %get-tuple-element.24.refs_1_, f32[128,512]{1,0:T(8,128)S(1)} %get-tuple-element.25.refs_2_, bf16[3,10240]{1,0:T(4,128)(2,1)S(1)} %collective-permute-done.x_rim.b_rim.c_rim.refs_3_.refs_4_.refs_5_, ...), custom_call_target="tpu_custom_call" | custom-call | tf_op jit(solution)/shard_map/conv_states/pallas_call | solution.py:336
  13.3 11.4 %all-to-all-start.1 = ((bf16[32,136,128]{2,1,0:T(8,128)(2,1)}), bf16[32,136,128]{2,1,0:T(8,128)(2,1)S(1)}, u32[]{:S(2)}, u32[]{:S(2)}) async-start(bf16[32,136,128]{2,1,0:T(8,128)(2,1)} %conv_states.3), calls=%async_computation.1 | async-start | bytes 2228224 | tf_op jit(solution)/shard_map/all_to_all | solution.py:426
  24.7 5.2 %conv_states.2 = (bf16[128,4096]{1,0:T(8,128)(2,1)}, bf16[128,512]{1,0:T(8,128)(2,1)}, bf16[128,512]{1,0:T(8,128)(2,1)}, bf16[32,128,128]{2,1,0:T(8,128)(2,1)}) custom-call(bf16[128,10240]{1,0:T(8,128)(2,1)} %c_in.5, bf16[128,10240]{1,0:T(8,128)(2,1)} %c_in.5, bf16[128,10240]{1,0:T(8,128)(2,1)} %c_in.5, ...), custom_call_target="tpu_custom_call" | custom-call | tf_op jit(solution)/shard_map/conv_states/pallas_call | solution.py:336
  29.9 23.8 %all-to-all-done.1.states.decays = bf16[32,136,128]{2,1,0:T(8,128)(2,1)S(1)} async-done(((bf16[32,136,128]{2,1,0:T(8,128)(2,1)}), bf16[32,136,128]{2,1,0:T(8,128)(2,1)S(1)}, u32[]{:S(2)}, u32[]{:S(2)}) %all-to-all-start.1) | async-done | bytes 1114144 | tf_op jit(solution)/shard_map/all_to_all | solution.py:426
  53.7 5.2 %all-to-all-start = ((bf16[32,128,128]{2,1,0:T(8,128)(2,1)}), bf16[32,128,128]{2,1,0:T(8,128)(2,1)S(1)}, u32[]{:S(2)}, u32[]{:S(2)}) async-start(bf16[32,128,128]{2,1,0:T(8,128)(2,1)} %get-tuple-element.22), calls=%async_computation | async-start | bytes 2097152 | tf_op jit(solution)/shard_map/all_to_all | solution.py:426
  58.9 1.5 section_total.2
  60.4 19.9 %all-gather = bf16[2176,128]{1,0:T(8,128)(2,1)S(1)} all-gather(bf16[136,128]{1,0:T(8,128)(2,1)S(1)} %section_total.2), channel_id=2, replica_groups=mesh['sec'=16,'cp'=32] {'sec'}, dimensions={0}, use_global_device_ids=true | all-gather | bytes 591872 | tf_op jit(solution)/shard_map/all_gather | solution.py:444
  80.3 2.7 %entering.2 = bf16[32,128,128]{2,1,0:T(8,128)(2,1)} custom-call(bf16[32,136,128]{2,1,0:T(8,128)(2,1)} %copy-done.4, bf16[32,136,128]{2,1,0:T(8,128)(2,1)} %copy-done.4, bf16[16,136,128]{2,1,0:T(8,128)(2,1)S(1)} %bitcast.4), custom_call_target="tpu_custom_call" | custom-call | tf_op jit(solution)/shard_map/entering/pallas_call | solution.py:392
  83.0 3.8 %all-to-all-done.states = bf16[32,128,128]{2,1,0:T(8,128)(2,1)S(1)} async-done(((bf16[32,128,128]{2,1,0:T(8,128)(2,1)}), bf16[32,128,128]{2,1,0:T(8,128)(2,1)S(1)}, u32[]{:S(2)}, u32[]{:S(2)}) %all-to-all-start) | async-done | bytes 1048608 | tf_op jit(solution)/shard_map/all_to_all | solution.py:426
  86.9 5.9 %all-to-all-start.2 = ((bf16[32,128,128]{2,1,0:T(8,128)(2,1)}), bf16[32,128,128]{2,1,0:T(8,128)(2,1)S(1)}, u32[]{:S(2)}, u32[]{:S(2)}) async-start(bf16[32,128,128]{2,1,0:T(8,128)(2,1)} %entering.2), calls=%async_computation.2 | async-start | bytes 2097152 | tf_op jit(solution)/shard_map/all_to_all | solution.py:426
  92.8 1.5 section_total.3
  94.3 19.2 %all-gather.1 = bf16[2176,128]{1,0:T(8,128)(2,1)S(1)} all-gather(bf16[136,128]{1,0:T(8,128)(2,1)S(1)} %section_total.3), channel_id=3, replica_groups=mesh['sec'=16,'cp'=32] {'sec'}, dimensions={0}, use_global_device_ids=true | all-gather | bytes 591872 | tf_op jit(solution)/shard_map/all_gather | solution.py:444
  113.5 2.7 %entering.3 = bf16[32,128,128]{2,1,0:T(8,128)(2,1)} custom-call(bf16[32,128,128]{2,1,0:T(8,128)(2,1)} %copy-done.5, bf16[32,136,128]{2,1,0:T(8,128)(2,1)} %copy-done.4, bf16[16,136,128]{2,1,0:T(8,128)(2,1)S(1)} %bitcast.3), custom_call_target="tpu_custom_call" | custom-call | tf_op jit(solution)/shard_map/entering/pallas_call | solution.py:392
  116.2 5.2 %all-to-all-done.2.entering = bf16[32,128,128]{2,1,0:T(8,128)(2,1)S(1)} async-done(((bf16[32,128,128]{2,1,0:T(8,128)(2,1)}), bf16[32,128,128]{2,1,0:T(8,128)(2,1)S(1)}, u32[]{:S(2)}, u32[]{:S(2)}) %all-to-all-start.2) | async-done | bytes 1048608 | tf_op jit(solution)/shard_map/all_to_all | solution.py:426
  121.4 5.6 %all-to-all-start.3 = ((bf16[32,128,128]{2,1,0:T(8,128)(2,1)}), bf16[32,128,128]{2,1,0:T(8,128)(2,1)S(1)}, u32[]{:S(2)}, u32[]{:S(2)}) async-start(bf16[32,128,128]{2,1,0:T(8,128)(2,1)} %entering.3), calls=%async_computation.3 | async-start | bytes 2097152 | tf_op jit(solution)/shard_map/all_to_all | solution.py:426
  127.8 4.0 %conv.1 = (bf16[128,4096]{1,0:T(8,128)(2,1)}, bf16[128,512]{1,0:T(8,128)(2,1)}, bf16[128,512]{1,0:T(8,128)(2,1)}) custom-call(bf16[128,10240]{1,0:T(8,128)(2,1)} %c_in.5, bf16[128,10240]{1,0:T(8,128)(2,1)} %c_in.5, bf16[128,10240]{1,0:T(8,128)(2,1)} %c_in.5, bf16[3,10240]{1,0:T(4,128)(2,1)S(1)} %collective-permute-done.x_rim.b_rim.c_rim.refs_3_.refs_4_.refs_5_, ...), custom_call_target="tpu_custom_call" | custom-call | tf_op jit(solution)/shard_map/conv/pallas_call | solution.py:326
  131.9 6.2 %within.3 = f32[128,4096]{1,0:T(8,128)} custom-call(bf16[128,4096]{1,0:T(8,128)(2,1)} %get-tuple-element.29.x_in, bf16[128,512]{1,0:T(8,128)(2,1)} %get-tuple-element.30.b_in, bf16[128,512]{1,0:T(8,128)(2,1)} %get-tuple-element.31.c_in, bf16[128,128]{1,0:T(8,128)(2,1)} %step.5, bf16[128,128]{1,0:T(8,128)(2,1)} %decay.9, f32[1,8192]{1,0:T(1,128)} %reshape_reshape.3.skip), custom_call_target="tpu_custom_call" | custom-call | tf_op jit(solution)/shard_map/within/pallas_call | solution.py:356
  138.1 6.4 %within.2 = f32[128,4096]{1,0:T(8,128)} custom-call(bf16[128,4096]{1,0:T(8,128)(2,1)} %get-tuple-element.19.x_in, bf16[128,512]{1,0:T(8,128)(2,1)} %get-tuple-element.20.b_in, bf16[128,512]{1,0:T(8,128)(2,1)} %get-tuple-element.21.c_in, bf16[128,128]{1,0:T(8,128)(2,1)} %step.5, bf16[128,128]{1,0:T(8,128)(2,1)} %decay.9, f32[1,8192]{1,0:T(1,128)} %reshape_reshape.3.skip), custom_call_target="tpu_custom_call" | custom-call | tf_op jit(solution)/shard_map/within/pallas_call | solution.py:356
  144.6 3.0 %outputs.2.rest_0_ = bf16[128,8192]{1,0:T(8,128)(2,1)} custom-call(f32[128,4096]{1,0:T(8,128)S(1)} %copy-done.1, bf16[128,512]{1,0:T(8,128)(2,1)} %get-tuple-element.31.c_in, bf16[128,128]{1,0:T(8,128)(2,1)} %decay.9, bf16[32,128,128]{2,1,0:T(8,128)(2,1)S(1)} %copy-done.3), custom_call_target="tpu_custom_call" | custom-call | tf_op jit(solution)/shard_map/outputs/pallas_call | solution.py:407
  147.5 7.8 %all-to-all-done.3.entering = bf16[32,128,128]{2,1,0:T(8,128)(2,1)S(1)} async-done(((bf16[32,128,128]{2,1,0:T(8,128)(2,1)}), bf16[32,128,128]{2,1,0:T(8,128)(2,1)S(1)}, u32[]{:S(2)}, u32[]{:S(2)}) %all-to-all-start.3) | async-done | bytes 1048608 | tf_op jit(solution)/shard_map/all_to_all | solution.py:426
  155.3 2.8 %outputs.3 = bf16[128,8192]{1,0:T(8,128)(2,1)} custom-call(f32[128,4096]{1,0:T(8,128)S(1)} %copy-done, bf16[128,512]{1,0:T(8,128)(2,1)} %get-tuple-element.21.c_in, bf16[128,128]{1,0:T(8,128)(2,1)} %decay.9, bf16[32,128,128]{2,1,0:T(8,128)(2,1)S(1)} %all-to-all-done.3.entering, bf16[128,8192]{1,0:T(8,128)(2,1)} %outputs.2.rest_0_), custom_call_target="tpu_custom_call", output_to_operand_aliasing={{}: (4, {})} | custom-call | tf_op jit(solution)/shard_map/outputs/pallas_call | solution.py:407
  (17 shorter events, 1.8 us)
Async XLA Ops:
  1.0 8.7 %collective-permute-start = (bf16[3,10240]{1,0:T(4,128)(2,1)S(1)}, bf16[3,10240]{1,0:T(4,128)(2,1)S(1)}, u32[]{:S(2)}, u32[]{:S(2)}) collective-permute-start(bf16[3,10240]{1,0:T(4,128)(2,1)S(1)} %slice.3), channel_id=1, source_target_pairs={{0,1},{1,2},{2,3},{3,4},{4,5},{5,6},{6,7},{7,8},{8,9},{9,10},{10,1... | collective-permute-start | bytes 184328 | tf_op jit(solution)/shard_map/ppermute | solution.py:267
  13.3 40.4 %all-to-all-start.1 = ((bf16[32,136,128]{2,1,0:T(8,128)(2,1)}), bf16[32,136,128]{2,1,0:T(8,128)(2,1)S(1)}, u32[]{:S(2)}, u32[]{:S(2)}) async-start(bf16[32,136,128]{2,1,0:T(8,128)(2,1)} %conv_states.3), calls=%async_computation.1 | async-start | bytes 2228224 | tf_op jit(solution)/shard_map/all_to_all | solution.py:426
  53.7 5.2 %copy-start.4 = (bf16[32,136,128]{2,1,0:T(8,128)(2,1)}, bf16[32,136,128]{2,1,0:T(8,128)(2,1)S(1)}, u32[]{:S(2)}) copy-start(bf16[32,136,128]{2,1,0:T(8,128)(2,1)S(1)} %all-to-all-done.1.states.decays) | copy-start | bytes 3342340
  53.7 33.2 %all-to-all-start = ((bf16[32,128,128]{2,1,0:T(8,128)(2,1)}), bf16[32,128,128]{2,1,0:T(8,128)(2,1)S(1)}, u32[]{:S(2)}, u32[]{:S(2)}) async-start(bf16[32,128,128]{2,1,0:T(8,128)(2,1)} %get-tuple-element.22), calls=%async_computation | async-start | bytes 2097152 | tf_op jit(solution)/shard_map/all_to_all | solution.py:426
  86.9 6.0 %copy-start.5 = (bf16[32,128,128]{2,1,0:T(8,128)(2,1)}, bf16[32,128,128]{2,1,0:T(8,128)(2,1)S(1)}, u32[]{:S(2)}) copy-start(bf16[32,128,128]{2,1,0:T(8,128)(2,1)S(1)} %all-to-all-done.states) | copy-start | bytes 3145732
  86.9 34.5 %all-to-all-start.2 = ((bf16[32,128,128]{2,1,0:T(8,128)(2,1)}), bf16[32,128,128]{2,1,0:T(8,128)(2,1)S(1)}, u32[]{:S(2)}, u32[]{:S(2)}) async-start(bf16[32,128,128]{2,1,0:T(8,128)(2,1)} %entering.2), calls=%async_computation.2 | async-start | bytes 2097152 | tf_op jit(solution)/shard_map/all_to_all | solution.py:426
  113.5 13.5 %copy-start.6 = (f32[128]{0:T(128)S(1)}, f32[128]{0:T(128)}, u32[]{:S(2)}) copy-start(f32[128]{0:T(128)} %param.11) | copy-start | bytes 1540
  121.4 10.5 %copy-start.2 = (bf16[32,128,128]{2,1,0:T(8,128)(2,1)}, bf16[32,128,128]{2,1,0:T(8,128)(2,1)S(1)}, u32[]{:S(2)}) copy-start(bf16[32,128,128]{2,1,0:T(8,128)(2,1)S(1)} %all-to-all-done.2.entering) | copy-start | bytes 3145732
  121.4 33.9 %all-to-all-start.3 = ((bf16[32,128,128]{2,1,0:T(8,128)(2,1)}), bf16[32,128,128]{2,1,0:T(8,128)(2,1)S(1)}, u32[]{:S(2)}, u32[]{:S(2)}) async-start(bf16[32,128,128]{2,1,0:T(8,128)(2,1)} %entering.3), calls=%async_computation.3 | async-start | bytes 2097152 | tf_op jit(solution)/shard_map/all_to_all | solution.py:426
  138.1 6.4 %copy-start.1 = (f32[128,4096]{1,0:T(8,128)S(1)}, f32[128,4096]{1,0:T(8,128)}, u32[]{:S(2)}) copy-start(f32[128,4096]{1,0:T(8,128)} %within.3) | copy-start | bytes 6291460
  138.1 6.4 %copy-start.3 = (bf16[32,128,128]{2,1,0:T(8,128)(2,1)S(1)}, bf16[32,128,128]{2,1,0:T(8,128)(2,1)}, u32[]{:S(2)}) copy-start(bf16[32,128,128]{2,1,0:T(8,128)(2,1)} %copy-done.2) | copy-start | bytes 3145732
  144.6 10.7 %copy-start = (f32[128,4096]{1,0:T(8,128)S(1)}, f32[128,4096]{1,0:T(8,128)}, u32[]{:S(2)}) copy-start(f32[128,4096]{1,0:T(8,128)} %within.2) | copy-start | bytes 6291460

commit v9 on v8

--- a/solution.py
+++ b/solution.py
@@ -80,7 +80,8 @@
         summed = jnp.concatenate([columns[:8, :] + added, columns[8:, :]], axis=0)
     else:
         summed = biases + taps(jnp.concatenate([top, columns.astype(F32)], axis=0), weights)
-    return (summed / (1.0 + jnp.exp(-summed))).astype(BF16)
+    half = 0.5 * summed
+    return (half * jnp.tanh(half) + half).astype(BF16)
 
 
 def conv_sums_kernel(x_in, b_in, c_in, x_w, b_w, c_w, x_bias, b_bias, c_bias, x_out, b_out, c_out):

time: 159 us -> 159 us (level)
  no operation moved by 1% of the time
where the time goes in v9:
time: 159 us; the launch traced here: 158 us
  waiting for transfers between devices  42.7 us (27%)
  Pallas kernels  41.9 us (26%)
  blocking collectives  39.1 us (25%)
  starting transfers between devices  32.4 us (20%)
  local copies, waits for them, and re-layouts  1.78 us (1%)
    all_to_all x4, waiting for transfers between devices, exchanged(): return lax.all_to_all(value, 'cp', split_axis=0, concat_axis=0, tiled=True)  40.8 us
    all_gather x2, blocking collectives, per_device(): totals = lax.all_gather(section_total(half, state, states[0]), 'sec')  39.1 us
    all_to_all x4, starting transfers between devices, exchanged(): return lax.all_to_all(value, 'cp', split_axis=0, concat_axis=0, tiled=True)  28.2 us
    pallas_call x2, Pallas kernels, within_chunk(): pl.pallas_call(functools.partial(within_kernel, first), grid=(groups,), i...  12.7 us
    pallas_call x2, Pallas kernels, conv_states(): pl.pallas_call(functools.partial(kernel, half * groups), grid=(groups //...  8.69 us
    pallas_call x2, Pallas kernels, outputs(): pl.pallas_call(functools.partial(outputs_kernel, half * groups), grid=(gr...  5.75 us
    pallas_call x2, Pallas kernels, entering_states(): pl.pallas_call(functools.partial(entering_kernel, half), grid=(1,), in_sp...  5.41 us
    ppermute x1, starting transfers between devices, per_device(): lax.ppermute(projected[rows - (KERNEL - 1):], ('sec', 'cp'), [(source, so...  4.28 us
  transfers between devices with their start and end apart: 5, of which 5 were waited for; matrix products, arithmetic and copies ran while one was open for 1% of the time, Pallas kernels for 23%

profile of v9, /device:TPU:64, one launch (start us, length us, event | category | flops | bytes accessed | tf_op | source)
XLA Modules:
  0.0 158.0 jit_solution(8193875717656670716)
XLA Ops:
  1.0 4.3 %collective-permute-start = (bf16[3,10240]{1,0:T(4,128)(2,1)S(1)}, bf16[3,10240]{1,0:T(4,128)(2,1)S(1)}, u32[]{:S(2)}, u32[]{:S(2)}) collective-permute-start(bf16[3,10240]{1,0:T(4,128)(2,1)S(1)} %slice.3), channel_id=1, source_target_pairs={{0,1},{1,2},{2,3},{3,4},{4,5},{5,6},{6,7},{7,8},{8,9},{9,10},{10,1... | collective-permute-start | bytes 184328 | tf_op jit(solution)/shard_map/ppermute | solution.py:268
  5.3 2.5 %conv_sums.1 = (f32[128,4096]{1,0:T(8,128)S(1)}, f32[128,512]{1,0:T(8,128)S(1)}, f32[128,512]{1,0:T(8,128)S(1)}) custom-call(bf16[128,10240]{1,0:T(8,128)(2,1)} %c_in.5, bf16[128,10240]{1,0:T(8,128)(2,1)} %c_in.5, bf16[128,10240]{1,0:T(8,128)(2,1)} %c_in.5, f32[4,10240]{1,0:T(4,128)} %c_w.5, f32[4,10240]{1,0:T(4,128)} %c_w.5, f32[4,10240]{1,0:T(4,128)} %c_w.5, ...), custom_call_target="tpu_custom_call" | custom-call | tf_op jit(solution)/shard_map/conv_sums/pallas_call | solution.py:302
  7.8 1.9 %collective-permute-done.x_rim.b_rim.c_rim.refs_3_.refs_4_.refs_5_ = bf16[3,10240]{1,0:T(4,128)(2,1)S(1)} collective-permute-done((bf16[3,10240]{1,0:T(4,128)(2,1)S(1)}, bf16[3,10240]{1,0:T(4,128)(2,1)S(1)}, u32[]{:S(2)}, u32[]{:S(2)}) %collective-permute-start) | collective-permute-done | bytes 61472 | tf_op jit(solution)/shard_map/ppermute | solution.py:268
  9.7 3.5 %conv_states.3 = bf16[32,136,128]{2,1,0:T(8,128)(2,1)} custom-call(f32[128,4096]{1,0:T(8,128)S(1)} %get-tuple-element.23.refs_0_, f32[128,512]{1,0:T(8,128)S(1)} %get-tuple-element.24.refs_1_, f32[128,512]{1,0:T(8,128)S(1)} %get-tuple-element.25.refs_2_, bf16[3,10240]{1,0:T(4,128)(2,1)S(1)} %collective-permute-done.x_rim.b_rim.c_rim.refs_3_.refs_4_.refs_5_, ...), custom_call_target="tpu_custom_call" | custom-call | tf_op jit(solution)/shard_map/conv_states/pallas_call | solution.py:337
  13.2 11.4 %all-to-all-start.1 = ((bf16[32,136,128]{2,1,0:T(8,128)(2,1)}), bf16[32,136,128]{2,1,0:T(8,128)(2,1)S(1)}, u32[]{:S(2)}, u32[]{:S(2)}) async-start(bf16[32,136,128]{2,1,0:T(8,128)(2,1)} %conv_states.3), calls=%async_computation.1 | async-start | bytes 2228224 | tf_op jit(solution)/shard_map/all_to_all | solution.py:427
  24.6 5.2 %conv_states.2 = (bf16[128,4096]{1,0:T(8,128)(2,1)}, bf16[128,512]{1,0:T(8,128)(2,1)}, bf16[128,512]{1,0:T(8,128)(2,1)}, bf16[32,128,128]{2,1,0:T(8,128)(2,1)}) custom-call(bf16[128,10240]{1,0:T(8,128)(2,1)} %c_in.5, bf16[128,10240]{1,0:T(8,128)(2,1)} %c_in.5, bf16[128,10240]{1,0:T(8,128)(2,1)} %c_in.5, ...), custom_call_target="tpu_custom_call" | custom-call | tf_op jit(solution)/shard_map/conv_states/pallas_call | solution.py:337
  29.8 23.8 %all-to-all-done.1.states.decays = bf16[32,136,128]{2,1,0:T(8,128)(2,1)S(1)} async-done(((bf16[32,136,128]{2,1,0:T(8,128)(2,1)}), bf16[32,136,128]{2,1,0:T(8,128)(2,1)S(1)}, u32[]{:S(2)}, u32[]{:S(2)}) %all-to-all-start.1) | async-done | bytes 1114144 | tf_op jit(solution)/shard_map/all_to_all | solution.py:427
  53.6 5.2 %all-to-all-start = ((bf16[32,128,128]{2,1,0:T(8,128)(2,1)}), bf16[32,128,128]{2,1,0:T(8,128)(2,1)S(1)}, u32[]{:S(2)}, u32[]{:S(2)}) async-start(bf16[32,128,128]{2,1,0:T(8,128)(2,1)} %get-tuple-element.22), calls=%async_computation | async-start | bytes 2097152 | tf_op jit(solution)/shard_map/all_to_all | solution.py:427
  58.8 1.5 section_total.2
  60.3 19.9 %all-gather = bf16[2176,128]{1,0:T(8,128)(2,1)S(1)} all-gather(bf16[136,128]{1,0:T(8,128)(2,1)S(1)} %section_total.2), channel_id=2, replica_groups=mesh['sec'=16,'cp'=32] {'sec'}, dimensions={0}, use_global_device_ids=true | all-gather | bytes 591872 | tf_op jit(solution)/shard_map/all_gather | solution.py:445
  80.3 2.7 %entering.2 = bf16[32,128,128]{2,1,0:T(8,128)(2,1)} custom-call(bf16[32,136,128]{2,1,0:T(8,128)(2,1)} %copy-done.4, bf16[32,136,128]{2,1,0:T(8,128)(2,1)} %copy-done.4, bf16[16,136,128]{2,1,0:T(8,128)(2,1)S(1)} %bitcast.4), custom_call_target="tpu_custom_call" | custom-call | tf_op jit(solution)/shard_map/entering/pallas_call | solution.py:393
  82.9 3.8 %all-to-all-done.states = bf16[32,128,128]{2,1,0:T(8,128)(2,1)S(1)} async-done(((bf16[32,128,128]{2,1,0:T(8,128)(2,1)}), bf16[32,128,128]{2,1,0:T(8,128)(2,1)S(1)}, u32[]{:S(2)}, u32[]{:S(2)}) %all-to-all-start) | async-done | bytes 1048608 | tf_op jit(solution)/shard_map/all_to_all | solution.py:427
  86.8 6.0 %all-to-all-start.2 = ((bf16[32,128,128]{2,1,0:T(8,128)(2,1)}), bf16[32,128,128]{2,1,0:T(8,128)(2,1)S(1)}, u32[]{:S(2)}, u32[]{:S(2)}) async-start(bf16[32,128,128]{2,1,0:T(8,128)(2,1)} %entering.2), calls=%async_computation.2 | async-start | bytes 2097152 | tf_op jit(solution)/shard_map/all_to_all | solution.py:427
  92.8 1.5 section_total.3
  94.3 19.2 %all-gather.1 = bf16[2176,128]{1,0:T(8,128)(2,1)S(1)} all-gather(bf16[136,128]{1,0:T(8,128)(2,1)S(1)} %section_total.3), channel_id=3, replica_groups=mesh['sec'=16,'cp'=32] {'sec'}, dimensions={0}, use_global_device_ids=true | all-gather | bytes 591872 | tf_op jit(solution)/shard_map/all_gather | solution.py:445
  113.5 2.7 %entering.3 = bf16[32,128,128]{2,1,0:T(8,128)(2,1)} custom-call(bf16[32,128,128]{2,1,0:T(8,128)(2,1)} %copy-done.5, bf16[32,136,128]{2,1,0:T(8,128)(2,1)} %copy-done.4, bf16[16,136,128]{2,1,0:T(8,128)(2,1)S(1)} %bitcast.3), custom_call_target="tpu_custom_call" | custom-call | tf_op jit(solution)/shard_map/entering/pallas_call | solution.py:393
  116.2 5.2 %all-to-all-done.2.entering = bf16[32,128,128]{2,1,0:T(8,128)(2,1)S(1)} async-done(((bf16[32,128,128]{2,1,0:T(8,128)(2,1)}), bf16[32,128,128]{2,1,0:T(8,128)(2,1)S(1)}, u32[]{:S(2)}, u32[]{:S(2)}) %all-to-all-start.2) | async-done | bytes 1048608 | tf_op jit(solution)/shard_map/all_to_all | solution.py:427
  121.3 5.6 %all-to-all-start.3 = ((bf16[32,128,128]{2,1,0:T(8,128)(2,1)}), bf16[32,128,128]{2,1,0:T(8,128)(2,1)S(1)}, u32[]{:S(2)}, u32[]{:S(2)}) async-start(bf16[32,128,128]{2,1,0:T(8,128)(2,1)} %entering.3), calls=%async_computation.3 | async-start | bytes 2097152 | tf_op jit(solution)/shard_map/all_to_all | solution.py:427
  127.8 3.9 %conv.1 = (bf16[128,4096]{1,0:T(8,128)(2,1)}, bf16[128,512]{1,0:T(8,128)(2,1)}, bf16[128,512]{1,0:T(8,128)(2,1)}) custom-call(bf16[128,10240]{1,0:T(8,128)(2,1)} %c_in.5, bf16[128,10240]{1,0:T(8,128)(2,1)} %c_in.5, bf16[128,10240]{1,0:T(8,128)(2,1)} %c_in.5, bf16[3,10240]{1,0:T(4,128)(2,1)S(1)} %collective-permute-done.x_rim.b_rim.c_rim.refs_3_.refs_4_.refs_5_, ...), custom_call_target="tpu_custom_call" | custom-call | tf_op jit(solution)/shard_map/conv/pallas_call | solution.py:327
  131.6 6.2 %within.3 = f32[128,4096]{1,0:T(8,128)} custom-call(bf16[128,4096]{1,0:T(8,128)(2,1)} %get-tuple-element.29.x_in, bf16[128,512]{1,0:T(8,128)(2,1)} %get-tuple-element.30.b_in, bf16[128,512]{1,0:T(8,128)(2,1)} %get-tuple-element.31.c_in, bf16[128,128]{1,0:T(8,128)(2,1)} %step.5, bf16[128,128]{1,0:T(8,128)(2,1)} %decay.9, f32[1,8192]{1,0:T(1,128)} %reshape_reshape.3.skip), custom_call_target="tpu_custom_call" | custom-call | tf_op jit(solution)/shard_map/within/pallas_call | solution.py:357
  137.9 6.4 %within.2 = f32[128,4096]{1,0:T(8,128)} custom-call(bf16[128,4096]{1,0:T(8,128)(2,1)} %get-tuple-element.19.x_in, bf16[128,512]{1,0:T(8,128)(2,1)} %get-tuple-element.20.b_in, bf16[128,512]{1,0:T(8,128)(2,1)} %get-tuple-element.21.c_in, bf16[128,128]{1,0:T(8,128)(2,1)} %step.5, bf16[128,128]{1,0:T(8,128)(2,1)} %decay.9, f32[1,8192]{1,0:T(1,128)} %reshape_reshape.3.skip), custom_call_target="tpu_custom_call" | custom-call | tf_op jit(solution)/shard_map/within/pallas_call | solution.py:357
  144.3 2.9 %outputs.2.rest_0_ = bf16[128,8192]{1,0:T(8,128)(2,1)} custom-call(f32[128,4096]{1,0:T(8,128)S(1)} %copy-done.1, bf16[128,512]{1,0:T(8,128)(2,1)} %get-tuple-element.31.c_in, bf16[128,128]{1,0:T(8,128)(2,1)} %decay.9, bf16[32,128,128]{2,1,0:T(8,128)(2,1)S(1)} %copy-done.3), custom_call_target="tpu_custom_call" | custom-call | tf_op jit(solution)/shard_map/outputs/pallas_call | solution.py:408
  147.3 7.9 %all-to-all-done.3.entering = bf16[32,128,128]{2,1,0:T(8,128)(2,1)S(1)} async-done(((bf16[32,128,128]{2,1,0:T(8,128)(2,1)}), bf16[32,128,128]{2,1,0:T(8,128)(2,1)S(1)}, u32[]{:S(2)}, u32[]{:S(2)}) %all-to-all-start.3) | async-done | bytes 1048608 | tf_op jit(solution)/shard_map/all_to_all | solution.py:427
  155.2 2.8 %outputs.3 = bf16[128,8192]{1,0:T(8,128)(2,1)} custom-call(f32[128,4096]{1,0:T(8,128)S(1)} %copy-done, bf16[128,512]{1,0:T(8,128)(2,1)} %get-tuple-element.21.c_in, bf16[128,128]{1,0:T(8,128)(2,1)} %decay.9, bf16[32,128,128]{2,1,0:T(8,128)(2,1)S(1)} %all-to-all-done.3.entering, bf16[128,8192]{1,0:T(8,128)(2,1)} %outputs.2.rest_0_), custom_call_target="tpu_custom_call", output_to_operand_aliasing={{}: (4, {})} | custom-call | tf_op jit(solution)/shard_map/outputs/pallas_call | solution.py:408
  (17 shorter events, 1.8 us)
Async XLA Ops:
  1.0 8.7 %collective-permute-start = (bf16[3,10240]{1,0:T(4,128)(2,1)S(1)}, bf16[3,10240]{1,0:T(4,128)(2,1)S(1)}, u32[]{:S(2)}, u32[]{:S(2)}) collective-permute-start(bf16[3,10240]{1,0:T(4,128)(2,1)S(1)} %slice.3), channel_id=1, source_target_pairs={{0,1},{1,2},{2,3},{3,4},{4,5},{5,6},{6,7},{7,8},{8,9},{9,10},{10,1... | collective-permute-start | bytes 184328 | tf_op jit(solution)/shard_map/ppermute | solution.py:268
  13.2 40.4 %all-to-all-start.1 = ((bf16[32,136,128]{2,1,0:T(8,128)(2,1)}), bf16[32,136,128]{2,1,0:T(8,128)(2,1)S(1)}, u32[]{:S(2)}, u32[]{:S(2)}) async-start(bf16[32,136,128]{2,1,0:T(8,128)(2,1)} %conv_states.3), calls=%async_computation.1 | async-start | bytes 2228224 | tf_op jit(solution)/shard_map/all_to_all | solution.py:427
  53.6 5.2 %copy-start.4 = (bf16[32,136,128]{2,1,0:T(8,128)(2,1)}, bf16[32,136,128]{2,1,0:T(8,128)(2,1)S(1)}, u32[]{:S(2)}) copy-start(bf16[32,136,128]{2,1,0:T(8,128)(2,1)S(1)} %all-to-all-done.1.states.decays) | copy-start | bytes 3342340
  53.6 33.2 %all-to-all-start = ((bf16[32,128,128]{2,1,0:T(8,128)(2,1)}), bf16[32,128,128]{2,1,0:T(8,128)(2,1)S(1)}, u32[]{:S(2)}, u32[]{:S(2)}) async-start(bf16[32,128,128]{2,1,0:T(8,128)(2,1)} %get-tuple-element.22), calls=%async_computation | async-start | bytes 2097152 | tf_op jit(solution)/shard_map/all_to_all | solution.py:427
  86.8 6.0 %copy-start.5 = (bf16[32,128,128]{2,1,0:T(8,128)(2,1)}, bf16[32,128,128]{2,1,0:T(8,128)(2,1)S(1)}, u32[]{:S(2)}) copy-start(bf16[32,128,128]{2,1,0:T(8,128)(2,1)S(1)} %all-to-all-done.states) | copy-start | bytes 3145732
  86.8 34.6 %all-to-all-start.2 = ((bf16[32,128,128]{2,1,0:T(8,128)(2,1)}), bf16[32,128,128]{2,1,0:T(8,128)(2,1)S(1)}, u32[]{:S(2)}, u32[]{:S(2)}) async-start(bf16[32,128,128]{2,1,0:T(8,128)(2,1)} %entering.2), calls=%async_computation.2 | async-start | bytes 2097152 | tf_op jit(solution)/shard_map/all_to_all | solution.py:427
  113.5 13.5 %copy-start.6 = (f32[128]{0:T(128)S(1)}, f32[128]{0:T(128)}, u32[]{:S(2)}) copy-start(f32[128]{0:T(128)} %param.11) | copy-start | bytes 1540
  121.3 10.3 %copy-start.2 = (bf16[32,128,128]{2,1,0:T(8,128)(2,1)}, bf16[32,128,128]{2,1,0:T(8,128)(2,1)S(1)}, u32[]{:S(2)}) copy-start(bf16[32,128,128]{2,1,0:T(8,128)(2,1)S(1)} %all-to-all-done.2.entering) | copy-start | bytes 3145732
  121.3 33.9 %all-to-all-start.3 = ((bf16[32,128,128]{2,1,0:T(8,128)(2,1)}), bf16[32,128,128]{2,1,0:T(8,128)(2,1)S(1)}, u32[]{:S(2)}, u32[]{:S(2)}) async-start(bf16[32,128,128]{2,1,0:T(8,128)(2,1)} %entering.3), calls=%async_computation.3 | async-start | bytes 2097152 | tf_op jit(solution)/shard_map/all_to_all | solution.py:427
  137.9 6.4 %copy-start.1 = (f32[128,4096]{1,0:T(8,128)S(1)}, f32[128,4096]{1,0:T(8,128)}, u32[]{:S(2)}) copy-start(f32[128,4096]{1,0:T(8,128)} %within.3) | copy-start | bytes 6291460
  137.9 6.4 %copy-start.3 = (bf16[32,128,128]{2,1,0:T(8,128)(2,1)S(1)}, bf16[32,128,128]{2,1,0:T(8,128)(2,1)}, u32[]{:S(2)}) copy-start(bf16[32,128,128]{2,1,0:T(8,128)(2,1)} %copy-done.2) | copy-start | bytes 3145732
  144.3 10.9 %copy-start = (f32[128,4096]{1,0:T(8,128)S(1)}, f32[128,4096]{1,0:T(8,128)}, u32[]{:S(2)}) copy-start(f32[128,4096]{1,0:T(8,128)} %within.2) | copy-start | bytes 6291460
